TPU v7x, 32 devices: a whole 2x2x4 slice. The times are simulated.
32 devices in a mesh: width: 8 (over z, x), thick: 4 (over y, core).
Axes of the slice: x: 2, y: 2, z: 4, core: 2. Of those that a mesh axis runs over, the one named last changes fastest.
Arguments:
- deviation: float32 [6, 16, 64, 1024], P(None, 'thick', 'width'), may hold values from -4.6 to 4.6, as said below
- velocity: float32 [3, 16, 64, 1024], P(None, 'thick', 'width'), may hold values from -4 to 4
- stiffness: float32 [16, 64, 1024], P('thick', 'width'), may hold values from 0.1 to 16, as said below
Outputs:
- deviation_next: float32 [6, 16, 64, 1024], P(None, 'thick', 'width')
- solution: float32 [3, 16, 64, 1024], P(None, 'thick', 'width')
Inputs may be any that keep to these rules, and one draw needn't show every extreme that they name: `deviation`: entries are independent across cells. `stiffness`: positive at every node.
All inputs are finite; a program needn't handle non-finite values.
Results may differ from a plain program's by a relative error of at most 0.0019.
Values sent between devices are 32-bit elements; how exact they have to be, the bound alone decides.
No kernel may reach another device: no remote copies, remote signals or barrier semaphores. Data moves between devices by JAX's collectives and lax.ppermute only.
A program may use at most 64 MiB of HBM per device.

v0:
```python
import jax
import jax.numpy as jnp
from jax import lax
from jax.sharding import PartitionSpec as P

ITERS = 2


TIME_STEP = 0.1
RELAX_TIME = 1.0
MOBILITY = 0.3
MODULUS = 10.0
pair_table = ((0, 0), (1, 1), (2, 2), (0, 1), (0, 2), (1, 2))
slot_table = ((0, 3, 4), (3, 1, 5), (4, 5, 2))


def padded_2(block, sides, width):
    for axis, dim in sides:
        count = lax.axis_size(axis)
        forward = [(i, i + 1) for i in range(count - 1)]
        backward = [(target, source) for source, target in forward]
        low = lax.ppermute(
            lax.slice_in_dim(block, block.shape[dim] - width, None, axis=dim), axis, forward
        )
        high = lax.ppermute(lax.slice_in_dim(block, 0, width, axis=dim), axis, backward)
        block = jnp.concatenate([low, block, high], axis=dim)
    return block


def shifted(value, axis, by):
    count = lax.axis_size(axis)
    pairs = [(i, i + by) for i in range(count) if 0 <= i + by < count]
    return lax.ppermute(value, axis, pairs)


def advance(padded):
    padded = jnp.pad(padded, ((0, 0), (0, 0), (0, 0), (1, 1)))
    extent = (padded.shape[1] - 2, padded.shape[2] - 2, padded.shape[3] - 2)

    def neighbour(axis_dim, offset):
        starts = [1, 1, 1]
        starts[axis_dim] += offset
        return padded[
            :,
            starts[0] : starts[0] + extent[0],
            starts[1] : starts[1] + extent[1],
            starts[2] : starts[2] + extent[2],
        ]

    centre = neighbour(0, 0)
    beneath = [neighbour(d, -1) for d in range(3)]
    above_cells = [neighbour(d, 1) for d in range(3)]
    gradient = [
        [0.5 * (above_cells[j][6 + i] - beneath[j][6 + i]) for j in range(3)] for i in range(3)
    ]
    tensor = [[centre[slot_table[i][j]] for j in range(3)] for i in range(3)]
    changes = []
    for p in range(6):
        i, j = pair_table[p]
        advected = jnp.zeros_like(centre[p])
        for d in range(3):
            flow_speed = centre[6 + d]
            advected = (
                advected
                + jnp.maximum(flow_speed, 0.0) * (centre[p] - beneath[d][p])
                + jnp.minimum(flow_speed, 0.0) * (above_cells[d][p] - centre[p])
            )
        stretch = sum(
            (gradient[i][k] * tensor[k][j] + gradient[j][k] * tensor[k][i] for k in range(3))
        )
        square = sum((tensor[i][k] * tensor[k][j] for k in range(3)))
        change = (
            -advected
            + gradient[i][j]
            + gradient[j][i]
            + stretch
            - (centre[p] + MOBILITY * square) / RELAX_TIME
        )
        changes.append(centre[p] + TIME_STEP * change)
    return jnp.stack(changes)


def pair_sum(values, axis_dim):
    reduced = values.shape[axis_dim] - 1
    return lax.slice_in_dim(values, 1, reduced + 1, axis=axis_dim) + lax.slice_in_dim(
        values, 0, reduced, axis=axis_dim
    )


def pair_diff(values, axis_dim):
    reduced = values.shape[axis_dim] - 1
    return lax.slice_in_dim(values, 1, reduced + 1, axis=axis_dim) - lax.slice_in_dim(
        values, 0, reduced, axis=axis_dim
    )


def assemble(stress):
    stress = jnp.pad(stress, ((0, 0), (0, 0), (0, 0), (1, 0)))
    result = []
    for i in range(3):
        summed = None
        for d in range(3):
            member = stress[slot_table[i][d]]
            for e in range(3):
                member = pair_diff(member, e) if e == d else pair_sum(member, e)
            summed = member if summed is None else summed + member
        result.append(summed)
    return 0.25 * MODULUS * jnp.stack(result)


def operate(nodal, stiffness):
    padded = padded_2(nodal, (("thick", 1), ("width", 2)), 1)
    padded = jnp.pad(padded, ((0, 0), (0, 0), (0, 0), (1, 1)))
    beside = padded[:, 2:, 1:-1, 1:-1] + padded[:, :-2, 1:-1, 1:-1]
    beside = beside + padded[:, 1:-1, 2:, 1:-1] + padded[:, 1:-1, :-2, 1:-1]
    beside = beside + padded[:, 1:-1, 1:-1, 2:] + padded[:, 1:-1, 1:-1, :-2]
    return (6.0 + stiffness)[None] * nodal - beside


def squares(residual):
    return lax.psum(jnp.sum(residual * residual), ("width", "thick"))


def on_device(deviation, velocity, stiffness):
    layers = deviation.shape[1]
    columns = deviation.shape[2]
    stacked = jnp.concatenate([deviation, velocity], axis=0)
    padded = padded_2(stacked, (("thick", 1), ("width", 2)), 1)
    deviation_next = advance(padded)
    partial_value = assemble(jnp.pad(deviation_next, ((0, 0), (1, 1), (1, 1), (0, 0))))
    arrived = shifted(partial_value[:, layers], "thick", 1)
    partial_value = partial_value[:, :layers].at[:, 0].add(arrived)
    arrived_side = shifted(partial_value[:, :, columns], "width", 1)
    forces = partial_value[:, :, :columns].at[:, :, 0].add(arrived_side)
    solution = jnp.zeros_like(forces)
    residual = forces
    direction = forces
    norm_now = squares(residual)
    for iterate in range(ITERS):
        mapped = operate(direction, stiffness)
        step_size = norm_now / lax.psum(jnp.sum(direction * mapped), ("width", "thick"))
        solution = solution + step_size * direction
        if iterate + 1 < ITERS:
            residual = residual - step_size * mapped
            norm_next = squares(residual)
            direction = residual + norm_next / norm_now * direction
            norm_now = norm_next
    return (deviation_next, solution)


def solution(mesh):
    placed = (
        P(None, "thick", "width", None),
        P(None, "thick", "width", None),
        P("thick", "width", None),
    )
    return jax.shard_map(
        on_device,
        mesh=mesh,
        in_specs=placed,
        out_specs=(P(None, "thick", "width", None), P(None, "thick", "width", None)),
        check_vma=False,
    )
```

profile of v0, /device:TPU:0, one launch (start us, length us, event | category | flops | bytes accessed | tf_op | source)
XLA Modules:
  0.0 215.0 jit_solution(14730910318901121988)
XLA Ops:
  0.6 1.2 constant_dynamic-update-slice_fusion.1
  2.0 2.4 %collective-permute-start = (f32[9,1,8,1024]{3,2,1,0:T(8,128)S(1)}, f32[9,1,8,1024]{3,2,1,0:T(8,128)S(1)}, u32[]{:S(2)}, u32[]{:S(2)}) collective-permute-start(f32[9,1,8,1024]{3,2,1,0:T(8,128)S(1)} %get-tuple-element.47), channel_id=1, source_target_pairs={{0,1},{1,2},{2,3},{4,5},{5,6},{6,7},{8,9},{9,10},{10,11},{12,13},{... | collective-permute-start | bytes 884744 | tf_op jit(solution)/shard_map/ppermute | solution.py:22
  4.4 1.3 collective-permute-start.1
  5.7 4.3 %collective-permute-done.1 = f32[9,1,8,1024]{3,2,1,0:T(8,128)S(1)} collective-permute-done((f32[9,1,8,1024]{3,2,1,0:T(8,128)S(1)}, f32[9,1,8,1024]{3,2,1,0:T(8,128)S(1)}, u32[]{:S(2)}, u32[]{:S(2)}) %collective-permute-start.1) | collective-permute-done | bytes 294944 | tf_op jit(solution)/shard_map/ppermute | solution.py:25
  10.2 3.4 %collective-permute-start.2 = (f32[9,6,1,1024]{3,2,1,0:T(1,128)S(1)}, f32[9,6,1,1024]{3,2,1,0:T(1,128)S(1)}, u32[]{:S(2)}, u32[]{:S(2)}) collective-permute-start(f32[9,6,1,1024]{3,2,1,0:T(1,128)S(1)} %get-tuple-element.43), channel_id=1, source_target_pairs={{0,4},{4,8},{8,12},{12,16},{16,20},{20,24},{24,28},{1,5},{5,9},{9,... | collective-permute-start | bytes 663560 | tf_op jit(solution)/shard_map/ppermute | solution.py:22
  13.6 1.3 collective-permute-start.3
  15.3 1.8 collective-permute-done.2
  17.1 4.4 %collective-permute-done.3 = f32[9,6,1,1024]{3,2,1,0:T(1,128)S(1)} collective-permute-done((f32[9,6,1,1024]{3,2,1,0:T(1,128)S(1)}, f32[9,6,1,1024]{3,2,1,0:T(1,128)S(1)}, u32[]{:S(2)}, u32[]{:S(2)}) %collective-permute-start.3) | collective-permute-done | bytes 221216 | tf_op jit(solution)/shard_map/ppermute | solution.py:25
  21.5 4.7 %select_maximum_fusion = f32[9,6,10,1026]{3,2,1,0:T(8,128)S(1)} fusion(f32[9,6,1,1024]{3,2,1,0:T(1,128)S(1)} %collective-permute-done.3, f32[9,6,1,1024]{3,2,1,0:T(1,128)S(1)} %collective-permute-done.2, f32[9,1,8,1024]{3,2,1,0:T(8,128)S(1)} %collective-permute-done.1, f32[9,4,8,1024]{3,2,1,0:T(8,128)S(1)} %constant_dynamic-update-slice_fusion, ...), kind=kLoop, calls=%fused_computation.14 | loop fusion | flops 6648480 | bytes 4428000 | tf_op jit(solution)/shard_map/concatenate | solution.py:26
  28.8 1.3 fusion.15
  31.7 6.5 %collective-permute-start.4 = (f32[3,9,1024]{2,0,1:T(4,128)S(1)}, f32[3,9,1024]{2,0,1:T(4,128)S(1)}, u32[]{:S(2)}, u32[]{:S(2)}) collective-permute-start(f32[3,9,1024]{2,0,1:T(4,128)S(1)} %bitcast.31), channel_id=1, source_target_pairs={{0,1},{1,2},{2,3},{4,5},{5,6},{6,7},{8,9},{9,10},{10,11},{12,13},{... | collective-permute-start | bytes 331784 | tf_op jit(solution)/shard_map/ppermute | solution.py:33
  38.2 0.9 collective-permute-done.4
  39.3 4.1 %collective-permute-start.5 = (f32[3,4,1024]{2,1,0:T(4,128)S(1)}, f32[3,4,1024]{2,1,0:T(4,128)S(1)}, u32[]{:S(2)}, u32[]{:S(2)}) collective-permute-start(f32[3,4,1024]{2,1,0:T(4,128)S(1)} %bitcast.32), channel_id=1, source_target_pairs={{0,4},{4,8},{8,12},{12,16},{16,20},{20,24},{24,28},{1,5},{5,9},{9,... | collective-permute-start | bytes 147464 | tf_op jit(solution)/shard_map/ppermute | solution.py:33
  43.4 1.7 collective-permute-done.5
  45.8 1.3 collective-permute-start.6
  47.1 3.4 %collective-permute-start.7 = (f32[3,1,8,1024]{3,2,1,0:T(8,128)S(1)}, f32[3,1,8,1024]{3,2,1,0:T(8,128)S(1)}, u32[]{:S(2)}, u32[]{:S(2)}) collective-permute-start(f32[3,1,8,1024]{3,2,1,0:T(8,128)S(1)} %get-tuple-element.63), channel_id=1, source_target_pairs={{0,1},{1,2},{2,3},{4,5},{5,6},{6,7},{8,9},{9,10},{10,11},{12,13},{... | collective-permute-start | bytes 294920 | tf_op jit(solution)/shard_map/ppermute | solution.py:22
  50.5 0.9 collective-permute-done.7
  51.5 1.3 collective-permute-start.8
  52.8 4.6 %collective-permute-start.9 = (f32[3,6,1,1024]{3,2,1,0:T(1,128)S(1)}, f32[3,6,1,1024]{3,2,1,0:T(1,128)S(1)}, u32[]{:S(2)}, u32[]{:S(2)}) collective-permute-start(f32[3,6,1,1024]{3,2,1,0:T(1,128)S(1)} %get-tuple-element.59), channel_id=1, source_target_pairs={{0,4},{4,8},{8,12},{12,16},{16,20},{20,24},{24,28},{1,5},{5,9},{9,... | collective-permute-start | bytes 221192 | tf_op jit(solution)/shard_map/ppermute | solution.py:22
  57.7 1.6 collective-permute-done.9
  60.1 1.0 multiply_reduce_fusion.1
  61.1 47.5 %all-reduce.5 = (f32[]{:T(128)}, f32[]{:T(128)}) all-reduce(f32[]{:T(128)} %get-tuple-element.33, f32[]{:T(128)} %get-tuple-element.32), channel_id=1, replica_groups=mesh['width'=8,'thick'=4] {'width','thick'}, use_global_device_ids=true, to_apply=%region_1.2 | all-reduce | flops 2 | bytes 16 | tf_op jit(solution)/shard_map/psum | solution.py:121
  110.7 42.1 %psum.30 = f32[]{:T(128)} all-reduce(f32[]{:T(128)} %multiply_reduce_fusion), channel_id=1, replica_groups=mesh['width'=8,'thick'=4] {'width','thick'}, use_global_device_ids=true, to_apply=%region_5.6 | all-reduce | flops 1 | bytes 8 | tf_op jit(solution)/shard_map/psum | solution.py:121
  154.1 1.3 collective-permute-start.10
  155.4 3.0 %collective-permute-start.11 = (f32[3,1,8,1024]{3,2,1,0:T(8,128)S(1)}, f32[3,1,8,1024]{3,2,1,0:T(8,128)S(1)}, u32[]{:S(2)}, u32[]{:S(2)}) collective-permute-start(f32[3,1,8,1024]{3,2,1,0:T(8,128)S(1)} %get-tuple-element.61), channel_id=1, source_target_pairs={{0,1},{1,2},{2,3},{4,5},{5,6},{6,7},{8,9},{9,10},{10,11},{12,13},{... | collective-permute-start | bytes 294920 | tf_op jit(solution)/shard_map/ppermute | solution.py:22
  158.5 0.9 collective-permute-done.11
  159.5 1.3 collective-permute-start.12
  160.8 4.8 %collective-permute-start.13 = (f32[3,6,1,1024]{3,2,1,0:T(1,128)S(1)}, f32[3,6,1,1024]{3,2,1,0:T(1,128)S(1)}, u32[]{:S(2)}, u32[]{:S(2)}) collective-permute-start(f32[3,6,1,1024]{3,2,1,0:T(1,128)S(1)} %get-tuple-element.57), channel_id=1, source_target_pairs={{0,4},{4,8},{8,12},{12,16},{16,20},{20,24},{24,28},{1,5},{5,9},{9,... | collective-permute-start | bytes 221192 | tf_op jit(solution)/shard_map/ppermute | solution.py:22
  166.0 1.7 collective-permute-done.13
  168.5 1.0 fusion.4
  169.5 43.4 %psum.31 = f32[]{:T(128)} all-reduce(f32[]{:T(128)} %fusion.4), channel_id=1, replica_groups=mesh['width'=8,'thick'=4] {'width','thick'}, use_global_device_ids=true, to_apply=%region_7.8 | all-reduce | flops 1 | bytes 8 | tf_op jit(solution)/shard_map/psum | solution.py:141
  214.2 0.8 multiply_add_fusion
  (49 shorter events, 8.9 us)
Async XLA Ops:
  0.6 1.3 copy-start.1
  2.0 3.7 %collective-permute-start = (f32[9,1,8,1024]{3,2,1,0:T(8,128)S(1)}, f32[9,1,8,1024]{3,2,1,0:T(8,128)S(1)}, u32[]{:S(2)}, u32[]{:S(2)}) collective-permute-start(f32[9,1,8,1024]{3,2,1,0:T(8,128)S(1)} %get-tuple-element.47), channel_id=1, source_target_pairs={{0,1},{1,2},{2,3},{4,5},{5,6},{6,7},{8,9},{9,10},{10,11},{12,13},{... | collective-permute-start | bytes 884744 | tf_op jit(solution)/shard_map/ppermute | solution.py:22
  4.4 5.6 %collective-permute-start.1 = (f32[9,1,8,1024]{3,2,1,0:T(8,128)S(1)}, f32[9,1,8,1024]{3,2,1,0:T(8,128)S(1)}, u32[]{:S(2)}, u32[]{:S(2)}) collective-permute-start(f32[9,1,8,1024]{3,2,1,0:T(8,128)S(1)} %get-tuple-element.48), channel_id=1, source_target_pairs={{1,0},{2,1},{3,2},{5,4},{6,5},{7,6},{9,8},{10,9},{11,10},{13,12},{... | collective-permute-start | bytes 884744 | tf_op jit(solution)/shard_map/ppermute | solution.py:25
  10.2 6.8 %collective-permute-start.2 = (f32[9,6,1,1024]{3,2,1,0:T(1,128)S(1)}, f32[9,6,1,1024]{3,2,1,0:T(1,128)S(1)}, u32[]{:S(2)}, u32[]{:S(2)}) collective-permute-start(f32[9,6,1,1024]{3,2,1,0:T(1,128)S(1)} %get-tuple-element.43), channel_id=1, source_target_pairs={{0,4},{4,8},{8,12},{12,16},{16,20},{20,24},{24,28},{1,5},{5,9},{9,... | collective-permute-start | bytes 663560 | tf_op jit(solution)/shard_map/ppermute | solution.py:22
  13.6 7.8 %collective-permute-start.3 = (f32[9,6,1,1024]{3,2,1,0:T(1,128)S(1)}, f32[9,6,1,1024]{3,2,1,0:T(1,128)S(1)}, u32[]{:S(2)}, u32[]{:S(2)}) collective-permute-start(f32[9,6,1,1024]{3,2,1,0:T(1,128)S(1)} %get-tuple-element.44), channel_id=1, source_target_pairs={{4,0},{8,4},{12,8},{16,12},{20,16},{24,20},{28,24},{5,1},{9,5},{13... | collective-permute-start | bytes 663560 | tf_op jit(solution)/shard_map/ppermute | solution.py:25
  15.3 10.9 %copy-start = (f32[6,4,8,1024]{3,2,1,0:T(8,128)S(1)}, f32[6,4,8,1024]{3,2,1,0:T(8,128)}, u32[]{:S(2)}) copy-start(f32[6,4,8,1024]{3,2,1,0:T(8,128)} %param.7) | copy-start | bytes 2359300
  28.8 1.3 copy-start.2
  31.7 7.4 %collective-permute-start.4 = (f32[3,9,1024]{2,0,1:T(4,128)S(1)}, f32[3,9,1024]{2,0,1:T(4,128)S(1)}, u32[]{:S(2)}, u32[]{:S(2)}) collective-permute-start(f32[3,9,1024]{2,0,1:T(4,128)S(1)} %bitcast.31), channel_id=1, source_target_pairs={{0,1},{1,2},{2,3},{4,5},{5,6},{6,7},{8,9},{9,10},{10,11},{12,13},{... | collective-permute-start | bytes 331784 | tf_op jit(solution)/shard_map/ppermute | solution.py:33
  39.2 18.2 %copy-start.3 = (f32[4,8,1024]{2,1,0:T(8,128)S(1)}, f32[4,8,1024]{2,1,0:T(8,128)}, u32[]{:S(2)}) copy-start(f32[4,8,1024]{2,1,0:T(8,128)} %param.9) | copy-start | bytes 393220
  39.3 5.8 %collective-permute-start.5 = (f32[3,4,1024]{2,1,0:T(4,128)S(1)}, f32[3,4,1024]{2,1,0:T(4,128)S(1)}, u32[]{:S(2)}, u32[]{:S(2)}) collective-permute-start(f32[3,4,1024]{2,1,0:T(4,128)S(1)} %bitcast.32), channel_id=1, source_target_pairs={{0,4},{4,8},{8,12},{12,16},{16,20},{20,24},{24,28},{1,5},{5,9},{9,... | collective-permute-start | bytes 147464 | tf_op jit(solution)/shard_map/ppermute | solution.py:33
  45.8 4.7 %collective-permute-start.6 = (f32[3,1,8,1024]{3,2,1,0:T(8,128)S(1)}, f32[3,1,8,1024]{3,2,1,0:T(8,128)S(1)}, u32[]{:S(2)}, u32[]{:S(2)}) collective-permute-start(f32[3,1,8,1024]{3,2,1,0:T(8,128)S(1)} %get-tuple-element.64), channel_id=1, source_target_pairs={{1,0},{2,1},{3,2},{5,4},{6,5},{7,6},{9,8},{10,9},{11,10},{13,12},{... | collective-permute-start | bytes 294920 | tf_op jit(solution)/shard_map/ppermute | solution.py:25
  47.1 4.3 %collective-permute-start.7 = (f32[3,1,8,1024]{3,2,1,0:T(8,128)S(1)}, f32[3,1,8,1024]{3,2,1,0:T(8,128)S(1)}, u32[]{:S(2)}, u32[]{:S(2)}) collective-permute-start(f32[3,1,8,1024]{3,2,1,0:T(8,128)S(1)} %get-tuple-element.63), channel_id=1, source_target_pairs={{0,1},{1,2},{2,3},{4,5},{5,6},{6,7},{8,9},{9,10},{10,11},{12,13},{... | collective-permute-start | bytes 294920 | tf_op jit(solution)/shard_map/ppermute | solution.py:22
  51.5 6.3 %collective-permute-start.8 = (f32[3,6,1,1024]{3,2,1,0:T(1,128)S(1)}, f32[3,6,1,1024]{3,2,1,0:T(1,128)S(1)}, u32[]{:S(2)}, u32[]{:S(2)}) collective-permute-start(f32[3,6,1,1024]{3,2,1,0:T(1,128)S(1)} %get-tuple-element.60), channel_id=1, source_target_pairs={{4,0},{8,4},{12,8},{16,12},{20,16},{24,20},{28,24},{5,1},{9,5},{13... | collective-permute-start | bytes 221192 | tf_op jit(solution)/shard_map/ppermute | solution.py:25
  52.8 6.5 %collective-permute-start.9 = (f32[3,6,1,1024]{3,2,1,0:T(1,128)S(1)}, f32[3,6,1,1024]{3,2,1,0:T(1,128)S(1)}, u32[]{:S(2)}, u32[]{:S(2)}) collective-permute-start(f32[3,6,1,1024]{3,2,1,0:T(1,128)S(1)} %get-tuple-element.59), channel_id=1, source_target_pairs={{0,4},{4,8},{8,12},{12,16},{16,20},{20,24},{24,28},{1,5},{5,9},{9,... | collective-permute-start | bytes 221192 | tf_op jit(solution)/shard_map/ppermute | solution.py:22
  154.1 4.3 %collective-permute-start.10 = (f32[3,1,8,1024]{3,2,1,0:T(8,128)S(1)}, f32[3,1,8,1024]{3,2,1,0:T(8,128)S(1)}, u32[]{:S(2)}, u32[]{:S(2)}) collective-permute-start(f32[3,1,8,1024]{3,2,1,0:T(8,128)S(1)} %get-tuple-element.62), channel_id=1, source_target_pairs={{1,0},{2,1},{3,2},{5,4},{6,5},{7,6},{9,8},{10,9},{11,10},{13,12},{... | collective-permute-start | bytes 294920 | tf_op jit(solution)/shard_map/ppermute | solution.py:25
  155.4 4.0 %collective-permute-start.11 = (f32[3,1,8,1024]{3,2,1,0:T(8,128)S(1)}, f32[3,1,8,1024]{3,2,1,0:T(8,128)S(1)}, u32[]{:S(2)}, u32[]{:S(2)}) collective-permute-start(f32[3,1,8,1024]{3,2,1,0:T(8,128)S(1)} %get-tuple-element.61), channel_id=1, source_target_pairs={{0,1},{1,2},{2,3},{4,5},{5,6},{6,7},{8,9},{9,10},{10,11},{12,13},{... | collective-permute-start | bytes 294920 | tf_op jit(solution)/shard_map/ppermute | solution.py:22
  159.5 6.5 %collective-permute-start.12 = (f32[3,6,1,1024]{3,2,1,0:T(1,128)S(1)}, f32[3,6,1,1024]{3,2,1,0:T(1,128)S(1)}, u32[]{:S(2)}, u32[]{:S(2)}) collective-permute-start(f32[3,6,1,1024]{3,2,1,0:T(1,128)S(1)} %get-tuple-element.58), channel_id=1, source_target_pairs={{4,0},{8,4},{12,8},{16,12},{20,16},{24,20},{28,24},{5,1},{9,5},{13... | collective-permute-start | bytes 221192 | tf_op jit(solution)/shard_map/ppermute | solution.py:25
  160.8 7.0 %collective-permute-start.13 = (f32[3,6,1,1024]{3,2,1,0:T(1,128)S(1)}, f32[3,6,1,1024]{3,2,1,0:T(1,128)S(1)}, u32[]{:S(2)}, u32[]{:S(2)}) collective-permute-start(f32[3,6,1,1024]{3,2,1,0:T(1,128)S(1)} %get-tuple-element.57), channel_id=1, source_target_pairs={{0,4},{4,8},{8,12},{12,16},{16,20},{20,24},{24,28},{1,5},{5,9},{9,... | collective-permute-start | bytes 221192 | tf_op jit(solution)/shard_map/ppermute | solution.py:22
where the time goes:
time: 216 us; the launch traced here: 215 us
  blocking collectives  133 us (62%)
  starting transfers between devices  39.9 us (18%)
  waiting for transfers between devices  19 us (9%)
  other arithmetic  15.7 us (7%)
  between operations  4.93 us (2%)
  local copies, waits for them, and re-layouts  2.43 us (1%)
    psum x2, blocking collectives, squares(): return lax.psum(jnp.sum(residual * residual), ('width', 'thick'))  89.6 us
    psum x1, blocking collectives, on_device(): lax.psum(jnp.sum(direction * mapped), ('width', 'thick'))  43.4 us
    ppermute x6, starting transfers between devices, padded_2(): lax.ppermute(lax.slice_in_dim(block, block.shape[dim] - width, None, axis...  21.6 us
    ppermute x2, starting transfers between devices, shifted(): return lax.ppermute(value, axis, pairs)  10.6 us
    ppermute x6, waiting for transfers between devices, padded_2(): lax.ppermute(lax.slice_in_dim(block, 0, width, axis=dim), axis, backward)  9.44 us
    ppermute x6, starting transfers between devices, padded_2(): lax.ppermute(lax.slice_in_dim(block, 0, width, axis=dim), axis, backward)  7.75 us
    ppermute x6, waiting for transfers between devices, padded_2(): lax.ppermute(lax.slice_in_dim(block, block.shape[dim] - width, None, axis...  6.9 us
    concatenate x5, other arithmetic, padded_2(): block = jnp.concatenate([low, block, high], axis=dim)  6.46 us
  transfers between devices with their start and end apart: 14, of which 11 were waited for; matrix products, arithmetic and copies ran while one was open for 0% of the time, Pallas kernels for 0%

commit v1 on v0

v1 whole, which is shorter than its diff:
```python
import functools

import jax
import jax.numpy as jnp
from jax import lax
from jax.experimental import pallas as pl
from jax.experimental.pallas import tpu as pltpu
from jax.sharding import PartitionSpec as P

TIME_STEP = 0.1
RELAX_TIME = 1.0
MOBILITY = 0.3
MODULUS = 10.0
LANES = 128
AXES = ("width", "thick")
PAIRS = ((0, 0), (1, 1), (2, 2), (0, 1), (0, 2), (1, 2))
SLOT = ((0, 3, 4), (3, 1, 5), (4, 5, 2))
VMEM_LIMIT = 40 * 1024 * 1024


def swap_pairs(wide, thick):
    def flat(fn):
        return [
            (w * thick + t, fn(w, t)[0] * thick + fn(w, t)[1])
            for w in range(wide)
            for t in range(thick)
        ]

    def width_second(w, t):
        return (w, t ^ 1) if w in (0, wide - 1) else (((w - 1) ^ 1) + 1, t)

    def thick_second(w, t):
        return (w ^ 2, t) if t in (0, thick - 1) else (w, ((t - 1) ^ 1) + 1)

    return (
        flat(lambda w, t: (w ^ 1, t)),
        flat(width_second),
        flat(lambda w, t: (w, t ^ 1)),
        flat(thick_second),
    )


def swap(value, pairs):
    return lax.ppermute(value, AXES, pairs)


def as_tiles(x):
    *lead, w, length = x.shape
    x = x.reshape(*lead, w, length // LANES, LANES)
    return jnp.swapaxes(x, -3, -2).reshape(*lead, length // LANES * w, LANES)


def from_tiles(x, w):
    *lead, rows, lanes = x.shape
    x = x.reshape(*lead, rows // w, w, lanes)
    return jnp.swapaxes(x, -3, -2).reshape(*lead, w, rows // w * lanes)


def row_of(ref, lead, w, columns, sub):
    return ref[(*lead, pl.ds(w, sub, stride=columns), slice(None))]


def edge_masks(sub):
    lane = lax.broadcasted_iota(jnp.int32, (sub, LANES), 1)
    row = lax.broadcasted_iota(jnp.int32, (sub, LANES), 0)
    first, last = lane == 0, lane == LANES - 1
    return first, first & (row == 0), last, last & (row == sub - 1)


def before(x, masks):
    first, corner = masks[0], masks[1]
    near = pltpu.roll(x, 1, axis=1)
    far = pltpu.roll(near, 1, axis=0)
    return jnp.where(corner, 0.0, jnp.where(first, far, near))


def after(x, masks):
    last, corner = masks[2], masks[3]
    sub = x.shape[0]
    near = pltpu.roll(x, LANES - 1, axis=1)
    far = pltpu.roll(near, sub - 1, axis=0)
    return jnp.where(corner, 0.0, jnp.where(last, far, near))


def place():
    w, t = lax.axis_index("width"), lax.axis_index("thick")
    return w, t, w % 2 == 0, t % 2 == 0


def pack_kernel(dims, dev, vel, stiff, wa, wb, ta, tb):
    layers, columns, sub = dims
    _, _, w_even, t_even = place()

    def source(c):
        if c < 6:
            return dev, (c,)
        if c < 9:
            return vel, (c - 6,)
        return stiff, ()

    for c in range(10):
        ref, lead = source(c)
        for t in range(layers):
            low = row_of(ref, (*lead, t), 0, columns, sub)
            high = row_of(ref, (*lead, t), columns - 1, columns, sub)
            wa[c, t] = jnp.where(w_even, high, low)
            wb[c, t] = jnp.where(w_even, low, high)
        bottom = ref[(*lead, 0)]
        top = ref[(*lead, layers - 1)]
        ta[c] = jnp.where(t_even, top, bottom)
        tb[c] = jnp.where(t_even, bottom, top)


def advance_kernel(
    dims, ends, dev, vel, wa, wb, ta, tb, new, part, sa, sb, ext, tau
):
    layers, columns, sub = dims
    w_at, t_at, w_even, t_even = place()
    masks = edge_masks(sub)
    zero = jnp.zeros((sub, LANES), jnp.float32)
    w_low, w_high = w_at > 0, w_at < ends[0] - 1
    t_low, t_high = t_at > 0, t_at < ends[1] - 1

    for c in range(9):
        ref, lead = (dev, (c,)) if c < 6 else (vel, (c - 6,))
        for t in range(layers):
            for w in range(columns):
                ext[c, t + 1, w + 1] = row_of(ref, (*lead, t), w, columns, sub)
            a, b = wa[c, t], wb[c, t]
            ext[c, t + 1, 0] = jnp.where(w_low, jnp.where(w_even, b, a), zero)
            ext[c, t + 1, columns + 1] = jnp.where(w_high, jnp.where(w_even, a, b), zero)
        for w in range(columns):
            a = row_of(ta, (c,), w, columns, sub)
            b = row_of(tb, (c,), w, columns, sub)
            ext[c, 0, w + 1] = jnp.where(t_low, jnp.where(t_even, b, a), zero)
            ext[c, layers + 1, w + 1] = jnp.where(t_high, jnp.where(t_even, a, b), zero)

    def cell(t, w):
        def at(c, d, off):
            where = [t + 1, w + 1]
            where[d] = where[d] + off
            return ext[c, where[0], where[1]]

        s = [ext[c, t + 1, w + 1] for c in range(6)]
        u = [ext[6 + c, t + 1, w + 1] for c in range(3)]
        half = 0.5 * TIME_STEP
        grad = [
            [half * (at(6 + i, j, 1) - at(6 + i, j, -1)) for j in range(2)]
            + [half * (after(u[i], masks) - before(u[i], masks))]
            for i in range(3)
        ]
        pos = [TIME_STEP * jnp.maximum(u[d], 0.0) for d in range(3)]
        neg = [TIME_STEP * jnp.minimum(u[d], 0.0) for d in range(3)]
        keep = (1.0 - TIME_STEP / RELAX_TIME) - (
            (pos[0] - neg[0]) + (pos[1] - neg[1]) + (pos[2] - neg[2])
        )
        bend = 0.5 * TIME_STEP * MOBILITY / RELAX_TIME
        scaled = [bend * s[c] for c in range(6)]
        turn = [[grad[i][k] - scaled[SLOT[i][k]] for k in range(3)] for i in range(3)]
        for p, (i, j) in enumerate(PAIRS):
            out = keep * s[p]
            for d in range(2):
                out = out + pos[d] * at(p, d, -1) - neg[d] * at(p, d, 1)
            out = out + pos[2] * before(s[p], masks) - neg[2] * after(s[p], masks)
            if i == j:
                more = grad[i][i]
                for k in range(3):
                    more = more + turn[i][k] * s[SLOT[k][i]]
                out = out + 2.0 * more
            else:
                out = out + (grad[i][j] + grad[j][i])
                for k in range(3):
                    out = out + turn[i][k] * s[SLOT[k][j]] + turn[j][k] * s[SLOT[k][i]]
            tau[p, t, w] = out

    def cells(step, carry):
        t, w = step // (columns // 2), step % (columns // 2)
        cell(t, 2 * w)
        cell(t, 2 * w + 1)
        return carry

    lax.fori_loop(0, layers * columns // 2, cells, 0)

    scale = 0.25 * MODULUS

    def column(w, carry):
        lower = None
        for t in range(layers + 1):
            plus = minus = None
            if t < layers:
                here = [tau[c, t, jnp.minimum(w, columns - 1)] for c in range(6)]
                back = [tau[c, t, jnp.maximum(w - 1, 0)] for c in range(6)]
                here = [jnp.where(w < columns, x, zero) for x in here]
                back = [jnp.where(w > 0, x, zero) for x in back]
                total = {c: here[c] + back[c] for c in (0, 2, 3, 4, 5)}
                delta = {c: here[c] - back[c] for c in (1, 3, 5)}
                level = []
                for i in range(3):
                    x = total[SLOT[i][0]]
                    m, q = delta[SLOT[i][1]], total[SLOT[i][2]]
                    level.append((x, m + q, m - q))
            for i in range(3):
                if t < layers:
                    x, y, z = level[i]
                    plus, minus = x + y, x + z
                    if t > 0:
                        plus, minus = plus + lower[i][0], minus + lower[i][1]
                else:
                    plus, minus = lower[i]
                part[i, t, w] = scale * (plus + before(minus, masks))
            if t < layers:
                lower = [(y - x, z - x) for x, y, z in level]
        return carry

    lax.fori_loop(0, columns + 1, column, 0)

    top = columns - 1
    for i in range(3):
        for t in range(layers + 1):
            for k in range(2):
                low, high = part[i, t, k], part[i, t, top + k]
                sa[i, t, k] = jnp.where(w_even, high, low)
                sb[i, t, k] = jnp.where(w_even, low, high)
    for c in range(6):
        for t in range(layers):
            for w in range(columns):
                new[c, t, pl.ds(w, sub, stride=columns), :] = tau[c, t, w]


def join_kernel(dims, ends, part, wa, wb, full, sa, sb):
    layers, columns, sub = dims
    w_at, t_at, w_even, t_even = place()
    zero = jnp.zeros((sub, LANES), jnp.float32)
    w_low, w_high = w_at > 0, w_at < ends[0] - 1
    for i in range(3):
        for t in range(layers + 1):
            low = [jnp.where(w_low, jnp.where(w_even, wb[i, t, k], wa[i, t, k]), zero) for k in range(2)]
            high = [jnp.where(w_high, jnp.where(w_even, wa[i, t, k], wb[i, t, k]), zero) for k in range(2)]
            full[i, t, 0] = low[0]
            full[i, t, 1] = part[i, t, 0] + low[1]
            for w in range(1, columns):
                full[i, t, w + 1] = part[i, t, w]
            full[i, t, columns + 1] = jnp.where(w_high, part[i, t, columns] + high[0], zero)
            full[i, t, columns + 2] = high[1]
    for i in range(3):
        for w in range(columns + 3):
            for k in range(2):
                low, high = full[i, k, w], full[i, layers - 1 + k, w]
                sa[i, k, w] = jnp.where(t_even, high, low)
                sb[i, k, w] = jnp.where(t_even, low, high)


def krylov_kernel(dims, ends, full, ta, tb, stiff, wsa, wsb, tsa, tsb, force, image, sums, ext, img):
    layers, columns, sub = dims
    w_at, t_at, w_even, t_even = place()
    masks = edge_masks(sub)
    zero = jnp.zeros((sub, LANES), jnp.float32)
    w_high = w_at < ends[0] - 1
    t_low, t_high = t_at > 0, t_at < ends[1] - 1
    for i in range(3):
        for w in range(columns + 3):
            low = [jnp.where(t_low, jnp.where(t_even, tb[i, k, w], ta[i, k, w]), zero) for k in range(2)]
            high = [jnp.where(t_high, jnp.where(t_even, ta[i, k, w], tb[i, k, w]), zero) for k in range(2)]
            ext[i, 0, w] = low[0]
            ext[i, 1, w] = full[i, 0, w] + low[1]
            for t in range(1, layers):
                ext[i, t + 1, w] = full[i, t, w]
            ext[i, layers + 1, w] = jnp.where(t_high, full[i, layers, w] + high[0], zero)
            ext[i, layers + 2, w] = high[1]

    def apply(i, t, w, diagonal):
        here = ext[i, t + 1, w + 1]
        beside = ext[i, t, w + 1] + ext[i, t + 2, w + 1]
        beside = beside + (ext[i, t + 1, w] + ext[i, t + 1, w + 2])
        beside = beside + (before(here, masks) + after(here, masks))
        return here, diagonal * here - beside

    for t in range(layers):
        d = 6.0 + jnp.where(w_even, wsa[t], wsb[t])
        for i in range(3):
            _, g = apply(i, t, columns, d)
            img[i, t, columns] = jnp.where(w_high, g, zero)
    for w in range(columns):
        d = 6.0 + jnp.where(
            t_even, row_of(tsa, (), w, columns, sub), row_of(tsb, (), w, columns, sub)
        )
        for i in range(3):
            _, g = apply(i, layers, w, d)
            img[i, layers, w] = jnp.where(t_high, g, zero)
    for t in range(layers):
        for w in range(columns):
            d = 6.0 + row_of(stiff, (t,), w, columns, sub)
            for i in range(3):
                f, g = apply(i, t, w, d)
                img[i, t, w] = g
                image[i, t, w] = g
                force[i, t, w] = f
    m0 = m1 = m2 = m3 = me = zero
    for t in range(layers):
        for w in range(columns):
            d = 6.0 + row_of(stiff, (t,), w, columns, sub)
            square = zero
            for i in range(3):
                f, g = ext[i, t + 1, w + 1], img[i, t, w]
                m0, m1 = m0 + f * f, m1 + f * g
                square = square + g * g
                me = me + g * (img[i, t + 1, w] + img[i, t, w + 1] + after(g, masks))
            m2, m3 = m2 + square, m3 + d * square
    m3 = m3 - 2.0 * me
    lane = lax.broadcasted_iota(jnp.int32, (1, LANES), 1)
    line = jnp.zeros((1, LANES), jnp.float32)
    for k, m in enumerate((m0, m1, m2, m3)):
        line = jnp.where(lane == k, jnp.sum(m, keepdims=True), line)
    sums[...] = jnp.broadcast_to(line[None], sums.shape)


def finish_kernel(dims, sums, force, image, out):
    layers, columns, sub = dims
    line = jnp.sum(sums[...], axis=0)
    lane = lax.broadcasted_iota(jnp.int32, (1, LANES), 1)
    m0, m1, m2, m3 = [
        jnp.sum(jnp.where(lane == k, line, 0.0), axis=1, keepdims=True) for k in range(4)
    ]
    a1 = m0 / m1
    left = a1 * a1 * m2 - m0
    grow = 1.0 + left / m0
    a2 = left / (grow * grow * m1 - 2.0 * grow * a1 * m2 + a1 * a1 * m3)
    c0 = jnp.broadcast_to(a1 + a2 * grow, (sub, LANES))
    c1 = jnp.broadcast_to(a1 * a2, (sub, LANES))
    for i in range(3):
        for t in range(layers):
            for w in range(columns):
                out[i, t, pl.ds(w, sub, stride=columns), :] = (
                    c0 * force[i, t, w] - c1 * image[i, t, w]
                )


def call(kernel, shapes, scratch=()):
    return pl.pallas_call(
        kernel,
        out_shape=[jax.ShapeDtypeStruct(s, jnp.float32) for s in shapes],
        scratch_shapes=[pltpu.VMEM(s, jnp.float32) for s in scratch],
        compiler_params=pltpu.CompilerParams(vmem_limit_bytes=VMEM_LIMIT),
    )


def on_device(ends, deviation, velocity, stiffness):
    _, layers, columns, length = deviation.shape
    sub = length // LANES
    dims = (layers, columns, sub)
    rows = columns * sub
    tile = (sub, LANES)
    w_first, w_second, t_first, t_second = swap_pairs(*ends)
    dev, vel, stiff = as_tiles(deviation), as_tiles(velocity), as_tiles(stiffness)

    wa, wb, ta, tb = call(
        functools.partial(pack_kernel, dims),
        [(10, layers, *tile)] * 2 + [(10, rows, LANES)] * 2,
    )(dev, vel, stiff)
    wa, wb = swap(wa, w_first), swap(wb, w_second)
    ta, tb = swap(ta, t_first), swap(tb, t_second)

    new, part, sa, sb = call(
        functools.partial(advance_kernel, dims, ends),
        [(6, layers, rows, LANES), (3, layers + 1, columns + 1, *tile)]
        + [(3, layers + 1, 2, *tile)] * 2,
        [(9, layers + 2, columns + 2, *tile), (6, layers, columns, *tile)],
    )(dev, vel, wa, wb, ta, tb)
    sa, sb = swap(sa, w_first), swap(sb, w_second)

    full, sa, sb = call(
        functools.partial(join_kernel, dims, ends),
        [(3, layers + 1, columns + 3, *tile)] + [(3, 2, columns + 3, *tile)] * 2,
    )(part, sa, sb)
    sa, sb = swap(sa, t_first), swap(sb, t_second)

    force, image, sums = call(
        functools.partial(krylov_kernel, dims, ends),
        [(3, layers, columns, *tile)] * 2 + [(ends[0] * ends[1], 1, LANES)],
        [(3, layers + 3, columns + 3, *tile), (3, layers + 1, columns + 1, *tile)],
    )(full, sa, sb, stiff, wa[9], wb[9], ta[9], tb[9])
    sums = lax.all_to_all(sums, AXES, 0, 0, tiled=True)

    (out,) = call(functools.partial(finish_kernel, dims), [(3, layers, rows, LANES)])(
        sums, force, image
    )
    return from_tiles(new, columns), from_tiles(out, columns)


def solution(mesh):
    placed = (
        P(None, "thick", "width", None),
        P(None, "thick", "width", None),
        P("thick", "width", None),
    )
    ends = (mesh.shape["width"], mesh.shape["thick"])
    return jax.shard_map(
        functools.partial(on_device, ends),
        mesh=mesh,
        in_specs=placed,
        out_specs=(P(None, "thick", "width", None), P(None, "thick", "width", None)),
        check_vma=False,
    )
```

time: 216 us -> 48.1 us (0.22)
  blocking collectives: 133 us -> 12.2 us
  starting transfers between devices: 39.9 us -> 10.5 us
  other arithmetic: 15.7 us -> 0 us
  Pallas kernels: 0 us -> 6.02 us
  between operations: 4.93 us -> 0.69 us
  waiting for transfers between devices: 19 us -> 15.4 us
    psum x3 -> x0, blocking collectives: 133 us -> none  [the longest x2 89.6 us: squares(): return lax.psum(jnp.sum(residual * residual), ('width', 'thick'))]
    ppermute x14 -> x8, starting transfers between devices: 39.9 us -> 10.5 us  [swap(): return lax.ppermute(value, AXES, pairs)]
    all_to_all x0 -> x1, blocking collectives: none -> 12.2 us  [on_device(): sums = lax.all_to_all(sums, AXES, 0, 0, tiled=True)]
    concatenate x5 -> x0, other arithmetic: 6.46 us -> none  [padded_2(): block = jnp.concatenate([low, block, high], axis=dim)]
    pallas_call x0 -> x5, Pallas kernels: none -> 6.02 us  [the longest x1 4.17 us: on_device(): call(functools.partial(advance_kernel, dims, ends), [(6, layers, rows, LA...]
    ppermute x14 -> x8, waiting for transfers between devices: 19 us -> 15.4 us  [swap(): return lax.ppermute(value, AXES, pairs)]
    reduce_sum x3 -> x0, other arithmetic: 2.64 us -> none  [the longest x2 1.93 us: on_device(): jnp.sum(direction * mapped)]
  transfers between devices with their start and end apart: 14 -> 8, of which waited for: 11 -> 4; matrix products, arithmetic and copies ran while one was open for 0% -> 0% of each run, Pallas kernels for 0% -> 0%
where the time goes in v1:
time: 48.1 us; the launch traced here: 47.9 us
  waiting for transfers between devices  15.4 us (32%)
  blocking collectives  12.2 us (25%)
  starting transfers between devices  10.5 us (22%)
  Pallas kernels  6.02 us (13%)
  local copies, waits for them, and re-layouts  3.04 us (6%)
  between operations  0.69 us (1%)
    ppermute x8, waiting for transfers between devices, swap(): return lax.ppermute(value, AXES, pairs)  15.4 us
    all_to_all x1, blocking collectives, on_device(): sums = lax.all_to_all(sums, AXES, 0, 0, tiled=True)  12.2 us
    ppermute x8, starting transfers between devices, swap(): return lax.ppermute(value, AXES, pairs)  10.5 us
    pallas_call x1, Pallas kernels, on_device(): call(functools.partial(advance_kernel, dims, ends), [(6, layers, rows, LA...  4.17 us
    unnamed x8, local copies, waits for them, and re-layouts  3.03 us
  transfers between devices with their start and end apart: 8, of which 4 were waited for; matrix products, arithmetic and copies ran while one was open for 0% of the time, Pallas kernels for 0%

profile of v1, /device:TPU:0, one launch (start us, length us, event | category | flops | bytes accessed | tf_op | source)
XLA Modules:
  0.0 47.9 jit_solution(10771627732121733077)
XLA Ops:
  0.6 0.0 copy-start
  0.6 1.1 %copy-done = f32[6,4,8,1024]{3,2,1,0:T(8,128)S(1)} copy-done((f32[6,4,8,1024]{3,2,1,0:T(8,128)S(1)}, f32[6,4,8,1024]{3,2,1,0:T(8,128)}, u32[]{:S(2)}) %copy-start) | copy-done | bytes 786456
  1.8 0.0 copy-start.1
  1.8 1.0 %copy-done.1 = f32[3,4,8,1024]{3,2,1,0:T(8,128)S(1)} copy-done((f32[3,4,8,1024]{3,2,1,0:T(8,128)S(1)}, f32[3,4,8,1024]{3,2,1,0:T(8,128)}, u32[]{:S(2)}) %copy-start.1) | copy-done | bytes 393240
  2.8 0.0 copy-start.2
  2.8 0.9 %copy-done.2 = f32[4,8,1024]{2,1,0:T(8,128)S(1)} copy-done((f32[4,8,1024]{2,1,0:T(8,128)S(1)}, f32[4,8,1024]{2,1,0:T(8,128)}, u32[]{:S(2)}) %copy-start.2) | copy-done | bytes 131096
  3.7 0.1 shard_map.50
  3.8 3.0 %collective-permute-start = (f32[10,4,8,128]{3,2,1,0:T(8,128)S(1)}, f32[10,4,8,128]{3,2,1,0:T(8,128)S(1)}, u32[]{:S(2)}, u32[]{:S(2)}) collective-permute-start(f32[10,4,8,128]{3,2,1,0:T(8,128)S(1)} %get-tuple-element.16), channel_id=1, source_target_pairs={{0,4},{1,5},{2,6},{3,7},{4,0},{5,1},{6,2},{7,3},{8,12},{9,13},{10,... | collective-permute-start | bytes 491528 | tf_op jit(solution)/shard_map/ppermute | solution.py:44
  6.8 0.0 collective-permute-start.2
  6.8 1.6 %collective-permute-start.3 = (f32[10,64,128]{2,1,0:T(8,128)S(1)}, f32[10,64,128]{2,1,0:T(8,128)S(1)}, u32[]{:S(2)}, u32[]{:S(2)}) collective-permute-start(f32[10,64,128]{2,1,0:T(8,128)S(1)} %get-tuple-element.19), channel_id=1, source_target_pairs={{0,8},{1,2},{2,1},{3,11},{4,12},{5,6},{6,5},{7,15},{8,0},{9,10},{1... | collective-permute-start | bytes 983048 | tf_op jit(solution)/shard_map/ppermute | solution.py:44
  8.4 0.1 collective-permute-start.1
  8.4 2.6 %collective-permute-done.wa = f32[10,4,8,128]{3,2,1,0:T(8,128)S(1)} collective-permute-done((f32[10,4,8,128]{3,2,1,0:T(8,128)S(1)}, f32[10,4,8,128]{3,2,1,0:T(8,128)S(1)}, u32[]{:S(2)}, u32[]{:S(2)}) %collective-permute-start) | collective-permute-done | bytes 163872 | tf_op jit(solution)/shard_map/ppermute | solution.py:44
  11.0 0.0 collective-permute-done.1.wb
  11.0 0.0 collective-permute-done.2.ta
  11.0 4.6 %collective-permute-done.3.tb = f32[10,64,128]{2,1,0:T(8,128)S(1)} collective-permute-done((f32[10,64,128]{2,1,0:T(8,128)S(1)}, f32[10,64,128]{2,1,0:T(8,128)S(1)}, u32[]{:S(2)}, u32[]{:S(2)}) %collective-permute-start.3) | collective-permute-done | bytes 327712 | tf_op jit(solution)/shard_map/ppermute | solution.py:44
  15.6 4.2 %shard_map.51 = (f32[6,4,64,128]{3,2,1,0:T(8,128)}, f32[3,5,9,8,128]{4,3,2,1,0:T(8,128)S(1)}, f32[3,5,2,8,128]{4,3,2,1,0:T(8,128)S(1)}, f32[3,5,2,8,128]{4,3,2,1,0:T(8,128)S(1)}) custom-call(f32[6,4,64,128]{3,2,1,0:T(8,128)S(1)} %bitcast.34, f32[3,4,64,128]{3,2,1,0:T(8,128)S(1)} %bitcast.36, f32[10,4,8,128]{3,2,1,0:T(8,128)S(1)} %collective-permute-done.wa, ...), custom_call_target="tpu_custom_call" | custom-call | tf_op jit(solution)/shard_map/pallas_call | solution.py:363
  19.8 3.2 %collective-permute-start.4 = (f32[3,5,2,8,128]{4,3,2,1,0:T(8,128)S(1)}, f32[3,5,2,8,128]{4,3,2,1,0:T(8,128)S(1)}, u32[]{:S(2)}, u32[]{:S(2)}) collective-permute-start(f32[3,5,2,8,128]{4,3,2,1,0:T(8,128)S(1)} %get-tuple-element.22), channel_id=1, source_target_pairs={{0,4},{1,5},{2,6},{3,7},{4,0},{5,1},{6,2},{7,3},{8,12},{9,13},{10,... | collective-permute-start | bytes 368648 | tf_op jit(solution)/shard_map/ppermute | solution.py:44
  23.0 0.0 collective-permute-start.5
  23.0 3.7 %collective-permute-done.4.wa = f32[3,5,2,8,128]{4,3,2,1,0:T(8,128)S(1)} collective-permute-done((f32[3,5,2,8,128]{4,3,2,1,0:T(8,128)S(1)}, f32[3,5,2,8,128]{4,3,2,1,0:T(8,128)S(1)}, u32[]{:S(2)}, u32[]{:S(2)}) %collective-permute-start.4) | collective-permute-done | bytes 122912 | tf_op jit(solution)/shard_map/ppermute | solution.py:44
  26.8 0.0 collective-permute-done.5.wb
  26.8 0.1 shard_map.52
  26.9 0.0 copy-start.3
  26.9 0.1 collective-permute-start.6
  26.9 2.6 %collective-permute-start.7 = (f32[3,2,11,8,128]{4,3,2,1,0:T(8,128)S(1)}, f32[3,2,11,8,128]{4,3,2,1,0:T(8,128)S(1)}, u32[]{:S(2)}, u32[]{:S(2)}) collective-permute-start(f32[3,2,11,8,128]{4,3,2,1,0:T(8,128)S(1)} %get-tuple-element.26), channel_id=1, source_target_pairs={{0,8},{1,2},{2,1},{3,11},{4,12},{5,6},{6,5},{7,15},{8,0},{9,10},{1... | collective-permute-start | bytes 811016 | tf_op jit(solution)/shard_map/ppermute | solution.py:44
  29.6 0.0 collective-permute-done.6.ta
  29.6 4.4 %collective-permute-done.7.tb = f32[3,2,11,8,128]{4,3,2,1,0:T(8,128)S(1)} collective-permute-done((f32[3,2,11,8,128]{4,3,2,1,0:T(8,128)S(1)}, f32[3,2,11,8,128]{4,3,2,1,0:T(8,128)S(1)}, u32[]{:S(2)}, u32[]{:S(2)}) %collective-permute-start.7) | collective-permute-done | bytes 270368 | tf_op jit(solution)/shard_map/ppermute | solution.py:44
  34.0 0.0 copy-done.3
  34.0 0.7 %shard_map.53 = (f32[3,4,8,8,128]{4,3,2,1,0:T(8,128)S(1)}, f32[3,4,8,8,128]{4,3,2,1,0:T(8,128)S(1)}, f32[32,1,128]{2,1,0:T(1,128)S(1)}) custom-call(f32[3,5,11,8,128]{4,3,2,1,0:T(8,128)S(1)} %get-tuple-element.24.full, f32[3,2,11,8,128]{4,3,2,1,0:T(8,128)S(1)} %collective-permute-done.6.ta, f32[3,2,11,8,128]{4,3,2,1,0:T(8,128)S(1)} %collective-permute-done.7.tb, ...), custom_call_target="tpu_custom_call" | custom-call | tf_op jit(solution)/shard_map/pallas_call | solution.py:377
  34.7 12.2 %all_to_all.5.sums = f32[32,1,128]{2,1,0:T(1,128)S(1)} all-to-all(f32[32,1,128]{2,1,0:T(1,128)S(1)} %get-tuple-element.27), channel_id=1, replica_groups=mesh['width'=8,'thick'=4] {'width','thick'}, dimensions={0} | all-to-all | bytes 32768 | tf_op jit(solution)/shard_map/all_to_all | solution.py:382
  46.9 0.9 %shard_map.54 = f32[3,4,64,128]{3,2,1,0:T(8,128)} custom-call(f32[32,1,128]{2,1,0:T(1,128)S(1)} %all_to_all.5.sums, f32[3,4,8,8,128]{4,3,2,1,0:T(8,128)S(1)} %get-tuple-element.28.force, f32[3,4,8,8,128]{4,3,2,1,0:T(8,128)S(1)} %get-tuple-element.29.image), custom_call_target="tpu_custom_call" | custom-call | tf_op jit(solution)/shard_map/pallas_call | solution.py:384
  (4 shorter events, 0.0 us)
Async XLA Ops:
  0.6 1.1 %copy-start = (f32[6,4,8,1024]{3,2,1,0:T(8,128)S(1)}, f32[6,4,8,1024]{3,2,1,0:T(8,128)}, u32[]{:S(2)}) copy-start(f32[6,4,8,1024]{3,2,1,0:T(8,128)} %param.3) | copy-start | bytes 2359300
  1.8 1.0 %copy-start.1 = (f32[3,4,8,1024]{3,2,1,0:T(8,128)S(1)}, f32[3,4,8,1024]{3,2,1,0:T(8,128)}, u32[]{:S(2)}) copy-start(f32[3,4,8,1024]{3,2,1,0:T(8,128)} %param.4) | copy-start | bytes 1179652
  2.8 0.9 %copy-start.2 = (f32[4,8,1024]{2,1,0:T(8,128)S(1)}, f32[4,8,1024]{2,1,0:T(8,128)}, u32[]{:S(2)}) copy-start(f32[4,8,1024]{2,1,0:T(8,128)} %param.5) | copy-start | bytes 393220
  3.8 7.2 %collective-permute-start = (f32[10,4,8,128]{3,2,1,0:T(8,128)S(1)}, f32[10,4,8,128]{3,2,1,0:T(8,128)S(1)}, u32[]{:S(2)}, u32[]{:S(2)}) collective-permute-start(f32[10,4,8,128]{3,2,1,0:T(8,128)S(1)} %get-tuple-element.16), channel_id=1, source_target_pairs={{0,4},{1,5},{2,6},{3,7},{4,0},{5,1},{6,2},{7,3},{8,12},{9,13},{10,... | collective-permute-start | bytes 491528 | tf_op jit(solution)/shard_map/ppermute | solution.py:44
  6.8 4.2 %collective-permute-start.2 = (f32[10,64,128]{2,1,0:T(8,128)S(1)}, f32[10,64,128]{2,1,0:T(8,128)S(1)}, u32[]{:S(2)}, u32[]{:S(2)}) collective-permute-start(f32[10,64,128]{2,1,0:T(8,128)S(1)} %get-tuple-element.18), channel_id=1, source_target_pairs={{0,1},{1,0},{2,3},{3,2},{4,5},{5,4},{6,7},{7,6},{8,9},{9,8},{10,11... | collective-permute-start | bytes 983048 | tf_op jit(solution)/shard_map/ppermute | solution.py:44
  6.8 8.8 %collective-permute-start.3 = (f32[10,64,128]{2,1,0:T(8,128)S(1)}, f32[10,64,128]{2,1,0:T(8,128)S(1)}, u32[]{:S(2)}, u32[]{:S(2)}) collective-permute-start(f32[10,64,128]{2,1,0:T(8,128)S(1)} %get-tuple-element.19), channel_id=1, source_target_pairs={{0,8},{1,2},{2,1},{3,11},{4,12},{5,6},{6,5},{7,15},{8,0},{9,10},{1... | collective-permute-start | bytes 983048 | tf_op jit(solution)/shard_map/ppermute | solution.py:44
  8.4 2.6 %collective-permute-start.1 = (f32[10,4,8,128]{3,2,1,0:T(8,128)S(1)}, f32[10,4,8,128]{3,2,1,0:T(8,128)S(1)}, u32[]{:S(2)}, u32[]{:S(2)}) collective-permute-start(f32[10,4,8,128]{3,2,1,0:T(8,128)S(1)} %get-tuple-element.17), channel_id=1, source_target_pairs={{0,1},{1,0},{2,3},{3,2},{4,8},{5,9},{6,10},{7,11},{8,4},{9,5},{10,... | collective-permute-start | bytes 491528 | tf_op jit(solution)/shard_map/ppermute | solution.py:44
  19.8 7.0 %collective-permute-start.4 = (f32[3,5,2,8,128]{4,3,2,1,0:T(8,128)S(1)}, f32[3,5,2,8,128]{4,3,2,1,0:T(8,128)S(1)}, u32[]{:S(2)}, u32[]{:S(2)}) collective-permute-start(f32[3,5,2,8,128]{4,3,2,1,0:T(8,128)S(1)} %get-tuple-element.22), channel_id=1, source_target_pairs={{0,4},{1,5},{2,6},{3,7},{4,0},{5,1},{6,2},{7,3},{8,12},{9,13},{10,... | collective-permute-start | bytes 368648 | tf_op jit(solution)/shard_map/ppermute | solution.py:44
  23.0 3.8 %collective-permute-start.5 = (f32[3,5,2,8,128]{4,3,2,1,0:T(8,128)S(1)}, f32[3,5,2,8,128]{4,3,2,1,0:T(8,128)S(1)}, u32[]{:S(2)}, u32[]{:S(2)}) collective-permute-start(f32[3,5,2,8,128]{4,3,2,1,0:T(8,128)S(1)} %get-tuple-element.23), channel_id=1, source_target_pairs={{0,1},{1,0},{2,3},{3,2},{4,8},{5,9},{6,10},{7,11},{8,4},{9,5},{10,... | collective-permute-start | bytes 368648 | tf_op jit(solution)/shard_map/ppermute | solution.py:44
  26.9 7.1 %copy-start.3 = (f32[4,8,1024]{2,1,0:T(8,128)S(1)}, f32[4,8,1024]{2,1,0:T(8,128)}, u32[]{:S(2)}) copy-start(f32[4,8,1024]{2,1,0:T(8,128)} %param.5) | copy-start | bytes 393220
  26.9 2.7 %collective-permute-start.6 = (f32[3,2,11,8,128]{4,3,2,1,0:T(8,128)S(1)}, f32[3,2,11,8,128]{4,3,2,1,0:T(8,128)S(1)}, u32[]{:S(2)}, u32[]{:S(2)}) collective-permute-start(f32[3,2,11,8,128]{4,3,2,1,0:T(8,128)S(1)} %get-tuple-element.25), channel_id=1, source_target_pairs={{0,1},{1,0},{2,3},{3,2},{4,5},{5,4},{6,7},{7,6},{8,9},{9,8},{10,11... | collective-permute-start | bytes 811016 | tf_op jit(solution)/shard_map/ppermute | solution.py:44
  26.9 7.0 %collective-permute-start.7 = (f32[3,2,11,8,128]{4,3,2,1,0:T(8,128)S(1)}, f32[3,2,11,8,128]{4,3,2,1,0:T(8,128)S(1)}, u32[]{:S(2)}, u32[]{:S(2)}) collective-permute-start(f32[3,2,11,8,128]{4,3,2,1,0:T(8,128)S(1)} %get-tuple-element.26), channel_id=1, source_target_pairs={{0,8},{1,2},{2,1},{3,11},{4,12},{5,6},{6,5},{7,15},{8,0},{9,10},{1... | collective-permute-start | bytes 811016 | tf_op jit(solution)/shard_map/ppermute | solution.py:44

commit v2 on v1

v2 whole, which is shorter than its diff:
```python
import functools

import jax
import jax.numpy as jnp
from jax import lax
from jax.experimental import pallas as pl
from jax.experimental.pallas import tpu as pltpu
from jax.sharding import PartitionSpec as P

TIME_STEP = 0.1
RELAX_TIME = 1.0
MOBILITY = 0.3
MODULUS = 10.0
LANES = 128
AXES = ("width", "thick")
PAIRS = ((0, 0), (1, 1), (2, 2), (0, 1), (0, 2), (1, 2))
SLOT = ((0, 3, 4), (3, 1, 5), (4, 5, 2))
VMEM_LIMIT = 40 * 1024 * 1024
PACK_LIMIT = 53 * 1024 * 1024


def swap_pairs(wide, thick):
    def flat(fn):
        return [
            (w * thick + t, fn(w, t)[0] * thick + fn(w, t)[1])
            for w in range(wide)
            for t in range(thick)
        ]

    def width_second(w, t):
        return (w, t ^ 1) if w in (0, wide - 1) else (((w - 1) ^ 1) + 1, t)

    def thick_second(w, t):
        return (w, thick - 1 - t) if t in (0, thick - 1) else (w, ((t - 1) ^ 1) + 1)

    return (
        flat(lambda w, t: (w ^ 1, t)),
        flat(width_second),
        flat(lambda w, t: (w, t ^ 1)),
        flat(thick_second),
    )


def swap(value, pairs):
    return lax.ppermute(value, AXES, pairs)


def as_tiles(x):
    *lead, w, length = x.shape
    x = x.reshape(*lead, w, length // LANES, LANES)
    return jnp.swapaxes(x, -3, -2).reshape(*lead, length // LANES * w, LANES)


def from_tiles(x, w):
    *lead, rows, lanes = x.shape
    x = x.reshape(*lead, rows // w, w, lanes)
    return jnp.swapaxes(x, -3, -2).reshape(*lead, w, rows // w * lanes)


def row_of(ref, lead, w, columns, sub):
    return ref[(*lead, pl.ds(w, sub, stride=columns), slice(None))]


def edge_masks(sub):
    lane = lax.broadcasted_iota(jnp.int32, (sub, LANES), 1)
    row = lax.broadcasted_iota(jnp.int32, (sub, LANES), 0)
    first, last = lane == 0, lane == LANES - 1
    return first, first & (row == 0), last, last & (row == sub - 1)


def before(x, masks):
    first, corner = masks[0], masks[1]
    near = pltpu.roll(x, 1, axis=1)
    far = pltpu.roll(near, 1, axis=0)
    return jnp.where(corner, 0.0, jnp.where(first, far, near))


def after(x, masks):
    last, corner = masks[2], masks[3]
    sub = x.shape[0]
    near = pltpu.roll(x, LANES - 1, axis=1)
    far = pltpu.roll(near, sub - 1, axis=0)
    return jnp.where(corner, 0.0, jnp.where(last, far, near))


def halves(axis, end):
    at = lax.axis_index(axis)
    even = at % 2 == 0
    has_low, has_high = at > 0, at < end - 1

    def low(first, second):
        return jnp.where(has_low, jnp.where(even, second, first), 0.0)

    def high(first, second):
        return jnp.where(has_high, jnp.where(even, first, second), 0.0)

    def send(low_face, high_face):
        return jnp.where(even, high_face, low_face), jnp.where(even, low_face, high_face)

    return low, high, send, has_high


def fetch(sources, targets, sems):
    copies = []
    for source, target in zip(sources, targets):
        for c in range(source.shape[0]):
            copies.append(pltpu.make_async_copy(source.at[c], target.at[c], sems.at[len(copies)]))
    for copy in copies:
        copy.start()
    for copy in copies:
        copy.wait()


def pack_kernel(dims, ends, dev_hbm, vel_hbm, wa, wb, ta, tb, dev, vel, sems):
    layers, columns, sub = dims
    send_w = halves("width", ends[0])[2]
    send_t = halves("thick", ends[1])[2]
    fetch((dev_hbm, vel_hbm), (dev, vel), sems)
    for c in range(9):
        ref, lead = (dev, (c,)) if c < 6 else (vel, (c - 6,))
        for t in range(layers):
            low = row_of(ref, (*lead, t), 0, columns, sub)
            high = row_of(ref, (*lead, t), columns - 1, columns, sub)
            wa[c, t], wb[c, t] = send_w(low, high)
        ta[c], tb[c] = send_t(ref[(*lead, 0)], ref[(*lead, layers - 1)])


HALF = 0.5 * TIME_STEP


def inner_kernel(dims, dev, vel, after_pack, ext, tau):
    layers, columns, sub = dims
    masks = edge_masks(sub)
    zero = jnp.zeros((sub, LANES), jnp.float32)
    for c in range(9):
        ref, lead = (dev, (c,)) if c < 6 else (vel, (c - 6,))
        for t in range(layers):
            for w in range(columns):
                ext[c, t + 1, w + 1] = row_of(ref, (*lead, t), w, columns, sub)
            ext[c, t + 1, 0] = zero
            ext[c, t + 1, columns + 1] = zero
        for w in range(columns):
            ext[c, 0, w + 1] = zero
            ext[c, layers + 1, w + 1] = zero

    def cell(t, w):
        def at(c, d, off):
            where = [t + 1, w + 1]
            where[d] = where[d] + off
            return ext[c, where[0], where[1]]

        s = [ext[c, t + 1, w + 1] for c in range(6)]
        u = [ext[6 + c, t + 1, w + 1] for c in range(3)]
        grad = [
            [HALF * (at(6 + i, j, 1) - at(6 + i, j, -1)) for j in range(2)]
            + [HALF * (after(u[i], masks) - before(u[i], masks))]
            for i in range(3)
        ]
        pos = [TIME_STEP * jnp.maximum(u[d], 0.0) for d in range(3)]
        neg = [TIME_STEP * jnp.minimum(u[d], 0.0) for d in range(3)]
        keep = (1.0 - TIME_STEP / RELAX_TIME) - (
            (pos[0] - neg[0]) + (pos[1] - neg[1]) + (pos[2] - neg[2])
        )
        bend = HALF * MOBILITY / RELAX_TIME
        scaled = [bend * s[c] for c in range(6)]
        turn = [[grad[i][k] - scaled[SLOT[i][k]] for k in range(3)] for i in range(3)]
        for p, (i, j) in enumerate(PAIRS):
            out = keep * s[p]
            for d in range(2):
                out = out + pos[d] * at(p, d, -1) - neg[d] * at(p, d, 1)
            out = out + pos[2] * before(s[p], masks) - neg[2] * after(s[p], masks)
            if i == j:
                more = grad[i][i]
                for k in range(3):
                    more = more + turn[i][k] * s[SLOT[k][i]]
                out = out + 2.0 * more
            else:
                out = out + (grad[i][j] + grad[j][i])
                for k in range(3):
                    out = out + turn[i][k] * s[SLOT[k][j]] + turn[j][k] * s[SLOT[k][i]]
            tau[p, t, w] = out

    def cells(step, carry):
        t, w = step // (columns // 2), step % (columns // 2)
        cell(t, 2 * w)
        cell(t, 2 * w + 1)
        return carry

    lax.fori_loop(0, layers * columns // 2, cells, 0)


def nodes(dims, tau, columns_of_nodes, put):
    layers, columns, sub = dims
    masks = edge_masks(sub)
    scale = 0.25 * MODULUS
    for w in columns_of_nodes:
        lower = None
        for t in range(layers + 1):
            level = []
            if t < layers:
                here = [tau[c, t, w] for c in range(6)] if w < columns else None
                back = [tau[c, t, w - 1] for c in range(6)] if w > 0 else None
                if here is None:
                    total, delta = back, [-x for x in back]
                elif back is None:
                    total = delta = here
                else:
                    total = [a + b for a, b in zip(here, back)]
                    delta = [a - b for a, b in zip(here, back)]
                for i in range(3):
                    m, q = delta[SLOT[i][1]], total[SLOT[i][2]]
                    level.append((total[SLOT[i][0]], m + q, m - q))
            for i in range(3):
                if t < layers:
                    x, y, z = level[i]
                    plus, minus = x + y, x + z
                    if t > 0:
                        plus, minus = plus + lower[i][0], minus + lower[i][1]
                else:
                    plus, minus = lower[i]
                put(i, t, w, scale * (plus + before(minus, masks)))
            lower = [(y - x, z - x) for x, y, z in level]


def outer_kernel(dims, ends, tau_in, ext, wa, wb, ta, tb, stiff, tau, part, sa, sb):
    layers, columns, sub = dims
    w_low, w_high, send_w, _ = halves("width", ends[0])
    t_low, t_high, _, _ = halves("thick", ends[1])

    def correct(t, w, d, sign, halo):
        s = [ext[c, t + 1, w + 1] for c in range(6)]
        u = ext[6 + d, t + 1, w + 1]
        speed = jnp.maximum(u, 0.0) if sign < 0 else -jnp.minimum(u, 0.0)
        speed = TIME_STEP * speed
        h = [(sign * HALF) * halo[6 + i] for i in range(3)]
        q = [s[SLOT[d][j]] for j in range(3)]
        q[d] = q[d] + 1.0
        for p, (i, j) in enumerate(PAIRS):
            bent = 2.0 * (h[i] * q[i]) if i == j else h[i] * q[j] + h[j] * q[i]
            tau[p, t, w] = tau[p, t, w] + (speed * halo[p] + bent)

    def side(t, carry):
        a, b = [wa[c, t] for c in range(9)], [wb[c, t] for c in range(9)]
        correct(t, 0, 1, -1.0, [w_low(x, y) for x, y in zip(a, b)])
        correct(t, columns - 1, 1, 1.0, [w_high(x, y) for x, y in zip(a, b)])
        return carry

    lax.fori_loop(0, layers, side, 0)
    for w in range(columns):
        a = [row_of(ta, (c,), w, columns, sub) for c in range(9)]
        b = [row_of(tb, (c,), w, columns, sub) for c in range(9)]
        correct(0, w, 0, -1.0, [t_low(x, y) for x, y in zip(a, b)])
        correct(layers - 1, w, 0, 1.0, [t_high(x, y) for x, y in zip(a, b)])

    slot = {0: 0, 1: 1, columns - 1: 2, columns: 3}

    def put(i, t, w, value):
        part[i, t, slot[w]] = value

    nodes(dims, tau, slot, put)
    count = 2 * (layers + 1)
    for i in range(3):
        for t in range(layers + 1):
            for k in range(2):
                at = i * count + t * 2 + k
                sa[at], sb[at] = send_w(part[i, t, k], part[i, t, 2 + k])
    for t in range(layers):
        row = row_of(stiff, (t,), 0, columns, sub)
        sa[3 * count + t] = row
        sb[3 * count + t] = row


def middle_kernel(dims, ends, tau, part, stiff, mid, sa, sb):
    layers, columns, sub = dims
    send_t = halves("thick", ends[1])[2]

    def put(i, t, w, value):
        mid[i, t, w - 1] = value

    nodes(dims, tau, range(2, columns - 1), put)
    for i in range(3):
        for t in range(layers + 1):
            mid[i, t, 0] = part[i, t, 1]
            mid[i, t, columns - 2] = part[i, t, 2]
    inner = columns - 1
    for i in range(3):
        for k in range(2):
            for w in range(inner):
                at = (i * 2 + k) * inner + w
                sa[at], sb[at] = send_t(mid[i, k, w], mid[i, layers - 1 + k, w])
    for w in range(columns):
        row = row_of(stiff, (0,), w, columns, sub)
        sa[6 * inner + w] = row
        sb[6 * inner + w] = row


def emit_kernel(dims, tau, after_join, new):
    layers, columns, sub = dims
    for c in range(6):
        for t in range(layers):
            for w in range(columns):
                new[c, t, pl.ds(w, sub, stride=columns), :] = tau[c, t, w]


def join_kernel(dims, ends, part, wa, wb, side, sa, sb):
    layers, columns, sub = dims
    w_low, w_high, _, has_high = halves("width", ends[0])
    send_t = halves("thick", ends[1])[2]
    count = 2 * (layers + 1)
    for i in range(3):
        for t in range(layers + 1):
            at = i * count + t * 2
            below = [w_low(wa[at + k], wb[at + k]) for k in range(2)]
            above = [w_high(wa[at + k], wb[at + k]) for k in range(2)]
            side[i, t, 0] = below[0]
            side[i, t, 1] = part[i, t, 0] + below[1]
            side[i, t, 2] = jnp.where(has_high, part[i, t, 3] + above[0], 0.0)
            side[i, t, 3] = above[1]
    for i in range(3):
        for k in range(2):
            for w in range(4):
                at = (i * 2 + k) * 4 + w
                sa[at], sb[at] = send_t(side[i, k, w], side[i, layers - 1 + k, w])


def krylov_kernel(
    dims, ends, mid, side, ma, mb, ja, jb, wa, wb, stiff, force, image, sums, ext, img
):
    layers, columns, sub = dims
    w_high = halves("width", ends[0])[1]
    has_right = halves("width", ends[0])[3]
    t_low, t_high, _, has_top = halves("thick", ends[1])
    masks = edge_masks(sub)
    zero = jnp.zeros((sub, LANES), jnp.float32)
    inner = columns - 1
    edge = {0: 0, 1: 1, columns + 1: 2, columns + 2: 3}
    for i in range(3):
        for w in range(columns + 3):
            if w in edge:
                own, a, b, at, step = side, ja, jb, edge[w], 4
            else:
                own, a, b, at, step = mid, ma, mb, w - 2, inner
            a = [a[(i * 2 + k) * step + at] for k in range(2)]
            b = [b[(i * 2 + k) * step + at] for k in range(2)]
            below = [t_low(x, y) for x, y in zip(a, b)]
            above = [t_high(x, y) for x, y in zip(a, b)]
            ext[i, 0, w] = below[0]
            ext[i, 1, w] = own[i, 0, at] + below[1]
            for t in range(1, layers):
                ext[i, t + 1, w] = own[i, t, at]
            ext[i, layers + 1, w] = jnp.where(has_top, own[i, layers, at] + above[0], 0.0)
            ext[i, layers + 2, w] = above[1]

    def apply(i, t, w, diagonal):
        here = ext[i, t + 1, w + 1]
        beside = ext[i, t, w + 1] + ext[i, t + 2, w + 1]
        beside = beside + (ext[i, t + 1, w] + ext[i, t + 1, w + 2])
        beside = beside + (before(here, masks) + after(here, masks))
        return here, diagonal * here - beside

    count = 2 * (layers + 1)
    for t in range(layers):
        d = 6.0 + w_high(wa[3 * count + t], wb[3 * count + t])
        for i in range(3):
            _, g = apply(i, t, columns, d)
            img[i, t, columns] = jnp.where(has_right, g, 0.0)
    for w in range(columns):
        d = 6.0 + t_high(ma[6 * inner + w], mb[6 * inner + w])
        for i in range(3):
            _, g = apply(i, layers, w, d)
            img[i, layers, w] = jnp.where(has_top, g, 0.0)
    for t in range(layers):
        for w in range(columns):
            d = 6.0 + row_of(stiff, (t,), w, columns, sub)
            for i in range(3):
                f, g = apply(i, t, w, d)
                img[i, t, w] = g
                image[i, t, w] = g
                force[i, t, w] = f
    m0 = m1 = m2 = m3 = me = zero
    for t in range(layers):
        for w in range(columns):
            d = 6.0 + row_of(stiff, (t,), w, columns, sub)
            square = zero
            for i in range(3):
                f, g = ext[i, t + 1, w + 1], img[i, t, w]
                m0, m1 = m0 + f * f, m1 + f * g
                square = square + g * g
                me = me + g * (img[i, t + 1, w] + img[i, t, w + 1] + after(g, masks))
            m2, m3 = m2 + square, m3 + d * square
    m3 = m3 - 2.0 * me
    lane = lax.broadcasted_iota(jnp.int32, (1, LANES), 1)
    line = jnp.zeros((1, LANES), jnp.float32)
    for k, m in enumerate((m0, m1, m2, m3)):
        line = jnp.where(lane == k, jnp.sum(m, keepdims=True), line)
    sums[...] = jnp.broadcast_to(line[None], sums.shape)


def finish_kernel(dims, sums, force, image, out):
    layers, columns, sub = dims
    line = jnp.sum(sums[...], axis=0)
    lane = lax.broadcasted_iota(jnp.int32, (1, LANES), 1)
    m0, m1, m2, m3 = [
        jnp.sum(jnp.where(lane == k, line, 0.0), axis=1, keepdims=True) for k in range(4)
    ]
    a1 = m0 / m1
    left = a1 * a1 * m2 - m0
    grow = 1.0 + left / m0
    a2 = left / (grow * grow * m1 - 2.0 * grow * a1 * m2 + a1 * a1 * m3)
    c0 = jnp.broadcast_to(a1 + a2 * grow, (sub, LANES))
    c1 = jnp.broadcast_to(a1 * a2, (sub, LANES))
    for i in range(3):
        for t in range(layers):
            for w in range(columns):
                out[i, t, pl.ds(w, sub, stride=columns), :] = (
                    c0 * force[i, t, w] - c1 * image[i, t, w]
                )


def call(
    kernel, shapes, scratch=(), hbm=(), count=0, copies=0, aliases=None, cost=None, limit=VMEM_LIMIT
):
    anywhere, local = pl.BlockSpec(memory_space=pltpu.HBM), pl.BlockSpec(memory_space=pltpu.VMEM)
    extra = [pltpu.SemaphoreType.DMA((copies,))] if copies else []
    more = {}
    if cost is not None:
        more["cost_estimate"] = pl.CostEstimate(flops=0, transcendentals=0, bytes_accessed=cost)
    return pl.pallas_call(
        kernel,
        out_shape=[jax.ShapeDtypeStruct(s, jnp.float32) for s in shapes],
        in_specs=[anywhere if k in hbm else local for k in range(count)],
        scratch_shapes=[pltpu.VMEM(s, jnp.float32) for s in scratch] + extra,
        input_output_aliases=aliases or {},
        compiler_params=pltpu.CompilerParams(vmem_limit_bytes=limit),
        **more,
    )


def on_device(ends, deviation, velocity, stiffness):
    _, layers, columns, length = deviation.shape
    sub = length // LANES
    dims = (layers, columns, sub)
    rows = columns * sub
    tile = (sub, LANES)
    w_first, w_second, t_first, t_second = swap_pairs(*ends)
    dev, vel, stiff = as_tiles(deviation), as_tiles(velocity), as_tiles(stiffness)

    wa, wb, ta, tb = call(
        functools.partial(pack_kernel, dims, ends),
        [(9, layers, *tile)] * 2 + [(9, rows, LANES)] * 2,
        [(6, layers, rows, LANES), (3, layers, rows, LANES)],
        hbm=(0, 1), count=2, copies=9, limit=PACK_LIMIT,
    )(dev, vel)
    packed = wa
    tb = swap(tb, t_second)
    wb = swap(wb, w_second)
    wa = swap(wa, w_first)
    ta = swap(ta, t_first)

    ext, tau = call(
        functools.partial(inner_kernel, dims),
        [(9, layers + 2, columns + 2, *tile), (6, layers, columns, *tile)],
        hbm=(2,), count=3, cost=12 * 1024 * 1024,
    )(dev, vel, packed)

    face = 6 * (layers + 1) + layers
    tau, part, sa, sb = call(
        functools.partial(outer_kernel, dims, ends),
        [(6, layers, columns, *tile), (3, layers + 1, 4, *tile)] + [(face, *tile)] * 2,
        count=7, aliases={0: 0},
    )(tau, ext, wa, wb, ta, tb, stiff)
    wb = swap(sb, w_second)
    wa = swap(sa, w_first)

    broad = 6 * (columns - 1) + columns
    mid, sa, sb = call(
        functools.partial(middle_kernel, dims, ends),
        [(3, layers + 1, columns - 1, *tile)] + [(broad, *tile)] * 2,
        count=3, cost=2 * 1024 * 1024,
    )(tau, part, stiff)
    mb = swap(sb, t_second)
    ma = swap(sa, t_first)

    side, sa, sb = call(
        functools.partial(join_kernel, dims, ends),
        [(3, layers + 1, 4, *tile)] + [(24, *tile)] * 2,
        count=3,
    )(part, wa, wb)
    jb = swap(sb, t_second)
    ja = swap(sa, t_first)

    (new,) = call(
        functools.partial(emit_kernel, dims), [(6, layers, rows, LANES)],
        hbm=(1,), count=2, cost=6 * 1024 * 1024,
    )(tau, side)

    force, image, sums = call(
        functools.partial(krylov_kernel, dims, ends),
        [(3, layers, columns, *tile)] * 2 + [(ends[0] * ends[1], 1, LANES)],
        [(3, layers + 3, columns + 3, *tile), (3, layers + 1, columns + 1, *tile)],
        count=9,
    )(mid, side, ma, mb, ja, jb, wa, wb, stiff)
    sums = lax.all_to_all(sums, AXES, 0, 0, tiled=True)

    (out,) = call(
        functools.partial(finish_kernel, dims), [(3, layers, rows, LANES)], count=3
    )(sums, force, image)
    return from_tiles(new, columns), from_tiles(out, columns)


def solution(mesh):
    placed = (
        P(None, "thick", "width", None),
        P(None, "thick", "width", None),
        P("thick", "width", None),
    )
    ends = (mesh.shape["width"], mesh.shape["thick"])
    return jax.shard_map(
        functools.partial(on_device, ends),
        mesh=mesh,
        in_specs=placed,
        out_specs=(P(None, "thick", "width", None), P(None, "thick", "width", None)),
        check_vma=False,
    )
```

time: 48.1 us -> 42.6 us (0.89)
  blocking collectives: 12.2 us -> 0 us
  starting transfers between devices: 10.5 us -> 15.2 us
  Pallas kernels: 6.02 us -> 7.56 us
  waiting for transfers between devices: 15.4 us -> 16.8 us
  local copies, waits for them, and re-layouts: 3.04 us -> 2.13 us
    all_to_all x1 -> x0, blocking collectives: 12.2 us -> none  [on_device(): sums = lax.all_to_all(sums, AXES, 0, 0, tiled=True)]
    all_to_all x0 -> x1, waiting for transfers between devices: none -> 6.06 us  [on_device(): sums = lax.all_to_all(sums, AXES, 0, 0, tiled=True)]
    all_to_all x0 -> x1, starting transfers between devices: none -> 5 us  [on_device(): sums = lax.all_to_all(sums, AXES, 0, 0, tiled=True)]
    ppermute x8 -> x10, waiting for transfers between devices: 15.4 us -> 10.7 us  [swap(): return lax.ppermute(value, AXES, pairs)]
    pallas_call x4 -> x7, Pallas kernels: 5.32 us -> 6.28 us  [the longest x1 2.12 us: on_device(): call(functools.partial(inner_kernel, dims), [(9, layers + 2, columns + 2,...]
    unnamed x8 -> x6, local copies, waits for them, and re-layouts: 3.03 us -> 2.13 us
    pallas_call x1, Pallas kernels: 0.7 us -> 1.28 us  [on_device(): call(functools.partial(krylov_kernel, dims, ends), [(3, layers, columns,...]
    ppermute x8 -> x10, starting transfers between devices: 10.5 us -> 10.2 us  [swap(): return lax.ppermute(value, AXES, pairs)]
  transfers between devices with their start and end apart: 8 -> 11, of which waited for: 4 -> 5; matrix products, arithmetic and copies ran while one was open for 0% -> 0% of each run, Pallas kernels for 0% -> 8%
where the time goes in v2:
time: 42.6 us; the launch traced here: 42.4 us
  waiting for transfers between devices  16.8 us (39%)
  starting transfers between devices  15.2 us (36%)
  Pallas kernels  7.56 us (18%)
  local copies, waits for them, and re-layouts  2.13 us (5%)
  between operations  0.71 us (2%)
    ppermute x10, waiting for transfers between devices, swap(): return lax.ppermute(value, AXES, pairs)  10.7 us
    ppermute x10, starting transfers between devices, swap(): return lax.ppermute(value, AXES, pairs)  10.2 us
    all_to_all x1, waiting for transfers between devices, on_device(): sums = lax.all_to_all(sums, AXES, 0, 0, tiled=True)  6.06 us
    all_to_all x1, starting transfers between devices, on_device(): sums = lax.all_to_all(sums, AXES, 0, 0, tiled=True)  5 us
    unnamed x6, local copies, waits for them, and re-layouts  2.13 us
    pallas_call x1, Pallas kernels, on_device(): call(functools.partial(inner_kernel, dims), [(9, layers + 2, columns + 2,...  2.12 us
    pallas_call x1, Pallas kernels, on_device(): call(functools.partial(pack_kernel, dims, ends), [(9, layers, *tile)] * 2...  1.52 us
    pallas_call x1, Pallas kernels, on_device(): call(functools.partial(krylov_kernel, dims, ends), [(3, layers, columns,...  1.28 us
  transfers between devices with their start and end apart: 11, of which 5 were waited for; matrix products, arithmetic and copies ran while one was open for 0% of the time, Pallas kernels for 8%

profile of v2, /device:TPU:0, one launch (start us, length us, event | category | flops | bytes accessed | tf_op | source)
XLA Modules:
  0.0 42.4 jit_solution(11058170703996323148)
XLA Ops:
  0.6 0.0 copy-start.2
  0.6 1.5 %shard_map.50 = (f32[9,4,8,128]{3,2,1,0:T(8,128)S(1)}, f32[9,4,8,128]{3,2,1,0:T(8,128)S(1)}, f32[9,64,128]{2,1,0:T(8,128)S(1)}, f32[9,64,128]{2,1,0:T(8,128)S(1)}) custom-call(f32[6,4,64,128]{3,2,1,0:T(8,128)} %bitcast.25, f32[3,4,64,128]{3,2,1,0:T(8,128)} %bitcast.27), custom_call_target="tpu_custom_call" | custom-call | tf_op jit(solution)/shard_map/pallas_call | solution.py:448
  2.2 0.5 %collective-permute-start.2 = (f32[9,64,128]{2,1,0:T(8,128)S(1)}, f32[9,64,128]{2,1,0:T(8,128)S(1)}, u32[]{:S(2)}, u32[]{:S(2)}) collective-permute-start(f32[9,64,128]{2,1,0:T(8,128)S(1)} %get-tuple-element.25), channel_id=1, source_target_pairs={{0,1},{1,0},{2,3},{3,2},{4,5},{5,4},{6,7},{7,6},{8,9},{9,8},{10,11... | collective-permute-start | bytes 884744 | tf_op jit(solution)/shard_map/ppermute | solution.py:45
  2.7 2.6 %collective-permute-start.3 = (f32[9,64,128]{2,1,0:T(8,128)S(1)}, f32[9,64,128]{2,1,0:T(8,128)S(1)}, u32[]{:S(2)}, u32[]{:S(2)}) collective-permute-start(f32[9,64,128]{2,1,0:T(8,128)S(1)} %get-tuple-element.26), channel_id=1, source_target_pairs={{0,3},{1,2},{2,1},{3,0},{4,7},{5,6},{6,5},{7,4},{8,11},{9,10},{10,... | collective-permute-start | bytes 884744 | tf_op jit(solution)/shard_map/ppermute | solution.py:45
  5.3 0.1 collective-permute-start.1
  5.4 3.0 %collective-permute-start = (f32[9,4,8,128]{3,2,1,0:T(8,128)S(1)}, f32[9,4,8,128]{3,2,1,0:T(8,128)S(1)}, u32[]{:S(2)}, u32[]{:S(2)}) collective-permute-start(f32[9,4,8,128]{3,2,1,0:T(8,128)S(1)} %get-tuple-element.21.after_pack), channel_id=1, source_target_pairs={{0,4},{1,5},{2,6},{3,7},{4,0},{5,1},{6,2},{7,3},{8,12},{9,13},{10,... | collective-permute-start | bytes 442376 | tf_op jit(solution)/shard_map/ppermute | solution.py:45
  8.4 1.1 %copy-done = f32[6,4,8,1024]{3,2,1,0:T(8,128)S(1)} copy-done((f32[6,4,8,1024]{3,2,1,0:T(8,128)S(1)}, f32[6,4,8,1024]{3,2,1,0:T(8,128)}, u32[]{:S(2)}) %copy-start) | copy-done | bytes 786456
  9.5 1.0 %copy-done.1 = f32[3,4,8,1024]{3,2,1,0:T(8,128)S(1)} copy-done((f32[3,4,8,1024]{3,2,1,0:T(8,128)S(1)}, f32[3,4,8,1024]{3,2,1,0:T(8,128)}, u32[]{:S(2)}) %copy-start.1) | copy-done | bytes 393240
  10.5 2.1 %shard_map.51 = (f32[9,6,10,8,128]{4,3,2,1,0:T(8,128)S(1)}, f32[6,4,8,8,128]{4,3,2,1,0:T(8,128)S(1)}) custom-call(f32[6,4,64,128]{3,2,1,0:T(8,128)S(1)} %bitcast.26, f32[3,4,64,128]{3,2,1,0:T(8,128)S(1)} %bitcast.28, f32[9,4,8,128]{3,2,1,0:T(8,128)S(1)} %get-tuple-element.21.after_pack), custom_call_target="tpu_custom_call" | custom-call | bytes 12582912 | tf_op jit(solution)/shard_map/pallas_call | solution.py:460
  12.6 0.0 collective-permute-done.1.wb
  12.6 1.6 %collective-permute-done.wa = f32[9,4,8,128]{3,2,1,0:T(8,128)S(1)} collective-permute-done((f32[9,4,8,128]{3,2,1,0:T(8,128)S(1)}, f32[9,4,8,128]{3,2,1,0:T(8,128)S(1)}, u32[]{:S(2)}, u32[]{:S(2)}) %collective-permute-start) | collective-permute-done | bytes 147488 | tf_op jit(solution)/shard_map/ppermute | solution.py:45
  14.2 0.0 collective-permute-done.2.ta
  14.2 0.0 collective-permute-done.3.tb
  14.2 0.4 %shard_map.52 = (f32[6,4,8,8,128]{4,3,2,1,0:T(8,128)S(1)}, f32[3,5,4,8,128]{4,3,2,1,0:T(8,128)S(1)}, f32[34,8,128]{2,1,0:T(8,128)S(1)}, f32[34,8,128]{2,1,0:T(8,128)S(1)}) custom-call(f32[6,4,8,8,128]{4,3,2,1,0:T(8,128)S(1)} %get-tuple-element.22.tau_in, f32[9,6,10,8,128]{4,3,2,1,0:T(8,128)S(1)} %get-tuple-element.23.ext, ...), custom_call_target="tpu_custom_call", output_to_operand_aliasing={{0}: (0, {})} | custom-call | tf_op jit(solution)/shard_map/pallas_call | solution.py:467
  14.7 2.5 %collective-permute-start.4 = (f32[34,8,128]{2,1,0:T(8,128)S(1)}, f32[34,8,128]{2,1,0:T(8,128)S(1)}, u32[]{:S(2)}, u32[]{:S(2)}) collective-permute-start(f32[34,8,128]{2,1,0:T(8,128)S(1)} %get-tuple-element.29), channel_id=1, source_target_pairs={{0,4},{1,5},{2,6},{3,7},{4,0},{5,1},{6,2},{7,3},{8,12},{9,13},{10,... | collective-permute-start | bytes 417800 | tf_op jit(solution)/shard_map/ppermute | solution.py:45
  17.2 0.0 collective-permute-start.5
  17.2 0.2 shard_map.55
  17.4 0.6 %collective-permute-start.6 = (f32[50,8,128]{2,1,0:T(8,128)S(1)}, f32[50,8,128]{2,1,0:T(8,128)S(1)}, u32[]{:S(2)}, u32[]{:S(2)}) collective-permute-start(f32[50,8,128]{2,1,0:T(8,128)S(1)} %get-tuple-element.33), channel_id=1, source_target_pairs={{0,1},{1,0},{2,3},{3,2},{4,5},{5,4},{6,7},{7,6},{8,9},{9,8},{10,11... | collective-permute-start | bytes 614408 | tf_op jit(solution)/shard_map/ppermute | solution.py:45
  18.0 0.2 collective-permute-start.7
  18.2 5.1 %collective-permute-done.4.wa = f32[34,8,128]{2,1,0:T(8,128)S(1)} collective-permute-done((f32[34,8,128]{2,1,0:T(8,128)S(1)}, f32[34,8,128]{2,1,0:T(8,128)S(1)}, u32[]{:S(2)}, u32[]{:S(2)}) %collective-permute-start.4) | collective-permute-done | bytes 139296 | tf_op jit(solution)/shard_map/ppermute | solution.py:45
  23.3 0.0 collective-permute-done.5.wb
  23.4 0.1 collective-permute-start.8
  23.5 0.6 %collective-permute-start.9 = (f32[24,8,128]{2,1,0:T(8,128)S(1)}, f32[24,8,128]{2,1,0:T(8,128)S(1)}, u32[]{:S(2)}, u32[]{:S(2)}) collective-permute-start(f32[24,8,128]{2,1,0:T(8,128)S(1)} %get-tuple-element.36), channel_id=1, source_target_pairs={{0,3},{1,2},{2,1},{3,0},{4,7},{5,6},{6,5},{7,4},{8,11},{9,10},{10,... | collective-permute-start | bytes 294920 | tf_op jit(solution)/shard_map/ppermute | solution.py:45
  24.1 0.0 collective-permute-done.6.ma
  24.1 1.0 %collective-permute-done.7.mb = f32[50,8,128]{2,1,0:T(8,128)S(1)} collective-permute-done((f32[50,8,128]{2,1,0:T(8,128)S(1)}, f32[50,8,128]{2,1,0:T(8,128)S(1)}, u32[]{:S(2)}, u32[]{:S(2)}) %collective-permute-start.7) | collective-permute-done | bytes 204832 | tf_op jit(solution)/shard_map/ppermute | solution.py:45
  25.1 0.0 collective-permute-done.8.ja
  25.1 2.9 %collective-permute-done.9.jb = f32[24,8,128]{2,1,0:T(8,128)S(1)} collective-permute-done((f32[24,8,128]{2,1,0:T(8,128)S(1)}, f32[24,8,128]{2,1,0:T(8,128)S(1)}, u32[]{:S(2)}, u32[]{:S(2)}) %collective-permute-start.9) | collective-permute-done | bytes 98336 | tf_op jit(solution)/shard_map/ppermute | solution.py:45
  28.0 1.3 %shard_map.56 = (f32[3,4,8,8,128]{4,3,2,1,0:T(8,128)S(1)}, f32[3,4,8,8,128]{4,3,2,1,0:T(8,128)S(1)}, f32[32,1,128]{2,1,0:T(1,128)}) custom-call(f32[3,5,7,8,128]{4,3,2,1,0:T(8,128)S(1)} %get-tuple-element.32.mid, f32[3,5,4,8,128]{4,3,2,1,0:T(8,128)S(1)} %get-tuple-element.31.after_join.side, f32[50,8,128]{2,1,0:T(8,128)S(1)} %collective-permute-done.6.ma, ...), custom_call_target="tpu_custom_call" | custom-call | tf_op jit(solution)/shard_map/pallas_call | solution.py:497
  29.3 5.0 %all-to-all-start = ((f32[32,1,128]{2,1,0:T(1,128)}), f32[32,1,128]{2,1,0:T(1,128)S(1)}, u32[]{:S(2)}, u32[]{:S(2)}) async-start(f32[32,1,128]{2,1,0:T(1,128)} %get-tuple-element.37), calls=%async_computation | async-start | bytes 32768 | tf_op jit(solution)/shard_map/all_to_all | solution.py:503
  34.3 1.0 %shard_map.54 = f32[6,4,64,128]{3,2,1,0:T(8,128)} custom-call(f32[6,4,8,8,128]{4,3,2,1,0:T(8,128)S(1)} %get-tuple-element.27.tau, f32[3,5,4,8,128]{4,3,2,1,0:T(8,128)S(1)} %get-tuple-element.31.after_join.side), custom_call_target="tpu_custom_call" | custom-call | bytes 6291456 | tf_op jit(solution)/shard_map/pallas_call | solution.py:492
  35.3 6.1 %all-to-all-done.sums = f32[32,1,128]{2,1,0:T(1,128)S(1)} async-done(((f32[32,1,128]{2,1,0:T(1,128)}), f32[32,1,128]{2,1,0:T(1,128)S(1)}, u32[]{:S(2)}, u32[]{:S(2)}) %all-to-all-start) | async-done | bytes 16416 | tf_op jit(solution)/shard_map/all_to_all | solution.py:503
  41.4 0.9 %shard_map.57 = f32[3,4,64,128]{3,2,1,0:T(8,128)} custom-call(f32[32,1,128]{2,1,0:T(1,128)S(1)} %all-to-all-done.sums, f32[3,4,8,8,128]{4,3,2,1,0:T(8,128)S(1)} %get-tuple-element.38.force, f32[3,4,8,8,128]{4,3,2,1,0:T(8,128)S(1)} %get-tuple-element.39.image), custom_call_target="tpu_custom_call" | custom-call | tf_op jit(solution)/shard_map/pallas_call | solution.py:505
  (4 shorter events, 0.1 us)
Async XLA Ops:
  0.6 13.6 %copy-start.2 = (f32[4,8,1024]{2,1,0:T(8,128)S(1)}, f32[4,8,1024]{2,1,0:T(8,128)}, u32[]{:S(2)}) copy-start(f32[4,8,1024]{2,1,0:T(8,128)} %param.5) | copy-start | bytes 393220
  2.2 12.1 %collective-permute-start.2 = (f32[9,64,128]{2,1,0:T(8,128)S(1)}, f32[9,64,128]{2,1,0:T(8,128)S(1)}, u32[]{:S(2)}, u32[]{:S(2)}) collective-permute-start(f32[9,64,128]{2,1,0:T(8,128)S(1)} %get-tuple-element.25), channel_id=1, source_target_pairs={{0,1},{1,0},{2,3},{3,2},{4,5},{5,4},{6,7},{7,6},{8,9},{9,8},{10,11... | collective-permute-start | bytes 884744 | tf_op jit(solution)/shard_map/ppermute | solution.py:45
  2.7 11.5 %collective-permute-start.3 = (f32[9,64,128]{2,1,0:T(8,128)S(1)}, f32[9,64,128]{2,1,0:T(8,128)S(1)}, u32[]{:S(2)}, u32[]{:S(2)}) collective-permute-start(f32[9,64,128]{2,1,0:T(8,128)S(1)} %get-tuple-element.26), channel_id=1, source_target_pairs={{0,3},{1,2},{2,1},{3,0},{4,7},{5,6},{6,5},{7,4},{8,11},{9,10},{10,... | collective-permute-start | bytes 884744 | tf_op jit(solution)/shard_map/ppermute | solution.py:45
  5.3 7.3 %collective-permute-start.1 = (f32[9,4,8,128]{3,2,1,0:T(8,128)S(1)}, f32[9,4,8,128]{3,2,1,0:T(8,128)S(1)}, u32[]{:S(2)}, u32[]{:S(2)}) collective-permute-start(f32[9,4,8,128]{3,2,1,0:T(8,128)S(1)} %get-tuple-element.24), channel_id=1, source_target_pairs={{0,1},{1,0},{2,3},{3,2},{4,8},{5,9},{6,10},{7,11},{8,4},{9,5},{10,... | collective-permute-start | bytes 442376 | tf_op jit(solution)/shard_map/ppermute | solution.py:45
  5.4 8.8 %collective-permute-start = (f32[9,4,8,128]{3,2,1,0:T(8,128)S(1)}, f32[9,4,8,128]{3,2,1,0:T(8,128)S(1)}, u32[]{:S(2)}, u32[]{:S(2)}) collective-permute-start(f32[9,4,8,128]{3,2,1,0:T(8,128)S(1)} %get-tuple-element.21.after_pack), channel_id=1, source_target_pairs={{0,4},{1,5},{2,6},{3,7},{4,0},{5,1},{6,2},{7,3},{8,12},{9,13},{10,... | collective-permute-start | bytes 442376 | tf_op jit(solution)/shard_map/ppermute | solution.py:45
  8.4 1.1 %copy-start = (f32[6,4,8,1024]{3,2,1,0:T(8,128)S(1)}, f32[6,4,8,1024]{3,2,1,0:T(8,128)}, u32[]{:S(2)}) copy-start(f32[6,4,8,1024]{3,2,1,0:T(8,128)} %param.3) | copy-start | bytes 2359300
  9.5 1.0 %copy-start.1 = (f32[3,4,8,1024]{3,2,1,0:T(8,128)S(1)}, f32[3,4,8,1024]{3,2,1,0:T(8,128)}, u32[]{:S(2)}) copy-start(f32[3,4,8,1024]{3,2,1,0:T(8,128)} %param.4) | copy-start | bytes 1179652
  14.7 8.6 %collective-permute-start.4 = (f32[34,8,128]{2,1,0:T(8,128)S(1)}, f32[34,8,128]{2,1,0:T(8,128)S(1)}, u32[]{:S(2)}, u32[]{:S(2)}) collective-permute-start(f32[34,8,128]{2,1,0:T(8,128)S(1)} %get-tuple-element.29), channel_id=1, source_target_pairs={{0,4},{1,5},{2,6},{3,7},{4,0},{5,1},{6,2},{7,3},{8,12},{9,13},{10,... | collective-permute-start | bytes 417800 | tf_op jit(solution)/shard_map/ppermute | solution.py:45
  17.2 6.1 %collective-permute-start.5 = (f32[34,8,128]{2,1,0:T(8,128)S(1)}, f32[34,8,128]{2,1,0:T(8,128)S(1)}, u32[]{:S(2)}, u32[]{:S(2)}) collective-permute-start(f32[34,8,128]{2,1,0:T(8,128)S(1)} %get-tuple-element.30), channel_id=1, source_target_pairs={{0,1},{1,0},{2,3},{3,2},{4,8},{5,9},{6,10},{7,11},{8,4},{9,5},{10,... | collective-permute-start | bytes 417800 | tf_op jit(solution)/shard_map/ppermute | solution.py:45
  17.4 6.7 %collective-permute-start.6 = (f32[50,8,128]{2,1,0:T(8,128)S(1)}, f32[50,8,128]{2,1,0:T(8,128)S(1)}, u32[]{:S(2)}, u32[]{:S(2)}) collective-permute-start(f32[50,8,128]{2,1,0:T(8,128)S(1)} %get-tuple-element.33), channel_id=1, source_target_pairs={{0,1},{1,0},{2,3},{3,2},{4,5},{5,4},{6,7},{7,6},{8,9},{9,8},{10,11... | collective-permute-start | bytes 614408 | tf_op jit(solution)/shard_map/ppermute | solution.py:45
  18.0 7.1 %collective-permute-start.7 = (f32[50,8,128]{2,1,0:T(8,128)S(1)}, f32[50,8,128]{2,1,0:T(8,128)S(1)}, u32[]{:S(2)}, u32[]{:S(2)}) collective-permute-start(f32[50,8,128]{2,1,0:T(8,128)S(1)} %get-tuple-element.34), channel_id=1, source_target_pairs={{0,3},{1,2},{2,1},{3,0},{4,7},{5,6},{6,5},{7,4},{8,11},{9,10},{10,... | collective-permute-start | bytes 614408 | tf_op jit(solution)/shard_map/ppermute | solution.py:45
  23.4 1.7 %collective-permute-start.8 = (f32[24,8,128]{2,1,0:T(8,128)S(1)}, f32[24,8,128]{2,1,0:T(8,128)S(1)}, u32[]{:S(2)}, u32[]{:S(2)}) collective-permute-start(f32[24,8,128]{2,1,0:T(8,128)S(1)} %get-tuple-element.35), channel_id=1, source_target_pairs={{0,1},{1,0},{2,3},{3,2},{4,5},{5,4},{6,7},{7,6},{8,9},{9,8},{10,11... | collective-permute-start | bytes 294920 | tf_op jit(solution)/shard_map/ppermute | solution.py:45
  23.5 4.6 %collective-permute-start.9 = (f32[24,8,128]{2,1,0:T(8,128)S(1)}, f32[24,8,128]{2,1,0:T(8,128)S(1)}, u32[]{:S(2)}, u32[]{:S(2)}) collective-permute-start(f32[24,8,128]{2,1,0:T(8,128)S(1)} %get-tuple-element.36), channel_id=1, source_target_pairs={{0,3},{1,2},{2,1},{3,0},{4,7},{5,6},{6,5},{7,4},{8,11},{9,10},{10,... | collective-permute-start | bytes 294920 | tf_op jit(solution)/shard_map/ppermute | solution.py:45
  29.3 12.1 %all-to-all-start = ((f32[32,1,128]{2,1,0:T(1,128)}), f32[32,1,128]{2,1,0:T(1,128)S(1)}, u32[]{:S(2)}, u32[]{:S(2)}) async-start(f32[32,1,128]{2,1,0:T(1,128)} %get-tuple-element.37), calls=%async_computation | async-start | bytes 32768 | tf_op jit(solution)/shard_map/all_to_all | solution.py:503

commit v3 on v2

--- a/solution.py
+++ b/solution.py
@@ -128,7 +128,7 @@
 HALF = 0.5 * TIME_STEP
 
 
-def inner_kernel(dims, dev, vel, after_pack, ext, tau):
+def inner_kernel(dims, dev, vel, after_pack, stiff, ext, tau):
     layers, columns, sub = dims
     masks = edge_masks(sub)
     zero = jnp.zeros((sub, LANES), jnp.float32)
@@ -222,35 +222,40 @@
             lower = [(y - x, z - x) for x, y, z in level]
 
 
-def outer_kernel(dims, ends, tau_in, ext, wa, wb, ta, tb, stiff, tau, part, sa, sb):
-    layers, columns, sub = dims
-    w_low, w_high, send_w, _ = halves("width", ends[0])
-    t_low, t_high, _, _ = halves("thick", ends[1])
-
-    def correct(t, w, d, sign, halo):
-        s = [ext[c, t + 1, w + 1] for c in range(6)]
-        u = ext[6 + d, t + 1, w + 1]
-        speed = jnp.maximum(u, 0.0) if sign < 0 else -jnp.minimum(u, 0.0)
-        speed = TIME_STEP * speed
-        h = [(sign * HALF) * halo[6 + i] for i in range(3)]
-        q = [s[SLOT[d][j]] for j in range(3)]
-        q[d] = q[d] + 1.0
-        for p, (i, j) in enumerate(PAIRS):
-            bent = 2.0 * (h[i] * q[i]) if i == j else h[i] * q[j] + h[j] * q[i]
-            tau[p, t, w] = tau[p, t, w] + (speed * halo[p] + bent)
+def correct(tau, ext, t, w, d, sign, halo):
+    s = [ext[c, t + 1, w + 1] for c in range(6)]
+    u = ext[6 + d, t + 1, w + 1]
+    speed = TIME_STEP * (jnp.maximum(u, 0.0) if sign < 0 else -jnp.minimum(u, 0.0))
+    h = [(sign * HALF) * halo[6 + i] for i in range(3)]
+    q = [s[SLOT[d][j]] for j in range(3)]
+    q[d] = q[d] + 1.0
+    for p, (i, j) in enumerate(PAIRS):
+        bent = 2.0 * (h[i] * q[i]) if i == j else h[i] * q[j] + h[j] * q[i]
+        tau[p, t, w] = tau[p, t, w] + (speed * halo[p] + bent)
+
+
+def side_kernel(dims, ends, tau_in, ext, wa, wb, tau):
+    layers, columns, sub = dims
+    w_low, w_high, _, _ = halves("width", ends[0])
 
     def side(t, carry):
         a, b = [wa[c, t] for c in range(9)], [wb[c, t] for c in range(9)]
-        correct(t, 0, 1, -1.0, [w_low(x, y) for x, y in zip(a, b)])
-        correct(t, columns - 1, 1, 1.0, [w_high(x, y) for x, y in zip(a, b)])
+        correct(tau, ext, t, 0, 1, -1.0, [w_low(x, y) for x, y in zip(a, b)])
+        correct(tau, ext, t, columns - 1, 1, 1.0, [w_high(x, y) for x, y in zip(a, b)])
         return carry
 
     lax.fori_loop(0, layers, side, 0)
+
+
+def outer_kernel(dims, ends, tau_in, ext, ta, tb, stiff, tau, part, sa, sb):
+    layers, columns, sub = dims
+    send_w = halves("width", ends[0])[2]
+    t_low, t_high, _, _ = halves("thick", ends[1])
     for w in range(columns):
         a = [row_of(ta, (c,), w, columns, sub) for c in range(9)]
         b = [row_of(tb, (c,), w, columns, sub) for c in range(9)]
-        correct(0, w, 0, -1.0, [t_low(x, y) for x, y in zip(a, b)])
-        correct(layers - 1, w, 0, 1.0, [t_high(x, y) for x, y in zip(a, b)])
+        correct(tau, ext, 0, w, 0, -1.0, [t_low(x, y) for x, y in zip(a, b)])
+        correct(tau, ext, layers - 1, w, 0, 1.0, [t_high(x, y) for x, y in zip(a, b)])
 
     slot = {0: 0, 1: 1, columns - 1: 2, columns: 3}
 
@@ -294,15 +299,16 @@
         sb[6 * inner + w] = row
 
 
-def emit_kernel(dims, tau, after_join, new):
-    layers, columns, sub = dims
+def emit_kernel(dims, tau, after_join, new, done):
+    layers, columns, sub = dims
+    done[...] = jnp.zeros_like(done)
     for c in range(6):
         for t in range(layers):
             for w in range(columns):
                 new[c, t, pl.ds(w, sub, stride=columns), :] = tau[c, t, w]
 
 
-def join_kernel(dims, ends, part, wa, wb, side, sa, sb):
+def join_kernel(dims, ends, part, wb, wa, side, sa, sb):
     layers, columns, sub = dims
     w_low, w_high, _, has_high = halves("width", ends[0])
     send_t = halves("thick", ends[1])[2]
@@ -324,7 +330,7 @@
 
 
 def krylov_kernel(
-    dims, ends, mid, side, ma, mb, ja, jb, wa, wb, stiff, force, image, sums, ext, img
+    dims, ends, mid, side, mb, ma, jb, ja, wa, wb, stiff, after_emit, force, image, sums, ext, img
 ):
     layers, columns, sub = dims
     w_high = halves("width", ends[0])[1]
@@ -418,13 +424,13 @@
 
 
 def call(
-    kernel, shapes, scratch=(), hbm=(), count=0, copies=0, aliases=None, cost=None, limit=VMEM_LIMIT
+    kernel, shapes, scratch=(), hbm=(), count=0, copies=0, aliases=None, cost=None, work=0, limit=VMEM_LIMIT
 ):
-    anywhere, local = pl.BlockSpec(memory_space=pltpu.HBM), pl.BlockSpec(memory_space=pltpu.VMEM)
+    anywhere, local = pl.BlockSpec(memory_space=pl.ANY), pl.BlockSpec(memory_space=pltpu.VMEM)
     extra = [pltpu.SemaphoreType.DMA((copies,))] if copies else []
     more = {}
     if cost is not None:
-        more["cost_estimate"] = pl.CostEstimate(flops=0, transcendentals=0, bytes_accessed=cost)
+        more["cost_estimate"] = pl.CostEstimate(flops=work, transcendentals=0, bytes_accessed=cost)
     return pl.pallas_call(
         kernel,
         out_shape=[jax.ShapeDtypeStruct(s, jnp.float32) for s in shapes],
@@ -460,15 +466,21 @@
     ext, tau = call(
         functools.partial(inner_kernel, dims),
         [(9, layers + 2, columns + 2, *tile), (6, layers, columns, *tile)],
-        hbm=(2,), count=3, cost=12 * 1024 * 1024,
-    )(dev, vel, packed)
+        hbm=(2,), count=4, cost=12 * 1024 * 1024,
+    )(dev, vel, packed, stiff)
+
+    (tau,) = call(
+        functools.partial(side_kernel, dims, ends),
+        [(6, layers, columns, *tile)],
+        count=4, aliases={0: 0}, cost=1024 * 1024, work=10**10,
+    )(tau, ext, wa, wb)
 
     face = 6 * (layers + 1) + layers
     tau, part, sa, sb = call(
         functools.partial(outer_kernel, dims, ends),
         [(6, layers, columns, *tile), (3, layers + 1, 4, *tile)] + [(face, *tile)] * 2,
-        count=7, aliases={0: 0},
-    )(tau, ext, wa, wb, ta, tb, stiff)
+        count=5, aliases={0: 0},
+    )(tau, ext, ta, tb, stiff)
     wb = swap(sb, w_second)
     wa = swap(sa, w_first)
 
@@ -485,12 +497,12 @@
         functools.partial(join_kernel, dims, ends),
         [(3, layers + 1, 4, *tile)] + [(24, *tile)] * 2,
         count=3,
-    )(part, wa, wb)
+    )(part, wb, wa)
     jb = swap(sb, t_second)
     ja = swap(sa, t_first)
 
-    (new,) = call(
-        functools.partial(emit_kernel, dims), [(6, layers, rows, LANES)],
+    new, done = call(
+        functools.partial(emit_kernel, dims), [(6, layers, rows, LANES), tile],
         hbm=(1,), count=2, cost=6 * 1024 * 1024,
     )(tau, side)
 
@@ -498,8 +510,8 @@
         functools.partial(krylov_kernel, dims, ends),
         [(3, layers, columns, *tile)] * 2 + [(ends[0] * ends[1], 1, LANES)],
         [(3, layers + 3, columns + 3, *tile), (3, layers + 1, columns + 1, *tile)],
-        count=9,
-    )(mid, side, ma, mb, ja, jb, wa, wb, stiff)
+        count=10,
+    )(mid, side, mb, ma, jb, ja, wa, wb, stiff, done)
     sums = lax.all_to_all(sums, AXES, 0, 0, tiled=True)
 
     (out,) = call(

time: 42.6 us -> 43.3 us (1.016)
  blocking collectives: 0 us -> 12.7 us
  waiting for transfers between devices: 16.8 us -> 6.88 us
  starting transfers between devices: 15.2 us -> 12.7 us
  local copies, waits for them, and re-layouts: 2.13 us -> 3.04 us
  Pallas kernels: 7.56 us -> 6.95 us
    all_to_all x0 -> x1, blocking collectives: none -> 12.7 us  [on_device(): sums = lax.all_to_all(sums, AXES, 0, 0, tiled=True)]
    all_to_all x1 -> x0, waiting for transfers between devices: 6.06 us -> none  [on_device(): sums = lax.all_to_all(sums, AXES, 0, 0, tiled=True)]
    all_to_all x1 -> x0, starting transfers between devices: 5 us -> none  [on_device(): sums = lax.all_to_all(sums, AXES, 0, 0, tiled=True)]
    ppermute x10, waiting for transfers between devices: 10.7 us -> 6.88 us  [swap(): return lax.ppermute(value, AXES, pairs)]
    ppermute x10, starting transfers between devices: 10.2 us -> 12.7 us  [swap(): return lax.ppermute(value, AXES, pairs)]
    unnamed x6 -> x8, local copies, waits for them, and re-layouts: 2.13 us -> 3.04 us
    pallas_call x1, Pallas kernels: 1.28 us -> 0.7 us  [on_device(): call(functools.partial(krylov_kernel, dims, ends), [(3, layers, columns,...]
    pallas_call x1 -> x2, Pallas kernels: 1.02 us -> 1.13 us  [the longest x1 1.01 us: on_device(): call(functools.partial(emit_kernel, dims), [(6, layers, rows, LANES), til...]
  transfers between devices with their start and end apart: 11 -> 10, of which waited for: 5 -> 3; matrix products, arithmetic and copies ran while one was open for 0% -> 0% of each run, Pallas kernels for 8% -> 8%
where the time goes in v3:
time: 43.3 us; the launch traced here: 43 us
  starting transfers between devices  12.7 us (29%)
  blocking collectives  12.7 us (29%)
  Pallas kernels  6.95 us (16%)
  waiting for transfers between devices  6.88 us (16%)
  local copies, waits for them, and re-layouts  3.04 us (7%)
  between operations  0.72 us (2%)
    all_to_all x1, blocking collectives, on_device(): sums = lax.all_to_all(sums, AXES, 0, 0, tiled=True)  12.7 us
    ppermute x10, starting transfers between devices, swap(): return lax.ppermute(value, AXES, pairs)  12.7 us
    ppermute x10, waiting for transfers between devices, swap(): return lax.ppermute(value, AXES, pairs)  6.88 us
    unnamed x8, local copies, waits for them, and re-layouts  3.04 us
    pallas_call x1, Pallas kernels, on_device(): call(functools.partial(inner_kernel, dims), [(9, layers + 2, columns + 2,...  2.12 us
    pallas_call x1, Pallas kernels, on_device(): call(functools.partial(pack_kernel, dims, ends), [(9, layers, *tile)] * 2...  1.5 us
    pallas_call x1, Pallas kernels, on_device(): call(functools.partial(emit_kernel, dims), [(6, layers, rows, LANES), til...  1.01 us
    pallas_call x1, Pallas kernels, on_device(): call(functools.partial(finish_kernel, dims), [(3, layers, rows, LANES)],...  0.95 us
  transfers between devices with their start and end apart: 10, of which 3 were waited for; matrix products, arithmetic and copies ran while one was open for 0% of the time, Pallas kernels for 8%

profile of v3, /device:TPU:0, one launch (start us, length us, event | category | flops | bytes accessed | tf_op | source)
XLA Modules:
  0.0 43.0 jit_solution(10976980682768360418)
XLA Ops:
  0.6 1.5 %shard_map.50 = (f32[9,4,8,128]{3,2,1,0:T(8,128)S(1)}, f32[9,4,8,128]{3,2,1,0:T(8,128)S(1)}, f32[9,64,128]{2,1,0:T(8,128)S(1)}, f32[9,64,128]{2,1,0:T(8,128)S(1)}) custom-call(f32[6,4,64,128]{3,2,1,0:T(8,128)} %bitcast.25, f32[3,4,64,128]{3,2,1,0:T(8,128)} %bitcast.31), custom_call_target="tpu_custom_call" | custom-call | tf_op jit(solution)/shard_map/pallas_call | solution.py:454
  2.1 0.5 %collective-permute-start.1 = (f32[9,4,8,128]{3,2,1,0:T(8,128)S(1)}, f32[9,4,8,128]{3,2,1,0:T(8,128)S(1)}, u32[]{:S(2)}, u32[]{:S(2)}) collective-permute-start(f32[9,4,8,128]{3,2,1,0:T(8,128)S(1)} %get-tuple-element.26), channel_id=1, source_target_pairs={{0,1},{1,0},{2,3},{3,2},{4,8},{5,9},{6,10},{7,11},{8,4},{9,5},{10,... | collective-permute-start | bytes 442376 | tf_op jit(solution)/shard_map/ppermute | solution.py:45
  2.7 4.0 %collective-permute-start = (f32[9,4,8,128]{3,2,1,0:T(8,128)S(1)}, f32[9,4,8,128]{3,2,1,0:T(8,128)S(1)}, u32[]{:S(2)}, u32[]{:S(2)}) collective-permute-start(f32[9,4,8,128]{3,2,1,0:T(8,128)S(1)} %get-tuple-element.23.after_pack), channel_id=1, source_target_pairs={{0,4},{1,5},{2,6},{3,7},{4,0},{5,1},{6,2},{7,3},{8,12},{9,13},{10,... | collective-permute-start | bytes 442376 | tf_op jit(solution)/shard_map/ppermute | solution.py:45
  6.7 0.0 collective-permute-start.2
  6.7 1.6 %collective-permute-start.3 = (f32[9,64,128]{2,1,0:T(8,128)S(1)}, f32[9,64,128]{2,1,0:T(8,128)S(1)}, u32[]{:S(2)}, u32[]{:S(2)}) collective-permute-start(f32[9,64,128]{2,1,0:T(8,128)S(1)} %get-tuple-element.28), channel_id=1, source_target_pairs={{0,3},{1,2},{2,1},{3,0},{4,7},{5,6},{6,5},{7,4},{8,11},{9,10},{10,... | collective-permute-start | bytes 884744 | tf_op jit(solution)/shard_map/ppermute | solution.py:45
  8.3 1.1 %copy-done = f32[6,4,8,1024]{3,2,1,0:T(8,128)S(1)} copy-done((f32[6,4,8,1024]{3,2,1,0:T(8,128)S(1)}, f32[6,4,8,1024]{3,2,1,0:T(8,128)}, u32[]{:S(2)}) %copy-start) | copy-done | bytes 786456
  9.5 0.9 %copy-done.1 = f32[4,8,1024]{2,1,0:T(8,128)S(1)} copy-done((f32[4,8,1024]{2,1,0:T(8,128)S(1)}, f32[4,8,1024]{2,1,0:T(8,128)}, u32[]{:S(2)}) %copy-start.1) | copy-done | bytes 131096
  10.4 1.0 %copy-done.3 = f32[3,4,8,1024]{3,2,1,0:T(8,128)S(1)} copy-done((f32[3,4,8,1024]{3,2,1,0:T(8,128)S(1)}, f32[3,4,8,1024]{3,2,1,0:T(8,128)}, u32[]{:S(2)}) %copy-start.3) | copy-done | bytes 393240
  11.4 2.1 %shard_map.51 = (f32[9,6,10,8,128]{4,3,2,1,0:T(8,128)S(1)}, f32[6,4,8,8,128]{4,3,2,1,0:T(8,128)S(1)}) custom-call(f32[6,4,64,128]{3,2,1,0:T(8,128)S(1)} %bitcast.26, f32[3,4,64,128]{3,2,1,0:T(8,128)S(1)} %bitcast.32, f32[9,4,8,128]{3,2,1,0:T(8,128)S(1)} %get-tuple-element.23.after_pack, f32[4,64,128]{2,1,0:T(8,128)S(1)} %bitcast.27), custom_call_target="tpu_custom_call" | custom-call | bytes 12582912 | tf_op jit(solution)/shard_map/pallas_call | solution.py:466
  13.5 0.0 collective-permute-done.wa
  13.5 0.1 shard_map.52.tau_in
  13.6 0.0 copy-start.2
  13.6 0.0 collective-permute-done.2.ta
  13.6 1.7 %collective-permute-done.3.tb = f32[9,64,128]{2,1,0:T(8,128)S(1)} collective-permute-done((f32[9,64,128]{2,1,0:T(8,128)S(1)}, f32[9,64,128]{2,1,0:T(8,128)S(1)}, u32[]{:S(2)}, u32[]{:S(2)}) %collective-permute-start.3) | collective-permute-done | bytes 294944 | tf_op jit(solution)/shard_map/ppermute | solution.py:45
  15.3 0.3 shard_map.53
  15.7 0.5 %collective-permute-start.4 = (f32[34,8,128]{2,1,0:T(8,128)S(1)}, f32[34,8,128]{2,1,0:T(8,128)S(1)}, u32[]{:S(2)}, u32[]{:S(2)}) collective-permute-start(f32[34,8,128]{2,1,0:T(8,128)S(1)} %get-tuple-element.31), channel_id=1, source_target_pairs={{0,1},{1,0},{2,3},{3,2},{4,8},{5,9},{6,10},{7,11},{8,4},{9,5},{10,... | collective-permute-start | bytes 417800 | tf_op jit(solution)/shard_map/ppermute | solution.py:45
  16.2 2.6 %collective-permute-start.5 = (f32[34,8,128]{2,1,0:T(8,128)S(1)}, f32[34,8,128]{2,1,0:T(8,128)S(1)}, u32[]{:S(2)}, u32[]{:S(2)}) collective-permute-start(f32[34,8,128]{2,1,0:T(8,128)S(1)} %get-tuple-element.32), channel_id=1, source_target_pairs={{0,4},{1,5},{2,6},{3,7},{4,0},{5,1},{6,2},{7,3},{8,12},{9,13},{10,... | collective-permute-start | bytes 417800 | tf_op jit(solution)/shard_map/ppermute | solution.py:45
  18.8 0.2 shard_map.56
  19.0 1.1 %collective-permute-start.6 = (f32[50,8,128]{2,1,0:T(8,128)S(1)}, f32[50,8,128]{2,1,0:T(8,128)S(1)}, u32[]{:S(2)}, u32[]{:S(2)}) collective-permute-start(f32[50,8,128]{2,1,0:T(8,128)S(1)} %get-tuple-element.36), channel_id=1, source_target_pairs={{0,3},{1,2},{2,1},{3,0},{4,7},{5,6},{6,5},{7,4},{8,11},{9,10},{10,... | collective-permute-start | bytes 614408 | tf_op jit(solution)/shard_map/ppermute | solution.py:45
  20.1 0.6 %collective-permute-start.7 = (f32[50,8,128]{2,1,0:T(8,128)S(1)}, f32[50,8,128]{2,1,0:T(8,128)S(1)}, u32[]{:S(2)}, u32[]{:S(2)}) collective-permute-start(f32[50,8,128]{2,1,0:T(8,128)S(1)} %get-tuple-element.37), channel_id=1, source_target_pairs={{0,1},{1,0},{2,3},{3,2},{4,5},{5,4},{6,7},{7,6},{8,9},{9,8},{10,11... | collective-permute-start | bytes 614408 | tf_op jit(solution)/shard_map/ppermute | solution.py:45
  20.7 0.0 collective-permute-done.4.wb
  20.7 2.9 %collective-permute-done.5.wa = f32[34,8,128]{2,1,0:T(8,128)S(1)} collective-permute-done((f32[34,8,128]{2,1,0:T(8,128)S(1)}, f32[34,8,128]{2,1,0:T(8,128)S(1)}, u32[]{:S(2)}, u32[]{:S(2)}) %collective-permute-start.5) | collective-permute-done | bytes 139296 | tf_op jit(solution)/shard_map/ppermute | solution.py:45
  23.6 0.1 shard_map.54
  23.7 1.2 %collective-permute-start.8 = (f32[24,8,128]{2,1,0:T(8,128)S(1)}, f32[24,8,128]{2,1,0:T(8,128)S(1)}, u32[]{:S(2)}, u32[]{:S(2)}) collective-permute-start(f32[24,8,128]{2,1,0:T(8,128)S(1)} %get-tuple-element.38), channel_id=1, source_target_pairs={{0,3},{1,2},{2,1},{3,0},{4,7},{5,6},{6,5},{7,4},{8,11},{9,10},{10,... | collective-permute-start | bytes 294920 | tf_op jit(solution)/shard_map/ppermute | solution.py:45
  24.9 0.5 %collective-permute-start.9 = (f32[24,8,128]{2,1,0:T(8,128)S(1)}, f32[24,8,128]{2,1,0:T(8,128)S(1)}, u32[]{:S(2)}, u32[]{:S(2)}) collective-permute-start(f32[24,8,128]{2,1,0:T(8,128)S(1)} %get-tuple-element.39), channel_id=1, source_target_pairs={{0,1},{1,0},{2,3},{3,2},{4,5},{5,4},{6,7},{7,6},{8,9},{9,8},{10,11... | collective-permute-start | bytes 294920 | tf_op jit(solution)/shard_map/ppermute | solution.py:45
  25.4 1.0 %shard_map.55 = (f32[6,4,64,128]{3,2,1,0:T(8,128)}, f32[8,128]{1,0:T(8,128)S(1)}) custom-call(f32[6,4,8,8,128]{4,3,2,1,0:T(8,128)S(1)} %get-tuple-element.29.tau, f32[3,5,4,8,128]{4,3,2,1,0:T(8,128)S(1)} %get-tuple-element.33.after_join.side), custom_call_target="tpu_custom_call" | custom-call | bytes 6291456 | tf_op jit(solution)/shard_map/pallas_call | solution.py:504
  26.4 0.0 collective-permute-done.6.mb
  26.4 0.0 collective-permute-done.7.ma
  26.4 2.2 %collective-permute-done.8.jb = f32[24,8,128]{2,1,0:T(8,128)S(1)} collective-permute-done((f32[24,8,128]{2,1,0:T(8,128)S(1)}, f32[24,8,128]{2,1,0:T(8,128)S(1)}, u32[]{:S(2)}, u32[]{:S(2)}) %collective-permute-start.8) | collective-permute-done | bytes 98336 | tf_op jit(solution)/shard_map/ppermute | solution.py:45
  28.6 0.7 %shard_map.57 = (f32[3,4,8,8,128]{4,3,2,1,0:T(8,128)S(1)}, f32[3,4,8,8,128]{4,3,2,1,0:T(8,128)S(1)}, f32[32,1,128]{2,1,0:T(1,128)S(1)}) custom-call(f32[3,5,7,8,128]{4,3,2,1,0:T(8,128)S(1)} %get-tuple-element.35.mid, f32[3,5,4,8,128]{4,3,2,1,0:T(8,128)S(1)} %get-tuple-element.33.after_join.side, f32[50,8,128]{2,1,0:T(8,128)S(1)} %collective-permute-done.6.mb, ...), custom_call_target="tpu_custom_call" | custom-call | tf_op jit(solution)/shard_map/pallas_call | solution.py:509
  29.3 12.7 %all_to_all.5.sums = f32[32,1,128]{2,1,0:T(1,128)S(1)} all-to-all(f32[32,1,128]{2,1,0:T(1,128)S(1)} %get-tuple-element.41), channel_id=1, replica_groups=mesh['width'=8,'thick'=4] {'width','thick'}, dimensions={0} | all-to-all | bytes 32768 | tf_op jit(solution)/shard_map/all_to_all | solution.py:515
  42.1 0.9 %shard_map.58 = f32[3,4,64,128]{3,2,1,0:T(8,128)} custom-call(f32[32,1,128]{2,1,0:T(1,128)S(1)} %all_to_all.5.sums, f32[3,4,8,8,128]{4,3,2,1,0:T(8,128)S(1)} %get-tuple-element.42.force, f32[3,4,8,8,128]{4,3,2,1,0:T(8,128)S(1)} %get-tuple-element.43.image), custom_call_target="tpu_custom_call" | custom-call | tf_op jit(solution)/shard_map/pallas_call | solution.py:517
  (6 shorter events, 0.0 us)
Async XLA Ops:
  2.1 11.3 %collective-permute-start.1 = (f32[9,4,8,128]{3,2,1,0:T(8,128)S(1)}, f32[9,4,8,128]{3,2,1,0:T(8,128)S(1)}, u32[]{:S(2)}, u32[]{:S(2)}) collective-permute-start(f32[9,4,8,128]{3,2,1,0:T(8,128)S(1)} %get-tuple-element.26), channel_id=1, source_target_pairs={{0,1},{1,0},{2,3},{3,2},{4,8},{5,9},{6,10},{7,11},{8,4},{9,5},{10,... | collective-permute-start | bytes 442376 | tf_op jit(solution)/shard_map/ppermute | solution.py:45
  2.7 10.8 %collective-permute-start = (f32[9,4,8,128]{3,2,1,0:T(8,128)S(1)}, f32[9,4,8,128]{3,2,1,0:T(8,128)S(1)}, u32[]{:S(2)}, u32[]{:S(2)}) collective-permute-start(f32[9,4,8,128]{3,2,1,0:T(8,128)S(1)} %get-tuple-element.23.after_pack), channel_id=1, source_target_pairs={{0,4},{1,5},{2,6},{3,7},{4,0},{5,1},{6,2},{7,3},{8,12},{9,13},{10,... | collective-permute-start | bytes 442376 | tf_op jit(solution)/shard_map/ppermute | solution.py:45
  6.7 6.9 %collective-permute-start.2 = (f32[9,64,128]{2,1,0:T(8,128)S(1)}, f32[9,64,128]{2,1,0:T(8,128)S(1)}, u32[]{:S(2)}, u32[]{:S(2)}) collective-permute-start(f32[9,64,128]{2,1,0:T(8,128)S(1)} %get-tuple-element.27), channel_id=1, source_target_pairs={{0,1},{1,0},{2,3},{3,2},{4,5},{5,4},{6,7},{7,6},{8,9},{9,8},{10,11... | collective-permute-start | bytes 884744 | tf_op jit(solution)/shard_map/ppermute | solution.py:45
  6.7 8.7 %collective-permute-start.3 = (f32[9,64,128]{2,1,0:T(8,128)S(1)}, f32[9,64,128]{2,1,0:T(8,128)S(1)}, u32[]{:S(2)}, u32[]{:S(2)}) collective-permute-start(f32[9,64,128]{2,1,0:T(8,128)S(1)} %get-tuple-element.28), channel_id=1, source_target_pairs={{0,3},{1,2},{2,1},{3,0},{4,7},{5,6},{6,5},{7,4},{8,11},{9,10},{10,... | collective-permute-start | bytes 884744 | tf_op jit(solution)/shard_map/ppermute | solution.py:45
  8.3 1.1 %copy-start = (f32[6,4,8,1024]{3,2,1,0:T(8,128)S(1)}, f32[6,4,8,1024]{3,2,1,0:T(8,128)}, u32[]{:S(2)}) copy-start(f32[6,4,8,1024]{3,2,1,0:T(8,128)} %param.3) | copy-start | bytes 2359300
  9.5 0.9 %copy-start.1 = (f32[4,8,1024]{2,1,0:T(8,128)S(1)}, f32[4,8,1024]{2,1,0:T(8,128)}, u32[]{:S(2)}) copy-start(f32[4,8,1024]{2,1,0:T(8,128)} %param.5) | copy-start | bytes 393220
  10.4 1.0 %copy-start.3 = (f32[3,4,8,1024]{3,2,1,0:T(8,128)S(1)}, f32[3,4,8,1024]{3,2,1,0:T(8,128)}, u32[]{:S(2)}) copy-start(f32[3,4,8,1024]{3,2,1,0:T(8,128)} %param.4) | copy-start | bytes 1179652
  13.6 5.2 %copy-start.2 = (f32[4,8,1024]{2,1,0:T(8,128)S(1)}, f32[4,8,1024]{2,1,0:T(8,128)}, u32[]{:S(2)}) copy-start(f32[4,8,1024]{2,1,0:T(8,128)} %param.5) | copy-start | bytes 393220
  15.7 5.0 %collective-permute-start.4 = (f32[34,8,128]{2,1,0:T(8,128)S(1)}, f32[34,8,128]{2,1,0:T(8,128)S(1)}, u32[]{:S(2)}, u32[]{:S(2)}) collective-permute-start(f32[34,8,128]{2,1,0:T(8,128)S(1)} %get-tuple-element.31), channel_id=1, source_target_pairs={{0,1},{1,0},{2,3},{3,2},{4,8},{5,9},{6,10},{7,11},{8,4},{9,5},{10,... | collective-permute-start | bytes 417800 | tf_op jit(solution)/shard_map/ppermute | solution.py:45
  16.2 7.4 %collective-permute-start.5 = (f32[34,8,128]{2,1,0:T(8,128)S(1)}, f32[34,8,128]{2,1,0:T(8,128)S(1)}, u32[]{:S(2)}, u32[]{:S(2)}) collective-permute-start(f32[34,8,128]{2,1,0:T(8,128)S(1)} %get-tuple-element.32), channel_id=1, source_target_pairs={{0,4},{1,5},{2,6},{3,7},{4,0},{5,1},{6,2},{7,3},{8,12},{9,13},{10,... | collective-permute-start | bytes 417800 | tf_op jit(solution)/shard_map/ppermute | solution.py:45
  19.0 7.4 %collective-permute-start.6 = (f32[50,8,128]{2,1,0:T(8,128)S(1)}, f32[50,8,128]{2,1,0:T(8,128)S(1)}, u32[]{:S(2)}, u32[]{:S(2)}) collective-permute-start(f32[50,8,128]{2,1,0:T(8,128)S(1)} %get-tuple-element.36), channel_id=1, source_target_pairs={{0,3},{1,2},{2,1},{3,0},{4,7},{5,6},{6,5},{7,4},{8,11},{9,10},{10,... | collective-permute-start | bytes 614408 | tf_op jit(solution)/shard_map/ppermute | solution.py:45
  20.1 6.3 %collective-permute-start.7 = (f32[50,8,128]{2,1,0:T(8,128)S(1)}, f32[50,8,128]{2,1,0:T(8,128)S(1)}, u32[]{:S(2)}, u32[]{:S(2)}) collective-permute-start(f32[50,8,128]{2,1,0:T(8,128)S(1)} %get-tuple-element.37), channel_id=1, source_target_pairs={{0,1},{1,0},{2,3},{3,2},{4,5},{5,4},{6,7},{7,6},{8,9},{9,8},{10,11... | collective-permute-start | bytes 614408 | tf_op jit(solution)/shard_map/ppermute | solution.py:45
  23.7 5.0 %collective-permute-start.8 = (f32[24,8,128]{2,1,0:T(8,128)S(1)}, f32[24,8,128]{2,1,0:T(8,128)S(1)}, u32[]{:S(2)}, u32[]{:S(2)}) collective-permute-start(f32[24,8,128]{2,1,0:T(8,128)S(1)} %get-tuple-element.38), channel_id=1, source_target_pairs={{0,3},{1,2},{2,1},{3,0},{4,7},{5,6},{6,5},{7,4},{8,11},{9,10},{10,... | collective-permute-start | bytes 294920 | tf_op jit(solution)/shard_map/ppermute | solution.py:45
  24.9 3.7 %collective-permute-start.9 = (f32[24,8,128]{2,1,0:T(8,128)S(1)}, f32[24,8,128]{2,1,0:T(8,128)S(1)}, u32[]{:S(2)}, u32[]{:S(2)}) collective-permute-start(f32[24,8,128]{2,1,0:T(8,128)S(1)} %get-tuple-element.39), channel_id=1, source_target_pairs={{0,1},{1,0},{2,3},{3,2},{4,5},{5,4},{6,7},{7,6},{8,9},{9,8},{10,11... | collective-permute-start | bytes 294920 | tf_op jit(solution)/shard_map/ppermute | solution.py:45

commit v4 on v3

--- a/solution.py
+++ b/solution.py
@@ -31,6 +31,9 @@
         return (w, t ^ 1) if w in (0, wide - 1) else (((w - 1) ^ 1) + 1, t)
 
     def thick_second(w, t):
+        return (w ^ 2, t) if t in (0, thick - 1) else (w, ((t - 1) ^ 1) + 1)
+
+    def thick_across(w, t):
         return (w, thick - 1 - t) if t in (0, thick - 1) else (w, ((t - 1) ^ 1) + 1)
 
     return (
@@ -38,6 +41,7 @@
         flat(width_second),
         flat(lambda w, t: (w, t ^ 1)),
         flat(thick_second),
+        flat(thick_across),
     )
 
 
@@ -308,7 +312,7 @@
                 new[c, t, pl.ds(w, sub, stride=columns), :] = tau[c, t, w]
 
 
-def join_kernel(dims, ends, part, wb, wa, side, sa, sb):
+def join_kernel(dims, ends, part, wa, wb, side, sa, sb):
     layers, columns, sub = dims
     w_low, w_high, _, has_high = halves("width", ends[0])
     send_t = halves("thick", ends[1])[2]
@@ -448,7 +452,7 @@
     dims = (layers, columns, sub)
     rows = columns * sub
     tile = (sub, LANES)
-    w_first, w_second, t_first, t_second = swap_pairs(*ends)
+    w_first, w_second, t_first, t_second, t_across = swap_pairs(*ends)
     dev, vel, stiff = as_tiles(deviation), as_tiles(velocity), as_tiles(stiffness)
 
     wa, wb, ta, tb = call(
@@ -490,14 +494,14 @@
         [(3, layers + 1, columns - 1, *tile)] + [(broad, *tile)] * 2,
         count=3, cost=2 * 1024 * 1024,
     )(tau, part, stiff)
-    mb = swap(sb, t_second)
+    mb = swap(sb, t_across)
     ma = swap(sa, t_first)
 
     side, sa, sb = call(
         functools.partial(join_kernel, dims, ends),
         [(3, layers + 1, 4, *tile)] + [(24, *tile)] * 2,
         count=3,
-    )(part, wb, wa)
+    )(part, wa, wb)
     jb = swap(sb, t_second)
     ja = swap(sa, t_first)
 

time: 43.3 us -> 40.4 us (0.933)
  blocking collectives: 12.7 us -> 11.5 us
  waiting for transfers between devices: 6.88 us -> 5.79 us
  starting transfers between devices: 12.7 us -> 12.1 us
    all_to_all x1, blocking collectives: 12.7 us -> 11.5 us  [on_device(): sums = lax.all_to_all(sums, AXES, 0, 0, tiled=True)]
    ppermute x10, waiting for transfers between devices: 6.88 us -> 5.79 us  [swap(): return lax.ppermute(value, AXES, pairs)]
    ppermute x10, starting transfers between devices: 12.7 us -> 12.1 us  [swap(): return lax.ppermute(value, AXES, pairs)]
  transfers between devices with their start and end apart: 10 -> 10, of which waited for: 3 -> 2; matrix products, arithmetic and copies ran while one was open for 0% -> 0% of each run, Pallas kernels for 8% -> 9%
where the time goes in v4:
time: 40.4 us; the launch traced here: 40.1 us
  starting transfers between devices  12.1 us (30%)
  blocking collectives  11.5 us (28%)
  Pallas kernels  6.95 us (17%)
  waiting for transfers between devices  5.79 us (14%)
  local copies, waits for them, and re-layouts  3.04 us (8%)
  between operations  0.73 us (2%)
    ppermute x10, starting transfers between devices, swap(): return lax.ppermute(value, AXES, pairs)  12.1 us
    all_to_all x1, blocking collectives, on_device(): sums = lax.all_to_all(sums, AXES, 0, 0, tiled=True)  11.5 us
    ppermute x10, waiting for transfers between devices, swap(): return lax.ppermute(value, AXES, pairs)  5.79 us
    unnamed x8, local copies, waits for them, and re-layouts  3.04 us
    pallas_call x1, Pallas kernels, on_device(): call(functools.partial(inner_kernel, dims), [(9, layers + 2, columns + 2,...  2.12 us
    pallas_call x1, Pallas kernels, on_device(): call(functools.partial(pack_kernel, dims, ends), [(9, layers, *tile)] * 2...  1.5 us
    pallas_call x1, Pallas kernels, on_device(): call(functools.partial(emit_kernel, dims), [(6, layers, rows, LANES), til...  1.01 us
    pallas_call x1, Pallas kernels, on_device(): call(functools.partial(finish_kernel, dims), [(3, layers, rows, LANES)],...  0.95 us
  transfers between devices with their start and end apart: 10, of which 2 were waited for; matrix products, arithmetic and copies ran while one was open for 0% of the time, Pallas kernels for 9%

profile of v4, /device:TPU:0, one launch (start us, length us, event | category | flops | bytes accessed | tf_op | source)
XLA Modules:
  0.0 40.1 jit_solution(11117636677473494263)
XLA Ops:
  0.6 1.5 %shard_map.50 = (f32[9,4,8,128]{3,2,1,0:T(8,128)S(1)}, f32[9,4,8,128]{3,2,1,0:T(8,128)S(1)}, f32[9,64,128]{2,1,0:T(8,128)S(1)}, f32[9,64,128]{2,1,0:T(8,128)S(1)}) custom-call(f32[6,4,64,128]{3,2,1,0:T(8,128)} %bitcast.25, f32[3,4,64,128]{3,2,1,0:T(8,128)} %bitcast.31), custom_call_target="tpu_custom_call" | custom-call | tf_op jit(solution)/shard_map/pallas_call | solution.py:458
  2.1 0.5 %collective-permute-start.1 = (f32[9,4,8,128]{3,2,1,0:T(8,128)S(1)}, f32[9,4,8,128]{3,2,1,0:T(8,128)S(1)}, u32[]{:S(2)}, u32[]{:S(2)}) collective-permute-start(f32[9,4,8,128]{3,2,1,0:T(8,128)S(1)} %get-tuple-element.26), channel_id=1, source_target_pairs={{0,1},{1,0},{2,3},{3,2},{4,8},{5,9},{6,10},{7,11},{8,4},{9,5},{10,... | collective-permute-start | bytes 442376 | tf_op jit(solution)/shard_map/ppermute | solution.py:49
  2.7 4.0 %collective-permute-start = (f32[9,4,8,128]{3,2,1,0:T(8,128)S(1)}, f32[9,4,8,128]{3,2,1,0:T(8,128)S(1)}, u32[]{:S(2)}, u32[]{:S(2)}) collective-permute-start(f32[9,4,8,128]{3,2,1,0:T(8,128)S(1)} %get-tuple-element.23.after_pack), channel_id=1, source_target_pairs={{0,4},{1,5},{2,6},{3,7},{4,0},{5,1},{6,2},{7,3},{8,12},{9,13},{10,... | collective-permute-start | bytes 442376 | tf_op jit(solution)/shard_map/ppermute | solution.py:49
  6.7 0.0 collective-permute-start.2
  6.7 1.6 %collective-permute-start.3 = (f32[9,64,128]{2,1,0:T(8,128)S(1)}, f32[9,64,128]{2,1,0:T(8,128)S(1)}, u32[]{:S(2)}, u32[]{:S(2)}) collective-permute-start(f32[9,64,128]{2,1,0:T(8,128)S(1)} %get-tuple-element.28), channel_id=1, source_target_pairs={{0,8},{1,2},{2,1},{3,11},{4,12},{5,6},{6,5},{7,15},{8,0},{9,10},{1... | collective-permute-start | bytes 884744 | tf_op jit(solution)/shard_map/ppermute | solution.py:49
  8.3 1.1 %copy-done = f32[6,4,8,1024]{3,2,1,0:T(8,128)S(1)} copy-done((f32[6,4,8,1024]{3,2,1,0:T(8,128)S(1)}, f32[6,4,8,1024]{3,2,1,0:T(8,128)}, u32[]{:S(2)}) %copy-start) | copy-done | bytes 786456
  9.4 0.9 %copy-done.1 = f32[4,8,1024]{2,1,0:T(8,128)S(1)} copy-done((f32[4,8,1024]{2,1,0:T(8,128)S(1)}, f32[4,8,1024]{2,1,0:T(8,128)}, u32[]{:S(2)}) %copy-start.1) | copy-done | bytes 131096
  10.3 1.0 %copy-done.3 = f32[3,4,8,1024]{3,2,1,0:T(8,128)S(1)} copy-done((f32[3,4,8,1024]{3,2,1,0:T(8,128)S(1)}, f32[3,4,8,1024]{3,2,1,0:T(8,128)}, u32[]{:S(2)}) %copy-start.3) | copy-done | bytes 393240
  11.3 2.1 %shard_map.51 = (f32[9,6,10,8,128]{4,3,2,1,0:T(8,128)S(1)}, f32[6,4,8,8,128]{4,3,2,1,0:T(8,128)S(1)}) custom-call(f32[6,4,64,128]{3,2,1,0:T(8,128)S(1)} %bitcast.26, f32[3,4,64,128]{3,2,1,0:T(8,128)S(1)} %bitcast.32, f32[9,4,8,128]{3,2,1,0:T(8,128)S(1)} %get-tuple-element.23.after_pack, f32[4,64,128]{2,1,0:T(8,128)S(1)} %bitcast.27), custom_call_target="tpu_custom_call" | custom-call | bytes 12582912 | tf_op jit(solution)/shard_map/pallas_call | solution.py:470
  13.4 0.0 collective-permute-done.1.wb
  13.4 0.0 collective-permute-done.wa
  13.4 0.1 shard_map.52.tau_in
  13.6 0.0 copy-start.2
  13.6 0.0 collective-permute-done.2.ta
  13.6 0.0 collective-permute-done.3.tb
  13.6 0.3 shard_map.53
  13.9 1.4 %collective-permute-start.4 = (f32[34,8,128]{2,1,0:T(8,128)S(1)}, f32[34,8,128]{2,1,0:T(8,128)S(1)}, u32[]{:S(2)}, u32[]{:S(2)}) collective-permute-start(f32[34,8,128]{2,1,0:T(8,128)S(1)} %get-tuple-element.31), channel_id=1, source_target_pairs={{0,4},{1,5},{2,6},{3,7},{4,0},{5,1},{6,2},{7,3},{8,12},{9,13},{10,... | collective-permute-start | bytes 417800 | tf_op jit(solution)/shard_map/ppermute | solution.py:49
  15.3 0.0 collective-permute-start.5
  15.3 0.2 shard_map.56
  15.5 1.7 %collective-permute-start.6 = (f32[50,8,128]{2,1,0:T(8,128)S(1)}, f32[50,8,128]{2,1,0:T(8,128)S(1)}, u32[]{:S(2)}, u32[]{:S(2)}) collective-permute-start(f32[50,8,128]{2,1,0:T(8,128)S(1)} %get-tuple-element.36), channel_id=1, source_target_pairs={{0,3},{1,2},{2,1},{3,0},{4,7},{5,6},{6,5},{7,4},{8,11},{9,10},{10,... | collective-permute-start | bytes 614408 | tf_op jit(solution)/shard_map/ppermute | solution.py:49
  17.2 0.0 collective-permute-start.7
  17.2 4.2 %collective-permute-done.4.wa = f32[34,8,128]{2,1,0:T(8,128)S(1)} collective-permute-done((f32[34,8,128]{2,1,0:T(8,128)S(1)}, f32[34,8,128]{2,1,0:T(8,128)S(1)}, u32[]{:S(2)}, u32[]{:S(2)}) %collective-permute-start.4) | collective-permute-done | bytes 139296 | tf_op jit(solution)/shard_map/ppermute | solution.py:49
  21.4 0.0 collective-permute-done.5.wb
  21.5 2.8 %collective-permute-start.8 = (f32[24,8,128]{2,1,0:T(8,128)S(1)}, f32[24,8,128]{2,1,0:T(8,128)S(1)}, u32[]{:S(2)}, u32[]{:S(2)}) collective-permute-start(f32[24,8,128]{2,1,0:T(8,128)S(1)} %get-tuple-element.38), channel_id=1, source_target_pairs={{0,8},{1,2},{2,1},{3,11},{4,12},{5,6},{6,5},{7,15},{8,0},{9,10},{1... | collective-permute-start | bytes 294920 | tf_op jit(solution)/shard_map/ppermute | solution.py:49
  24.3 0.0 collective-permute-start.9
  24.3 1.0 %shard_map.55 = (f32[6,4,64,128]{3,2,1,0:T(8,128)}, f32[8,128]{1,0:T(8,128)S(1)}) custom-call(f32[6,4,8,8,128]{4,3,2,1,0:T(8,128)S(1)} %get-tuple-element.29.tau, f32[3,5,4,8,128]{4,3,2,1,0:T(8,128)S(1)} %get-tuple-element.33.after_join.side), custom_call_target="tpu_custom_call" | custom-call | bytes 6291456 | tf_op jit(solution)/shard_map/pallas_call | solution.py:508
  25.3 0.0 collective-permute-done.6.mb
  25.3 0.0 collective-permute-done.7.ma
  25.3 1.6 %collective-permute-done.8.jb = f32[24,8,128]{2,1,0:T(8,128)S(1)} collective-permute-done((f32[24,8,128]{2,1,0:T(8,128)S(1)}, f32[24,8,128]{2,1,0:T(8,128)S(1)}, u32[]{:S(2)}, u32[]{:S(2)}) %collective-permute-start.8) | collective-permute-done | bytes 98336 | tf_op jit(solution)/shard_map/ppermute | solution.py:49
  26.9 0.7 %shard_map.57 = (f32[3,4,8,8,128]{4,3,2,1,0:T(8,128)S(1)}, f32[3,4,8,8,128]{4,3,2,1,0:T(8,128)S(1)}, f32[32,1,128]{2,1,0:T(1,128)S(1)}) custom-call(f32[3,5,7,8,128]{4,3,2,1,0:T(8,128)S(1)} %get-tuple-element.35.mid, f32[3,5,4,8,128]{4,3,2,1,0:T(8,128)S(1)} %get-tuple-element.33.after_join.side, f32[50,8,128]{2,1,0:T(8,128)S(1)} %collective-permute-done.6.mb, ...), custom_call_target="tpu_custom_call" | custom-call | tf_op jit(solution)/shard_map/pallas_call | solution.py:513
  27.6 11.5 %all_to_all.5.sums = f32[32,1,128]{2,1,0:T(1,128)S(1)} all-to-all(f32[32,1,128]{2,1,0:T(1,128)S(1)} %get-tuple-element.41), channel_id=1, replica_groups=mesh['width'=8,'thick'=4] {'width','thick'}, dimensions={0} | all-to-all | bytes 32768 | tf_op jit(solution)/shard_map/all_to_all | solution.py:519
  39.2 0.9 %shard_map.58 = f32[3,4,64,128]{3,2,1,0:T(8,128)} custom-call(f32[32,1,128]{2,1,0:T(1,128)S(1)} %all_to_all.5.sums, f32[3,4,8,8,128]{4,3,2,1,0:T(8,128)S(1)} %get-tuple-element.42.force, f32[3,4,8,8,128]{4,3,2,1,0:T(8,128)S(1)} %get-tuple-element.43.image), custom_call_target="tpu_custom_call" | custom-call | tf_op jit(solution)/shard_map/pallas_call | solution.py:521
  (6 shorter events, 0.1 us)
Async XLA Ops:
  2.1 11.3 %collective-permute-start.1 = (f32[9,4,8,128]{3,2,1,0:T(8,128)S(1)}, f32[9,4,8,128]{3,2,1,0:T(8,128)S(1)}, u32[]{:S(2)}, u32[]{:S(2)}) collective-permute-start(f32[9,4,8,128]{3,2,1,0:T(8,128)S(1)} %get-tuple-element.26), channel_id=1, source_target_pairs={{0,1},{1,0},{2,3},{3,2},{4,8},{5,9},{6,10},{7,11},{8,4},{9,5},{10,... | collective-permute-start | bytes 442376 | tf_op jit(solution)/shard_map/ppermute | solution.py:49
  2.7 10.8 %collective-permute-start = (f32[9,4,8,128]{3,2,1,0:T(8,128)S(1)}, f32[9,4,8,128]{3,2,1,0:T(8,128)S(1)}, u32[]{:S(2)}, u32[]{:S(2)}) collective-permute-start(f32[9,4,8,128]{3,2,1,0:T(8,128)S(1)} %get-tuple-element.23.after_pack), channel_id=1, source_target_pairs={{0,4},{1,5},{2,6},{3,7},{4,0},{5,1},{6,2},{7,3},{8,12},{9,13},{10,... | collective-permute-start | bytes 442376 | tf_op jit(solution)/shard_map/ppermute | solution.py:49
  6.7 6.9 %collective-permute-start.2 = (f32[9,64,128]{2,1,0:T(8,128)S(1)}, f32[9,64,128]{2,1,0:T(8,128)S(1)}, u32[]{:S(2)}, u32[]{:S(2)}) collective-permute-start(f32[9,64,128]{2,1,0:T(8,128)S(1)} %get-tuple-element.27), channel_id=1, source_target_pairs={{0,1},{1,0},{2,3},{3,2},{4,5},{5,4},{6,7},{7,6},{8,9},{9,8},{10,11... | collective-permute-start | bytes 884744 | tf_op jit(solution)/shard_map/ppermute | solution.py:49
  6.7 6.9 %collective-permute-start.3 = (f32[9,64,128]{2,1,0:T(8,128)S(1)}, f32[9,64,128]{2,1,0:T(8,128)S(1)}, u32[]{:S(2)}, u32[]{:S(2)}) collective-permute-start(f32[9,64,128]{2,1,0:T(8,128)S(1)} %get-tuple-element.28), channel_id=1, source_target_pairs={{0,8},{1,2},{2,1},{3,11},{4,12},{5,6},{6,5},{7,15},{8,0},{9,10},{1... | collective-permute-start | bytes 884744 | tf_op jit(solution)/shard_map/ppermute | solution.py:49
  8.3 1.1 %copy-start = (f32[6,4,8,1024]{3,2,1,0:T(8,128)S(1)}, f32[6,4,8,1024]{3,2,1,0:T(8,128)}, u32[]{:S(2)}) copy-start(f32[6,4,8,1024]{3,2,1,0:T(8,128)} %param.3) | copy-start | bytes 2359300
  9.4 0.9 %copy-start.1 = (f32[4,8,1024]{2,1,0:T(8,128)S(1)}, f32[4,8,1024]{2,1,0:T(8,128)}, u32[]{:S(2)}) copy-start(f32[4,8,1024]{2,1,0:T(8,128)} %param.5) | copy-start | bytes 393220
  10.3 1.0 %copy-start.3 = (f32[3,4,8,1024]{3,2,1,0:T(8,128)S(1)}, f32[3,4,8,1024]{3,2,1,0:T(8,128)}, u32[]{:S(2)}) copy-start(f32[3,4,8,1024]{3,2,1,0:T(8,128)} %param.4) | copy-start | bytes 1179652
  13.6 1.8 %copy-start.2 = (f32[4,8,1024]{2,1,0:T(8,128)S(1)}, f32[4,8,1024]{2,1,0:T(8,128)}, u32[]{:S(2)}) copy-start(f32[4,8,1024]{2,1,0:T(8,128)} %param.5) | copy-start | bytes 393220
  13.9 7.5 %collective-permute-start.4 = (f32[34,8,128]{2,1,0:T(8,128)S(1)}, f32[34,8,128]{2,1,0:T(8,128)S(1)}, u32[]{:S(2)}, u32[]{:S(2)}) collective-permute-start(f32[34,8,128]{2,1,0:T(8,128)S(1)} %get-tuple-element.31), channel_id=1, source_target_pairs={{0,4},{1,5},{2,6},{3,7},{4,0},{5,1},{6,2},{7,3},{8,12},{9,13},{10,... | collective-permute-start | bytes 417800 | tf_op jit(solution)/shard_map/ppermute | solution.py:49
  15.3 6.1 %collective-permute-start.5 = (f32[34,8,128]{2,1,0:T(8,128)S(1)}, f32[34,8,128]{2,1,0:T(8,128)S(1)}, u32[]{:S(2)}, u32[]{:S(2)}) collective-permute-start(f32[34,8,128]{2,1,0:T(8,128)S(1)} %get-tuple-element.32), channel_id=1, source_target_pairs={{0,1},{1,0},{2,3},{3,2},{4,8},{5,9},{6,10},{7,11},{8,4},{9,5},{10,... | collective-permute-start | bytes 417800 | tf_op jit(solution)/shard_map/ppermute | solution.py:49
  15.5 9.8 %collective-permute-start.6 = (f32[50,8,128]{2,1,0:T(8,128)S(1)}, f32[50,8,128]{2,1,0:T(8,128)S(1)}, u32[]{:S(2)}, u32[]{:S(2)}) collective-permute-start(f32[50,8,128]{2,1,0:T(8,128)S(1)} %get-tuple-element.36), channel_id=1, source_target_pairs={{0,3},{1,2},{2,1},{3,0},{4,7},{5,6},{6,5},{7,4},{8,11},{9,10},{10,... | collective-permute-start | bytes 614408 | tf_op jit(solution)/shard_map/ppermute | solution.py:49
  17.2 8.1 %collective-permute-start.7 = (f32[50,8,128]{2,1,0:T(8,128)S(1)}, f32[50,8,128]{2,1,0:T(8,128)S(1)}, u32[]{:S(2)}, u32[]{:S(2)}) collective-permute-start(f32[50,8,128]{2,1,0:T(8,128)S(1)} %get-tuple-element.37), channel_id=1, source_target_pairs={{0,1},{1,0},{2,3},{3,2},{4,5},{5,4},{6,7},{7,6},{8,9},{9,8},{10,11... | collective-permute-start | bytes 614408 | tf_op jit(solution)/shard_map/ppermute | solution.py:49
  21.5 5.4 %collective-permute-start.8 = (f32[24,8,128]{2,1,0:T(8,128)S(1)}, f32[24,8,128]{2,1,0:T(8,128)S(1)}, u32[]{:S(2)}, u32[]{:S(2)}) collective-permute-start(f32[24,8,128]{2,1,0:T(8,128)S(1)} %get-tuple-element.38), channel_id=1, source_target_pairs={{0,8},{1,2},{2,1},{3,11},{4,12},{5,6},{6,5},{7,15},{8,0},{9,10},{1... | collective-permute-start | bytes 294920 | tf_op jit(solution)/shard_map/ppermute | solution.py:49
  24.3 2.6 %collective-permute-start.9 = (f32[24,8,128]{2,1,0:T(8,128)S(1)}, f32[24,8,128]{2,1,0:T(8,128)S(1)}, u32[]{:S(2)}, u32[]{:S(2)}) collective-permute-start(f32[24,8,128]{2,1,0:T(8,128)S(1)} %get-tuple-element.39), channel_id=1, source_target_pairs={{0,1},{1,0},{2,3},{3,2},{4,5},{5,4},{6,7},{7,6},{8,9},{9,8},{10,11... | collective-permute-start | bytes 294920 | tf_op jit(solution)/shard_map/ppermute | solution.py:49

commit v5 on v4

--- a/solution.py
+++ b/solution.py
@@ -16,7 +16,6 @@
 PAIRS = ((0, 0), (1, 1), (2, 2), (0, 1), (0, 2), (1, 2))
 SLOT = ((0, 3, 4), (3, 1, 5), (4, 5, 2))
 VMEM_LIMIT = 40 * 1024 * 1024
-PACK_LIMIT = 53 * 1024 * 1024
 
 
 def swap_pairs(wide, thick):
@@ -42,6 +41,7 @@
         flat(lambda w, t: (w, t ^ 1)),
         flat(thick_second),
         flat(thick_across),
+        [p for p in flat(thick_across) if p[0] % thick not in (0, thick - 1)],
     )
 
 
@@ -111,28 +111,32 @@
             copies.append(pltpu.make_async_copy(source.at[c], target.at[c], sems.at[len(copies)]))
     for copy in copies:
         copy.start()
-    for copy in copies:
-        copy.wait()
-
-
-def pack_kernel(dims, ends, dev_hbm, vel_hbm, wa, wb, ta, tb, dev, vel, sems):
+    return copies
+
+
+def pack_kernel(
+    dims, ends, dev_hbm, vel_hbm, stiff_hbm, wa, wb, ta, tb, stiff, dev, vel, sems
+):
     layers, columns, sub = dims
     send_w = halves("width", ends[0])[2]
     send_t = halves("thick", ends[1])[2]
-    fetch((dev_hbm, vel_hbm), (dev, vel), sems)
+    copies = fetch((dev_hbm, vel_hbm, stiff_hbm), (dev, vel, stiff), sems)
     for c in range(9):
         ref, lead = (dev, (c,)) if c < 6 else (vel, (c - 6,))
+        copies[c].wait()
         for t in range(layers):
             low = row_of(ref, (*lead, t), 0, columns, sub)
             high = row_of(ref, (*lead, t), columns - 1, columns, sub)
             wa[c, t], wb[c, t] = send_w(low, high)
         ta[c], tb[c] = send_t(ref[(*lead, 0)], ref[(*lead, layers - 1)])
+    for copy in copies[9:]:
+        copy.wait()
 
 
 HALF = 0.5 * TIME_STEP
 
 
-def inner_kernel(dims, dev, vel, after_pack, stiff, ext, tau):
+def inner_kernel(dims, dev, vel, ext, tau):
     layers, columns, sub = dims
     masks = edge_masks(sub)
     zero = jnp.zeros((sub, LANES), jnp.float32)
@@ -428,7 +432,7 @@
 
 
 def call(
-    kernel, shapes, scratch=(), hbm=(), count=0, copies=0, aliases=None, cost=None, work=0, limit=VMEM_LIMIT
+    kernel, shapes, scratch=(), hbm=(), count=0, copies=0, aliases=None, cost=None, work=0
 ):
     anywhere, local = pl.BlockSpec(memory_space=pl.ANY), pl.BlockSpec(memory_space=pltpu.VMEM)
     extra = [pltpu.SemaphoreType.DMA((copies,))] if copies else []
@@ -441,7 +445,7 @@
         in_specs=[anywhere if k in hbm else local for k in range(count)],
         scratch_shapes=[pltpu.VMEM(s, jnp.float32) for s in scratch] + extra,
         input_output_aliases=aliases or {},
-        compiler_params=pltpu.CompilerParams(vmem_limit_bytes=limit),
+        compiler_params=pltpu.CompilerParams(vmem_limit_bytes=VMEM_LIMIT),
         **more,
     )
 
@@ -452,17 +456,17 @@
     dims = (layers, columns, sub)
     rows = columns * sub
     tile = (sub, LANES)
-    w_first, w_second, t_first, t_second, t_across = swap_pairs(*ends)
+    w_first, w_second, t_first, t_second, t_across, t_missing = swap_pairs(*ends)
     dev, vel, stiff = as_tiles(deviation), as_tiles(velocity), as_tiles(stiffness)
 
-    wa, wb, ta, tb = call(
+    wa, wb, ta, tb, stiff, dev, vel = call(
         functools.partial(pack_kernel, dims, ends),
-        [(9, layers, *tile)] * 2 + [(9, rows, LANES)] * 2,
-        [(6, layers, rows, LANES), (3, layers, rows, LANES)],
-        hbm=(0, 1), count=2, copies=9, limit=PACK_LIMIT,
-    )(dev, vel)
-    packed = wa
-    tb = swap(tb, t_second)
+        [(9, layers, *tile)] * 2
+        + [(9, rows, LANES)] * 2
+        + [(layers, rows, LANES), (6, layers, rows, LANES), (3, layers, rows, LANES)],
+        hbm=(0, 1, 2), count=3, copies=9 + layers,
+    )(*[pltpu.with_memory_space_constraint(x, pltpu.HBM) for x in (dev, vel, stiff)])
+    tb = swap(tb, t_missing)
     wb = swap(wb, w_second)
     wa = swap(wa, w_first)
     ta = swap(ta, t_first)
@@ -470,8 +474,8 @@
     ext, tau = call(
         functools.partial(inner_kernel, dims),
         [(9, layers + 2, columns + 2, *tile), (6, layers, columns, *tile)],
-        hbm=(2,), count=4, cost=12 * 1024 * 1024,
-    )(dev, vel, packed, stiff)
+        count=2, cost=12 * 1024 * 1024,
+    )(dev, vel)
 
     (tau,) = call(
         functools.partial(side_kernel, dims, ends),

time: 40.4 us -> 39.5 us (0.978)
  local copies, waits for them, and re-layouts: 3.04 us -> 0 us
  blocking collectives: 11.5 us -> 12.8 us
  starting transfers between devices: 12.1 us -> 12.7 us
    unnamed x8 -> x0, local copies, waits for them, and re-layouts: 3.04 us -> none
    all_to_all x1, blocking collectives: 11.5 us -> 12.8 us  [on_device(): sums = lax.all_to_all(sums, AXES, 0, 0, tiled=True)]
    ppermute x10, starting transfers between devices: 12.1 us -> 12.7 us  [swap(): return lax.ppermute(value, AXES, pairs)]
  transfers between devices with their start and end apart: 10 -> 10, of which waited for: 2 -> 4; matrix products, arithmetic and copies ran while one was open for 0% -> 0% of each run, Pallas kernels for 9% -> 9%
where the time goes in v5:
time: 39.5 us; the launch traced here: 39.3 us
  blocking collectives  12.8 us (32%)
  starting transfers between devices  12.7 us (32%)
  Pallas kernels  6.9 us (17%)
  waiting for transfers between devices  6.17 us (16%)
  between operations  0.71 us (2%)
    all_to_all x1, blocking collectives, on_device(): sums = lax.all_to_all(sums, AXES, 0, 0, tiled=True)  12.8 us
    ppermute x10, starting transfers between devices, swap(): return lax.ppermute(value, AXES, pairs)  12.7 us
    ppermute x10, waiting for transfers between devices, swap(): return lax.ppermute(value, AXES, pairs)  6.17 us
    pallas_call x1, Pallas kernels, on_device(): call(functools.partial(inner_kernel, dims), [(9, layers + 2, columns + 2,...  2.12 us
    pallas_call x1, Pallas kernels, on_device(): call(functools.partial(pack_kernel, dims, ends), [(9, layers, *tile)] * 2...  1.46 us
    pallas_call x1, Pallas kernels, on_device(): call(functools.partial(emit_kernel, dims), [(6, layers, rows, LANES), til...  1.01 us
    pallas_call x1, Pallas kernels, on_device(): call(functools.partial(finish_kernel, dims), [(3, layers, rows, LANES)],...  0.95 us
  transfers between devices with their start and end apart: 10, of which 4 were waited for; matrix products, arithmetic and copies ran while one was open for 0% of the time, Pallas kernels for 9%

profile of v5, /device:TPU:0, one launch (start us, length us, event | category | flops | bytes accessed | tf_op | source)
XLA Modules:
  0.0 39.3 jit_solution(6383269985122567225)
XLA Ops:
  0.6 1.5 %shard_map.50 = (f32[9,4,8,128]{3,2,1,0:T(8,128)S(1)}, f32[9,4,8,128]{3,2,1,0:T(8,128)S(1)}, f32[9,64,128]{2,1,0:T(8,128)S(1)}, f32[9,64,128]{2,1,0:T(8,128)S(1)...) custom-call(f32[6,4,64,128]{3,2,1,0:T(8,128)} %bitcast.25, ...), custom_call_target="tpu_custom_call" | custom-call | tf_op jit(solution)/shard_map/pallas_call | solution.py:462
  2.1 3.0 %collective-permute-start = (f32[9,4,8,128]{3,2,1,0:T(8,128)S(1)}, f32[9,4,8,128]{3,2,1,0:T(8,128)S(1)}, u32[]{:S(2)}, u32[]{:S(2)}) collective-permute-start(f32[9,4,8,128]{3,2,1,0:T(8,128)S(1)} %get-tuple-element.30), channel_id=1, source_target_pairs={{0,4},{1,5},{2,6},{3,7},{4,0},{5,1},{6,2},{7,3},{8,12},{9,13},{10,... | collective-permute-start | bytes 442376 | tf_op jit(solution)/shard_map/ppermute | solution.py:49
  5.1 0.0 collective-permute-start.1
  5.1 0.5 %collective-permute-start.2 = (f32[9,64,128]{2,1,0:T(8,128)S(1)}, f32[9,64,128]{2,1,0:T(8,128)S(1)}, u32[]{:S(2)}, u32[]{:S(2)}) collective-permute-start(f32[9,64,128]{2,1,0:T(8,128)S(1)} %get-tuple-element.32), channel_id=1, source_target_pairs={{0,1},{1,0},{2,3},{3,2},{4,5},{5,4},{6,7},{7,6},{8,9},{9,8},{10,11... | collective-permute-start | bytes 884744 | tf_op jit(solution)/shard_map/ppermute | solution.py:49
  5.6 0.7 %collective-permute-start.3 = (f32[9,64,128]{2,1,0:T(8,128)S(1)}, f32[9,64,128]{2,1,0:T(8,128)S(1)}, u32[]{:S(2)}, u32[]{:S(2)}) collective-permute-start(f32[9,64,128]{2,1,0:T(8,128)S(1)} %get-tuple-element.33), channel_id=1, source_target_pairs={{1,2},{2,1},{5,6},{6,5},{9,10},{10,9},{13,14},{14,13},{17,18},{18,... | collective-permute-start | bytes 884744 | tf_op jit(solution)/shard_map/ppermute | solution.py:49
  6.3 2.1 %shard_map.51 = (f32[9,6,10,8,128]{4,3,2,1,0:T(8,128)S(1)}, f32[6,4,8,8,128]{4,3,2,1,0:T(8,128)S(1)}) custom-call(f32[6,4,64,128]{3,2,1,0:T(8,128)S(1)} %get-tuple-element.26.dev, f32[3,4,64,128]{3,2,1,0:T(8,128)S(1)} %get-tuple-element.27.vel), custom_call_target="tpu_custom_call" | custom-call | bytes 12582912 | tf_op jit(solution)/shard_map/pallas_call | solution.py:474
  8.4 3.0 %collective-permute-done.wa = f32[9,4,8,128]{3,2,1,0:T(8,128)S(1)} collective-permute-done((f32[9,4,8,128]{3,2,1,0:T(8,128)S(1)}, f32[9,4,8,128]{3,2,1,0:T(8,128)S(1)}, u32[]{:S(2)}, u32[]{:S(2)}) %collective-permute-start) | collective-permute-done | bytes 147488 | tf_op jit(solution)/shard_map/ppermute | solution.py:49
  11.4 0.0 collective-permute-done.1.wb
  11.4 0.1 shard_map.52.tau_in
  11.5 0.0 collective-permute-done.2.ta
  11.5 0.0 collective-permute-done.3.tb
  11.5 0.3 shard_map.53
  11.8 2.5 %collective-permute-start.4 = (f32[34,8,128]{2,1,0:T(8,128)S(1)}, f32[34,8,128]{2,1,0:T(8,128)S(1)}, u32[]{:S(2)}, u32[]{:S(2)}) collective-permute-start(f32[34,8,128]{2,1,0:T(8,128)S(1)} %get-tuple-element.37), channel_id=1, source_target_pairs={{0,4},{1,5},{2,6},{3,7},{4,0},{5,1},{6,2},{7,3},{8,12},{9,13},{10,... | collective-permute-start | bytes 417800 | tf_op jit(solution)/shard_map/ppermute | solution.py:49
  14.4 2.4 %collective-permute-start.5 = (f32[34,8,128]{2,1,0:T(8,128)S(1)}, f32[34,8,128]{2,1,0:T(8,128)S(1)}, u32[]{:S(2)}, u32[]{:S(2)}) collective-permute-start(f32[34,8,128]{2,1,0:T(8,128)S(1)} %get-tuple-element.38), channel_id=1, source_target_pairs={{0,1},{1,0},{2,3},{3,2},{4,8},{5,9},{6,10},{7,11},{8,4},{9,5},{10,... | collective-permute-start | bytes 417800 | tf_op jit(solution)/shard_map/ppermute | solution.py:49
  16.8 0.2 shard_map.56
  17.0 1.5 %collective-permute-start.6 = (f32[50,8,128]{2,1,0:T(8,128)S(1)}, f32[50,8,128]{2,1,0:T(8,128)S(1)}, u32[]{:S(2)}, u32[]{:S(2)}) collective-permute-start(f32[50,8,128]{2,1,0:T(8,128)S(1)} %get-tuple-element.42), channel_id=1, source_target_pairs={{0,3},{1,2},{2,1},{3,0},{4,7},{5,6},{6,5},{7,4},{8,11},{9,10},{10,... | collective-permute-start | bytes 614408 | tf_op jit(solution)/shard_map/ppermute | solution.py:49
  18.5 0.0 collective-permute-start.7
  18.5 1.6 %collective-permute-done.4.wa = f32[34,8,128]{2,1,0:T(8,128)S(1)} collective-permute-done((f32[34,8,128]{2,1,0:T(8,128)S(1)}, f32[34,8,128]{2,1,0:T(8,128)S(1)}, u32[]{:S(2)}, u32[]{:S(2)}) %collective-permute-start.4) | collective-permute-done | bytes 139296 | tf_op jit(solution)/shard_map/ppermute | solution.py:49
  20.1 0.0 collective-permute-done.5.wb
  20.2 2.0 %collective-permute-start.8 = (f32[24,8,128]{2,1,0:T(8,128)S(1)}, f32[24,8,128]{2,1,0:T(8,128)S(1)}, u32[]{:S(2)}, u32[]{:S(2)}) collective-permute-start(f32[24,8,128]{2,1,0:T(8,128)S(1)} %get-tuple-element.44), channel_id=1, source_target_pairs={{0,8},{1,2},{2,1},{3,11},{4,12},{5,6},{6,5},{7,15},{8,0},{9,10},{1... | collective-permute-start | bytes 294920 | tf_op jit(solution)/shard_map/ppermute | solution.py:49
  22.1 0.1 collective-permute-start.9
  22.3 1.0 %shard_map.55 = (f32[6,4,64,128]{3,2,1,0:T(8,128)}, f32[8,128]{1,0:T(8,128)S(1)}) custom-call(f32[6,4,8,8,128]{4,3,2,1,0:T(8,128)S(1)} %get-tuple-element.35.tau, f32[3,5,4,8,128]{4,3,2,1,0:T(8,128)S(1)} %get-tuple-element.39.after_join.side), custom_call_target="tpu_custom_call" | custom-call | bytes 6291456 | tf_op jit(solution)/shard_map/pallas_call | solution.py:512
  23.3 1.0 %collective-permute-done.6.mb = f32[50,8,128]{2,1,0:T(8,128)S(1)} collective-permute-done((f32[50,8,128]{2,1,0:T(8,128)S(1)}, f32[50,8,128]{2,1,0:T(8,128)S(1)}, u32[]{:S(2)}, u32[]{:S(2)}) %collective-permute-start.6) | collective-permute-done | bytes 204832 | tf_op jit(solution)/shard_map/ppermute | solution.py:49
  24.3 0.0 collective-permute-done.7.ma
  24.3 0.6 %collective-permute-done.8.jb = f32[24,8,128]{2,1,0:T(8,128)S(1)} collective-permute-done((f32[24,8,128]{2,1,0:T(8,128)S(1)}, f32[24,8,128]{2,1,0:T(8,128)S(1)}, u32[]{:S(2)}, u32[]{:S(2)}) %collective-permute-start.8) | collective-permute-done | bytes 98336 | tf_op jit(solution)/shard_map/ppermute | solution.py:49
  24.8 0.0 collective-permute-done.9.ja
  24.8 0.7 %shard_map.57 = (f32[3,4,8,8,128]{4,3,2,1,0:T(8,128)S(1)}, f32[3,4,8,8,128]{4,3,2,1,0:T(8,128)S(1)}, f32[32,1,128]{2,1,0:T(1,128)S(1)}) custom-call(f32[3,5,7,8,128]{4,3,2,1,0:T(8,128)S(1)} %get-tuple-element.41.mid, f32[3,5,4,8,128]{4,3,2,1,0:T(8,128)S(1)} %get-tuple-element.39.after_join.side, f32[50,8,128]{2,1,0:T(8,128)S(1)} %collective-permute-done.6.mb, ...), custom_call_target="tpu_custom_call" | custom-call | tf_op jit(solution)/shard_map/pallas_call | solution.py:517
  25.5 12.8 %all_to_all.5.sums = f32[32,1,128]{2,1,0:T(1,128)S(1)} all-to-all(f32[32,1,128]{2,1,0:T(1,128)S(1)} %get-tuple-element.47), channel_id=1, replica_groups=mesh['width'=8,'thick'=4] {'width','thick'}, dimensions={0} | all-to-all | bytes 32768 | tf_op jit(solution)/shard_map/all_to_all | solution.py:523
  38.4 0.9 %shard_map.58 = f32[3,4,64,128]{3,2,1,0:T(8,128)} custom-call(f32[32,1,128]{2,1,0:T(1,128)S(1)} %all_to_all.5.sums, f32[3,4,8,8,128]{4,3,2,1,0:T(8,128)S(1)} %get-tuple-element.48.force, f32[3,4,8,8,128]{4,3,2,1,0:T(8,128)S(1)} %get-tuple-element.49.image), custom_call_target="tpu_custom_call" | custom-call | tf_op jit(solution)/shard_map/pallas_call | solution.py:525
  (1 shorter events, 0.0 us)
Async XLA Ops:
  2.1 9.3 %collective-permute-start = (f32[9,4,8,128]{3,2,1,0:T(8,128)S(1)}, f32[9,4,8,128]{3,2,1,0:T(8,128)S(1)}, u32[]{:S(2)}, u32[]{:S(2)}) collective-permute-start(f32[9,4,8,128]{3,2,1,0:T(8,128)S(1)} %get-tuple-element.30), channel_id=1, source_target_pairs={{0,4},{1,5},{2,6},{3,7},{4,0},{5,1},{6,2},{7,3},{8,12},{9,13},{10,... | collective-permute-start | bytes 442376 | tf_op jit(solution)/shard_map/ppermute | solution.py:49
  5.1 6.3 %collective-permute-start.1 = (f32[9,4,8,128]{3,2,1,0:T(8,128)S(1)}, f32[9,4,8,128]{3,2,1,0:T(8,128)S(1)}, u32[]{:S(2)}, u32[]{:S(2)}) collective-permute-start(f32[9,4,8,128]{3,2,1,0:T(8,128)S(1)} %get-tuple-element.31), channel_id=1, source_target_pairs={{0,1},{1,0},{2,3},{3,2},{4,8},{5,9},{6,10},{7,11},{8,4},{9,5},{10,... | collective-permute-start | bytes 442376 | tf_op jit(solution)/shard_map/ppermute | solution.py:49
  5.1 6.4 %collective-permute-start.2 = (f32[9,64,128]{2,1,0:T(8,128)S(1)}, f32[9,64,128]{2,1,0:T(8,128)S(1)}, u32[]{:S(2)}, u32[]{:S(2)}) collective-permute-start(f32[9,64,128]{2,1,0:T(8,128)S(1)} %get-tuple-element.32), channel_id=1, source_target_pairs={{0,1},{1,0},{2,3},{3,2},{4,5},{5,4},{6,7},{7,6},{8,9},{9,8},{10,11... | collective-permute-start | bytes 884744 | tf_op jit(solution)/shard_map/ppermute | solution.py:49
  5.6 5.9 %collective-permute-start.3 = (f32[9,64,128]{2,1,0:T(8,128)S(1)}, f32[9,64,128]{2,1,0:T(8,128)S(1)}, u32[]{:S(2)}, u32[]{:S(2)}) collective-permute-start(f32[9,64,128]{2,1,0:T(8,128)S(1)} %get-tuple-element.33), channel_id=1, source_target_pairs={{1,2},{2,1},{5,6},{6,5},{9,10},{10,9},{13,14},{14,13},{17,18},{18,... | collective-permute-start | bytes 884744 | tf_op jit(solution)/shard_map/ppermute | solution.py:49
  11.8 8.3 %collective-permute-start.4 = (f32[34,8,128]{2,1,0:T(8,128)S(1)}, f32[34,8,128]{2,1,0:T(8,128)S(1)}, u32[]{:S(2)}, u32[]{:S(2)}) collective-permute-start(f32[34,8,128]{2,1,0:T(8,128)S(1)} %get-tuple-element.37), channel_id=1, source_target_pairs={{0,4},{1,5},{2,6},{3,7},{4,0},{5,1},{6,2},{7,3},{8,12},{9,13},{10,... | collective-permute-start | bytes 417800 | tf_op jit(solution)/shard_map/ppermute | solution.py:49
  14.4 5.7 %collective-permute-start.5 = (f32[34,8,128]{2,1,0:T(8,128)S(1)}, f32[34,8,128]{2,1,0:T(8,128)S(1)}, u32[]{:S(2)}, u32[]{:S(2)}) collective-permute-start(f32[34,8,128]{2,1,0:T(8,128)S(1)} %get-tuple-element.38), channel_id=1, source_target_pairs={{0,1},{1,0},{2,3},{3,2},{4,8},{5,9},{6,10},{7,11},{8,4},{9,5},{10,... | collective-permute-start | bytes 417800 | tf_op jit(solution)/shard_map/ppermute | solution.py:49
  17.0 7.3 %collective-permute-start.6 = (f32[50,8,128]{2,1,0:T(8,128)S(1)}, f32[50,8,128]{2,1,0:T(8,128)S(1)}, u32[]{:S(2)}, u32[]{:S(2)}) collective-permute-start(f32[50,8,128]{2,1,0:T(8,128)S(1)} %get-tuple-element.42), channel_id=1, source_target_pairs={{0,3},{1,2},{2,1},{3,0},{4,7},{5,6},{6,5},{7,4},{8,11},{9,10},{10,... | collective-permute-start | bytes 614408 | tf_op jit(solution)/shard_map/ppermute | solution.py:49
  18.5 5.8 %collective-permute-start.7 = (f32[50,8,128]{2,1,0:T(8,128)S(1)}, f32[50,8,128]{2,1,0:T(8,128)S(1)}, u32[]{:S(2)}, u32[]{:S(2)}) collective-permute-start(f32[50,8,128]{2,1,0:T(8,128)S(1)} %get-tuple-element.43), channel_id=1, source_target_pairs={{0,1},{1,0},{2,3},{3,2},{4,5},{5,4},{6,7},{7,6},{8,9},{9,8},{10,11... | collective-permute-start | bytes 614408 | tf_op jit(solution)/shard_map/ppermute | solution.py:49
  20.2 4.7 %collective-permute-start.8 = (f32[24,8,128]{2,1,0:T(8,128)S(1)}, f32[24,8,128]{2,1,0:T(8,128)S(1)}, u32[]{:S(2)}, u32[]{:S(2)}) collective-permute-start(f32[24,8,128]{2,1,0:T(8,128)S(1)} %get-tuple-element.44), channel_id=1, source_target_pairs={{0,8},{1,2},{2,1},{3,11},{4,12},{5,6},{6,5},{7,15},{8,0},{9,10},{1... | collective-permute-start | bytes 294920 | tf_op jit(solution)/shard_map/ppermute | solution.py:49
  22.1 2.7 %collective-permute-start.9 = (f32[24,8,128]{2,1,0:T(8,128)S(1)}, f32[24,8,128]{2,1,0:T(8,128)S(1)}, u32[]{:S(2)}, u32[]{:S(2)}) collective-permute-start(f32[24,8,128]{2,1,0:T(8,128)S(1)} %get-tuple-element.45), channel_id=1, source_target_pairs={{0,1},{1,0},{2,3},{3,2},{4,5},{5,4},{6,7},{7,6},{8,9},{9,8},{10,11... | collective-permute-start | bytes 294920 | tf_op jit(solution)/shard_map/ppermute | solution.py:49

commit v6 on v5

--- a/solution.py
+++ b/solution.py
@@ -107,8 +107,7 @@
 def fetch(sources, targets, sems):
     copies = []
     for source, target in zip(sources, targets):
-        for c in range(source.shape[0]):
-            copies.append(pltpu.make_async_copy(source.at[c], target.at[c], sems.at[len(copies)]))
+        copies.append(pltpu.make_async_copy(source, target, sems.at[len(copies)]))
     for copy in copies:
         copy.start()
     return copies
@@ -121,15 +120,16 @@
     send_w = halves("width", ends[0])[2]
     send_t = halves("thick", ends[1])[2]
     copies = fetch((dev_hbm, vel_hbm, stiff_hbm), (dev, vel, stiff), sems)
+    copies[0].wait()
+    copies[1].wait()
     for c in range(9):
         ref, lead = (dev, (c,)) if c < 6 else (vel, (c - 6,))
-        copies[c].wait()
         for t in range(layers):
             low = row_of(ref, (*lead, t), 0, columns, sub)
             high = row_of(ref, (*lead, t), columns - 1, columns, sub)
             wa[c, t], wb[c, t] = send_w(low, high)
         ta[c], tb[c] = send_t(ref[(*lead, 0)], ref[(*lead, layers - 1)])
-    for copy in copies[9:]:
+    for copy in copies[2:]:
         copy.wait()
 
 
@@ -337,71 +337,118 @@
                 sa[at], sb[at] = send_t(side[i, k, w], side[i, layers - 1 + k, w])
 
 
-def krylov_kernel(
-    dims, ends, mid, side, mb, ma, jb, ja, wa, wb, stiff, after_emit, force, image, sums, ext, img
-):
-    layers, columns, sub = dims
-    w_high = halves("width", ends[0])[1]
+def krylov_part(dims, ends, late, ext, img, stiff, top_stiff, right_stiff):
+    layers, columns, sub = dims
     has_right = halves("width", ends[0])[3]
-    t_low, t_high, _, has_top = halves("thick", ends[1])
+    has_top = halves("thick", ends[1])[3]
     masks = edge_masks(sub)
     zero = jnp.zeros((sub, LANES), jnp.float32)
-    inner = columns - 1
-    edge = {0: 0, 1: 1, columns + 1: 2, columns + 2: 3}
-    for i in range(3):
-        for w in range(columns + 3):
-            if w in edge:
-                own, a, b, at, step = side, ja, jb, edge[w], 4
-            else:
-                own, a, b, at, step = mid, ma, mb, w - 2, inner
-            a = [a[(i * 2 + k) * step + at] for k in range(2)]
-            b = [b[(i * 2 + k) * step + at] for k in range(2)]
-            below = [t_low(x, y) for x, y in zip(a, b)]
-            above = [t_high(x, y) for x, y in zip(a, b)]
-            ext[i, 0, w] = below[0]
-            ext[i, 1, w] = own[i, 0, at] + below[1]
-            for t in range(1, layers):
-                ext[i, t + 1, w] = own[i, t, at]
-            ext[i, layers + 1, w] = jnp.where(has_top, own[i, layers, at] + above[0], 0.0)
-            ext[i, layers + 2, w] = above[1]
+
+    def stage(t, w):
+        if 2 <= w <= columns - 2:
+            return 0
+        rim = 2 if w in (0, columns) else 1
+        return 0 if rim <= t <= layers - rim else 1
 
     def apply(i, t, w, diagonal):
         here = ext[i, t + 1, w + 1]
         beside = ext[i, t, w + 1] + ext[i, t + 2, w + 1]
         beside = beside + (ext[i, t + 1, w] + ext[i, t + 1, w + 2])
-        beside = beside + (before(here, masks) + after(here, masks))
-        return here, diagonal * here - beside
-
-    count = 2 * (layers + 1)
+        near, far = before(here, masks), after(here, masks)
+        return here, diagonal * here - (beside + (near + far))
+
     for t in range(layers):
-        d = 6.0 + w_high(wa[3 * count + t], wb[3 * count + t])
-        for i in range(3):
-            _, g = apply(i, t, columns, d)
-            img[i, t, columns] = jnp.where(has_right, g, 0.0)
+        if stage(t, columns) == late:
+            d = 6.0 + right_stiff(t)
+            for i in range(3):
+                _, g = apply(i, t, columns, d)
+                img[i, t, columns] = jnp.where(has_right, g, 0.0)
     for w in range(columns):
-        d = 6.0 + t_high(ma[6 * inner + w], mb[6 * inner + w])
-        for i in range(3):
-            _, g = apply(i, layers, w, d)
-            img[i, layers, w] = jnp.where(has_top, g, 0.0)
-    for t in range(layers):
-        for w in range(columns):
-            d = 6.0 + row_of(stiff, (t,), w, columns, sub)
+        if stage(layers, w) == late:
+            d = 6.0 + top_stiff(w)
             for i in range(3):
-                f, g = apply(i, t, w, d)
-                img[i, t, w] = g
-                image[i, t, w] = g
-                force[i, t, w] = f
+                _, g = apply(i, layers, w, d)
+                img[i, layers, w] = jnp.where(has_top, g, 0.0)
     m0 = m1 = m2 = m3 = me = zero
     for t in range(layers):
         for w in range(columns):
-            d = 6.0 + row_of(stiff, (t,), w, columns, sub)
-            square = zero
+            if stage(t, w) == late:
+                d = 6.0 + row_of(stiff, (t,), w, columns, sub)
+                square = zero
+                for i in range(3):
+                    f, g = apply(i, t, w, d)
+                    img[i, t, w] = g
+                    m0, m1 = m0 + f * f, m1 + f * g
+                    square = square + g * g
+                    me = me + g * after(g, masks)
+                m2, m3 = m2 + square, m3 + d * square
+    for t in range(layers):
+        for w in range(columns):
+            beside = [p for p in ((t + 1, w), (t, w + 1)) if max(stage(t, w), stage(*p)) == late]
             for i in range(3):
-                f, g = ext[i, t + 1, w + 1], img[i, t, w]
-                m0, m1 = m0 + f * f, m1 + f * g
-                square = square + g * g
-                me = me + g * (img[i, t + 1, w] + img[i, t, w + 1] + after(g, masks))
-            m2, m3 = m2 + square, m3 + d * square
+                if beside:
+                    total = img[i, beside[0][0], beside[0][1]]
+                    for p in beside[1:]:
+                        total = total + img[i, p[0], p[1]]
+                    me = me + img[i, t, w] * total
+    return m0, m1, m2, m3, me
+
+
+def early_kernel(dims, ends, mid, side, mb, ma, wa, wb, stiff, ext, img, held):
+    layers, columns, sub = dims
+    w_high = halves("width", ends[0])[1]
+    t_low, t_high, _, has_top = halves("thick", ends[1])
+    inner = columns - 1
+    for i in range(3):
+        for at in range(inner):
+            a = [ma[(i * 2 + k) * inner + at] for k in range(2)]
+            b = [mb[(i * 2 + k) * inner + at] for k in range(2)]
+            below = [t_low(x, y) for x, y in zip(a, b)]
+            above = [t_high(x, y) for x, y in zip(a, b)]
+            w = at + 2
+            ext[i, 0, w] = below[0]
+            ext[i, 1, w] = mid[i, 0, at] + below[1]
+            for t in range(1, layers):
+                ext[i, t + 1, w] = mid[i, t, at]
+            ext[i, layers + 1, w] = jnp.where(has_top, mid[i, layers, at] + above[0], 0.0)
+            ext[i, layers + 2, w] = above[1]
+        for at, w in enumerate((0, 1, columns + 1, columns + 2)):
+            for t in range(1, layers):
+                ext[i, t + 1, w] = side[i, t, at]
+    count = 6 * (layers + 1)
+    sums = krylov_part(
+        dims, ends, 0, ext, img, stiff,
+        lambda w: t_high(ma[6 * inner + w], mb[6 * inner + w]),
+        lambda t: w_high(wa[count + t], wb[count + t]),
+    )
+    for k, m in enumerate(sums):
+        held[k] = m
+
+
+def late_kernel(
+    dims, ends, ext_in, img_in, held, side, jb, ja, mb, ma, wa, wb, stiff, after_emit, ext, img, sums
+):
+    layers, columns, sub = dims
+    w_high = halves("width", ends[0])[1]
+    t_low, t_high, _, has_top = halves("thick", ends[1])
+    inner = columns - 1
+    for i in range(3):
+        for at, w in enumerate((0, 1, columns + 1, columns + 2)):
+            a = [ja[(i * 2 + k) * 4 + at] for k in range(2)]
+            b = [jb[(i * 2 + k) * 4 + at] for k in range(2)]
+            below = [t_low(x, y) for x, y in zip(a, b)]
+            above = [t_high(x, y) for x, y in zip(a, b)]
+            ext[i, 0, w] = below[0]
+            ext[i, 1, w] = side[i, 0, at] + below[1]
+            ext[i, layers + 1, w] = jnp.where(has_top, side[i, layers, at] + above[0], 0.0)
+            ext[i, layers + 2, w] = above[1]
+    count = 6 * (layers + 1)
+    more = krylov_part(
+        dims, ends, 1, ext, img, stiff,
+        lambda w: t_high(ma[6 * inner + w], mb[6 * inner + w]),
+        lambda t: w_high(wa[count + t], wb[count + t]),
+    )
+    m0, m1, m2, m3, me = [held[k] + m for k, m in enumerate(more)]
     m3 = m3 - 2.0 * me
     lane = lax.broadcasted_iota(jnp.int32, (1, LANES), 1)
     line = jnp.zeros((1, LANES), jnp.float32)
@@ -427,7 +474,7 @@
         for t in range(layers):
             for w in range(columns):
                 out[i, t, pl.ds(w, sub, stride=columns), :] = (
-                    c0 * force[i, t, w] - c1 * image[i, t, w]
+                    c0 * force[i, t + 1, w + 1] - c1 * image[i, t, w]
                 )
 
 
@@ -464,7 +511,7 @@
         [(9, layers, *tile)] * 2
         + [(9, rows, LANES)] * 2
         + [(layers, rows, LANES), (6, layers, rows, LANES), (3, layers, rows, LANES)],
-        hbm=(0, 1, 2), count=3, copies=9 + layers,
+        hbm=(0, 1, 2), count=3, copies=3,
     )(*[pltpu.with_memory_space_constraint(x, pltpu.HBM) for x in (dev, vel, stiff)])
     tb = swap(tb, t_missing)
     wb = swap(wb, w_second)
@@ -514,12 +561,17 @@
         hbm=(1,), count=2, cost=6 * 1024 * 1024,
     )(tau, side)
 
+    around = [(3, layers + 3, columns + 3, *tile), (3, layers + 1, columns + 1, *tile)]
+    force, image, held = call(
+        functools.partial(early_kernel, dims, ends),
+        around + [(5, *tile)],
+        count=7, cost=2 * 1024 * 1024,
+    )(mid, side, mb, ma, wa, wb, stiff)
     force, image, sums = call(
-        functools.partial(krylov_kernel, dims, ends),
-        [(3, layers, columns, *tile)] * 2 + [(ends[0] * ends[1], 1, LANES)],
-        [(3, layers + 3, columns + 3, *tile), (3, layers + 1, columns + 1, *tile)],
-        count=10,
-    )(mid, side, mb, ma, jb, ja, wa, wb, stiff, done)
+        functools.partial(late_kernel, dims, ends),
+        around + [(ends[0] * ends[1], 1, LANES)],
+        count=12, aliases={0: 0, 1: 1},
+    )(force, image, held, side, jb, ja, mb, ma, wa, wb, stiff, done)
     sums = lax.all_to_all(sums, AXES, 0, 0, tiled=True)
 
     (out,) = call(

time: 39.5 us -> 39.1 us (0.990)
  waiting for transfers between devices: 6.17 us -> 5.61 us
    ppermute x10, waiting for transfers between devices: 6.17 us -> 5.61 us  [swap(): return lax.ppermute(value, AXES, pairs)]
    pallas_call x1 -> x2, Pallas kernels: 0.7 us -> 0.91 us  [the longest x1 0.54 us: on_device(): call(functools.partial(early_kernel, dims, ends), around + [(5, *tile)],...]
  transfers between devices with their start and end apart: 10 -> 10, of which waited for: 4 -> 3; matrix products, arithmetic and copies ran while one was open for 0% -> 0% of each run, Pallas kernels for 9% -> 10%
where the time goes in v6:
time: 39.1 us; the launch traced here: 38.9 us
  blocking collectives  12.8 us (33%)
  starting transfers between devices  12.7 us (32%)
  Pallas kernels  7.04 us (18%)
  waiting for transfers between devices  5.61 us (14%)
  between operations  0.7 us (2%)
    all_to_all x1, blocking collectives, on_device(): sums = lax.all_to_all(sums, AXES, 0, 0, tiled=True)  12.8 us
    ppermute x10, starting transfers between devices, swap(): return lax.ppermute(value, AXES, pairs)  12.7 us
    ppermute x10, waiting for transfers between devices, swap(): return lax.ppermute(value, AXES, pairs)  5.61 us
    pallas_call x1, Pallas kernels, on_device(): call(functools.partial(inner_kernel, dims), [(9, layers + 2, columns + 2,...  2.12 us
    pallas_call x1, Pallas kernels, on_device(): call(functools.partial(pack_kernel, dims, ends), [(9, layers, *tile)] * 2...  1.35 us
    pallas_call x1, Pallas kernels, on_device(): call(functools.partial(emit_kernel, dims), [(6, layers, rows, LANES), til...  1.01 us
    pallas_call x1, Pallas kernels, on_device(): call(functools.partial(finish_kernel, dims), [(3, layers, rows, LANES)],...  0.97 us
  transfers between devices with their start and end apart: 10, of which 3 were waited for; matrix products, arithmetic and copies ran while one was open for 0% of the time, Pallas kernels for 10%

profile of v6, /device:TPU:0, one launch (start us, length us, event | category | flops | bytes accessed | tf_op | source)
XLA Modules:
  0.0 38.9 jit_solution(5654845126034128457)
XLA Ops:
  0.6 1.4 %shard_map.50 = (f32[9,4,8,128]{3,2,1,0:T(8,128)S(1)}, f32[9,4,8,128]{3,2,1,0:T(8,128)S(1)}, f32[9,64,128]{2,1,0:T(8,128)S(1)}, f32[9,64,128]{2,1,0:T(8,128)S(1)...) custom-call(f32[6,4,64,128]{3,2,1,0:T(8,128)} %bitcast.25, ...), custom_call_target="tpu_custom_call" | custom-call | tf_op jit(solution)/shard_map/pallas_call | solution.py:509
  2.0 3.0 %collective-permute-start = (f32[9,4,8,128]{3,2,1,0:T(8,128)S(1)}, f32[9,4,8,128]{3,2,1,0:T(8,128)S(1)}, u32[]{:S(2)}, u32[]{:S(2)}) collective-permute-start(f32[9,4,8,128]{3,2,1,0:T(8,128)S(1)} %get-tuple-element.33), channel_id=1, source_target_pairs={{0,4},{1,5},{2,6},{3,7},{4,0},{5,1},{6,2},{7,3},{8,12},{9,13},{10,... | collective-permute-start | bytes 442376 | tf_op jit(solution)/shard_map/ppermute | solution.py:49
  5.0 0.0 collective-permute-start.1
  5.0 0.5 %collective-permute-start.2 = (f32[9,64,128]{2,1,0:T(8,128)S(1)}, f32[9,64,128]{2,1,0:T(8,128)S(1)}, u32[]{:S(2)}, u32[]{:S(2)}) collective-permute-start(f32[9,64,128]{2,1,0:T(8,128)S(1)} %get-tuple-element.35), channel_id=1, source_target_pairs={{0,1},{1,0},{2,3},{3,2},{4,5},{5,4},{6,7},{7,6},{8,9},{9,8},{10,11... | collective-permute-start | bytes 884744 | tf_op jit(solution)/shard_map/ppermute | solution.py:49
  5.5 0.7 %collective-permute-start.3 = (f32[9,64,128]{2,1,0:T(8,128)S(1)}, f32[9,64,128]{2,1,0:T(8,128)S(1)}, u32[]{:S(2)}, u32[]{:S(2)}) collective-permute-start(f32[9,64,128]{2,1,0:T(8,128)S(1)} %get-tuple-element.36), channel_id=1, source_target_pairs={{1,2},{2,1},{5,6},{6,5},{9,10},{10,9},{13,14},{14,13},{17,18},{18,... | collective-permute-start | bytes 884744 | tf_op jit(solution)/shard_map/ppermute | solution.py:49
  6.2 2.1 %shard_map.51 = (f32[9,6,10,8,128]{4,3,2,1,0:T(8,128)S(1)}, f32[6,4,8,8,128]{4,3,2,1,0:T(8,128)S(1)}) custom-call(f32[6,4,64,128]{3,2,1,0:T(8,128)S(1)} %get-tuple-element.29.dev, f32[3,4,64,128]{3,2,1,0:T(8,128)S(1)} %get-tuple-element.30.vel), custom_call_target="tpu_custom_call" | custom-call | bytes 12582912 | tf_op jit(solution)/shard_map/pallas_call | solution.py:521
  8.3 3.0 %collective-permute-done.wa = f32[9,4,8,128]{3,2,1,0:T(8,128)S(1)} collective-permute-done((f32[9,4,8,128]{3,2,1,0:T(8,128)S(1)}, f32[9,4,8,128]{3,2,1,0:T(8,128)S(1)}, u32[]{:S(2)}, u32[]{:S(2)}) %collective-permute-start) | collective-permute-done | bytes 147488 | tf_op jit(solution)/shard_map/ppermute | solution.py:49
  11.3 0.0 collective-permute-done.1.wb
  11.3 0.1 shard_map.52.tau_in
  11.4 0.0 collective-permute-done.2.ta
  11.4 0.0 collective-permute-done.3.tb
  11.4 0.3 shard_map.53
  11.7 2.5 %collective-permute-start.4 = (f32[34,8,128]{2,1,0:T(8,128)S(1)}, f32[34,8,128]{2,1,0:T(8,128)S(1)}, u32[]{:S(2)}, u32[]{:S(2)}) collective-permute-start(f32[34,8,128]{2,1,0:T(8,128)S(1)} %get-tuple-element.40), channel_id=1, source_target_pairs={{0,4},{1,5},{2,6},{3,7},{4,0},{5,1},{6,2},{7,3},{8,12},{9,13},{10,... | collective-permute-start | bytes 417800 | tf_op jit(solution)/shard_map/ppermute | solution.py:49
  14.3 2.4 %collective-permute-start.5 = (f32[34,8,128]{2,1,0:T(8,128)S(1)}, f32[34,8,128]{2,1,0:T(8,128)S(1)}, u32[]{:S(2)}, u32[]{:S(2)}) collective-permute-start(f32[34,8,128]{2,1,0:T(8,128)S(1)} %get-tuple-element.41), channel_id=1, source_target_pairs={{0,1},{1,0},{2,3},{3,2},{4,8},{5,9},{6,10},{7,11},{8,4},{9,5},{10,... | collective-permute-start | bytes 417800 | tf_op jit(solution)/shard_map/ppermute | solution.py:49
  16.7 0.2 shard_map.56
  16.9 1.5 %collective-permute-start.6 = (f32[50,8,128]{2,1,0:T(8,128)S(1)}, f32[50,8,128]{2,1,0:T(8,128)S(1)}, u32[]{:S(2)}, u32[]{:S(2)}) collective-permute-start(f32[50,8,128]{2,1,0:T(8,128)S(1)} %get-tuple-element.45), channel_id=1, source_target_pairs={{0,3},{1,2},{2,1},{3,0},{4,7},{5,6},{6,5},{7,4},{8,11},{9,10},{10,... | collective-permute-start | bytes 614408 | tf_op jit(solution)/shard_map/ppermute | solution.py:49
  18.4 0.0 collective-permute-start.7
  18.4 1.6 %collective-permute-done.4.wa = f32[34,8,128]{2,1,0:T(8,128)S(1)} collective-permute-done((f32[34,8,128]{2,1,0:T(8,128)S(1)}, f32[34,8,128]{2,1,0:T(8,128)S(1)}, u32[]{:S(2)}, u32[]{:S(2)}) %collective-permute-start.4) | collective-permute-done | bytes 139296 | tf_op jit(solution)/shard_map/ppermute | solution.py:49
  20.0 0.0 collective-permute-done.5.wb
  20.0 0.1 shard_map.54
  20.1 2.0 %collective-permute-start.8 = (f32[24,8,128]{2,1,0:T(8,128)S(1)}, f32[24,8,128]{2,1,0:T(8,128)S(1)}, u32[]{:S(2)}, u32[]{:S(2)}) collective-permute-start(f32[24,8,128]{2,1,0:T(8,128)S(1)} %get-tuple-element.50), channel_id=1, source_target_pairs={{0,8},{1,2},{2,1},{3,11},{4,12},{5,6},{6,5},{7,15},{8,0},{9,10},{1... | collective-permute-start | bytes 294920 | tf_op jit(solution)/shard_map/ppermute | solution.py:49
  22.0 0.1 collective-permute-start.9
  22.2 1.0 %shard_map.55 = (f32[6,4,64,128]{3,2,1,0:T(8,128)}, f32[8,128]{1,0:T(8,128)S(1)}) custom-call(f32[6,4,8,8,128]{4,3,2,1,0:T(8,128)S(1)} %get-tuple-element.38.tau, f32[3,5,4,8,128]{4,3,2,1,0:T(8,128)S(1)} %get-tuple-element.42.after_join.side), custom_call_target="tpu_custom_call" | custom-call | bytes 6291456 | tf_op jit(solution)/shard_map/pallas_call | solution.py:559
  23.2 1.0 %collective-permute-done.6.mb = f32[50,8,128]{2,1,0:T(8,128)S(1)} collective-permute-done((f32[50,8,128]{2,1,0:T(8,128)S(1)}, f32[50,8,128]{2,1,0:T(8,128)S(1)}, u32[]{:S(2)}, u32[]{:S(2)}) %collective-permute-start.6) | collective-permute-done | bytes 204832 | tf_op jit(solution)/shard_map/ppermute | solution.py:49
  24.2 0.0 collective-permute-done.7.ma
  24.2 0.5 %shard_map.57 = (f32[3,7,11,8,128]{4,3,2,1,0:T(8,128)S(1)}, f32[3,5,9,8,128]{4,3,2,1,0:T(8,128)S(1)}, f32[5,8,128]{2,1,0:T(8,128)S(1)}) custom-call(f32[3,5,7,8,128]{4,3,2,1,0:T(8,128)S(1)} %get-tuple-element.44.mid, f32[3,5,4,8,128]{4,3,2,1,0:T(8,128)S(1)} %get-tuple-element.42.after_join.side, f32[50,8,128]{2,1,0:T(8,128)S(1)} %collective-permute-done.6.mb, ...), custom_call_target="tpu_custom_call" | custom-call | bytes 2097152 | tf_op jit(solution)/shard_map/pallas_call | solution.py:565
  24.7 0.0 collective-permute-done.8.jb
  24.7 0.0 collective-permute-done.9.ja
  24.7 0.4 shard_map.58
  25.1 12.8 %all_to_all.5.sums = f32[32,1,128]{2,1,0:T(1,128)S(1)} all-to-all(f32[32,1,128]{2,1,0:T(1,128)S(1)} %get-tuple-element.53), channel_id=1, replica_groups=mesh['width'=8,'thick'=4] {'width','thick'}, dimensions={0} | all-to-all | bytes 32768 | tf_op jit(solution)/shard_map/all_to_all | solution.py:575
  37.9 1.0 %shard_map.59 = f32[3,4,64,128]{3,2,1,0:T(8,128)} custom-call(f32[32,1,128]{2,1,0:T(1,128)S(1)} %all_to_all.5.sums, f32[3,7,11,8,128]{4,3,2,1,0:T(8,128)S(1)} %get-tuple-element.54.force, f32[3,5,9,8,128]{4,3,2,1,0:T(8,128)S(1)} %get-tuple-element.55.image), custom_call_target="tpu_custom_call" | custom-call | tf_op jit(solution)/shard_map/pallas_call | solution.py:577
Async XLA Ops:
  2.0 9.3 %collective-permute-start = (f32[9,4,8,128]{3,2,1,0:T(8,128)S(1)}, f32[9,4,8,128]{3,2,1,0:T(8,128)S(1)}, u32[]{:S(2)}, u32[]{:S(2)}) collective-permute-start(f32[9,4,8,128]{3,2,1,0:T(8,128)S(1)} %get-tuple-element.33), channel_id=1, source_target_pairs={{0,4},{1,5},{2,6},{3,7},{4,0},{5,1},{6,2},{7,3},{8,12},{9,13},{10,... | collective-permute-start | bytes 442376 | tf_op jit(solution)/shard_map/ppermute | solution.py:49
  5.0 6.3 %collective-permute-start.1 = (f32[9,4,8,128]{3,2,1,0:T(8,128)S(1)}, f32[9,4,8,128]{3,2,1,0:T(8,128)S(1)}, u32[]{:S(2)}, u32[]{:S(2)}) collective-permute-start(f32[9,4,8,128]{3,2,1,0:T(8,128)S(1)} %get-tuple-element.34), channel_id=1, source_target_pairs={{0,1},{1,0},{2,3},{3,2},{4,8},{5,9},{6,10},{7,11},{8,4},{9,5},{10,... | collective-permute-start | bytes 442376 | tf_op jit(solution)/shard_map/ppermute | solution.py:49
  5.0 6.4 %collective-permute-start.2 = (f32[9,64,128]{2,1,0:T(8,128)S(1)}, f32[9,64,128]{2,1,0:T(8,128)S(1)}, u32[]{:S(2)}, u32[]{:S(2)}) collective-permute-start(f32[9,64,128]{2,1,0:T(8,128)S(1)} %get-tuple-element.35), channel_id=1, source_target_pairs={{0,1},{1,0},{2,3},{3,2},{4,5},{5,4},{6,7},{7,6},{8,9},{9,8},{10,11... | collective-permute-start | bytes 884744 | tf_op jit(solution)/shard_map/ppermute | solution.py:49
  5.5 5.9 %collective-permute-start.3 = (f32[9,64,128]{2,1,0:T(8,128)S(1)}, f32[9,64,128]{2,1,0:T(8,128)S(1)}, u32[]{:S(2)}, u32[]{:S(2)}) collective-permute-start(f32[9,64,128]{2,1,0:T(8,128)S(1)} %get-tuple-element.36), channel_id=1, source_target_pairs={{1,2},{2,1},{5,6},{6,5},{9,10},{10,9},{13,14},{14,13},{17,18},{18,... | collective-permute-start | bytes 884744 | tf_op jit(solution)/shard_map/ppermute | solution.py:49
  11.7 8.3 %collective-permute-start.4 = (f32[34,8,128]{2,1,0:T(8,128)S(1)}, f32[34,8,128]{2,1,0:T(8,128)S(1)}, u32[]{:S(2)}, u32[]{:S(2)}) collective-permute-start(f32[34,8,128]{2,1,0:T(8,128)S(1)} %get-tuple-element.40), channel_id=1, source_target_pairs={{0,4},{1,5},{2,6},{3,7},{4,0},{5,1},{6,2},{7,3},{8,12},{9,13},{10,... | collective-permute-start | bytes 417800 | tf_op jit(solution)/shard_map/ppermute | solution.py:49
  14.3 5.7 %collective-permute-start.5 = (f32[34,8,128]{2,1,0:T(8,128)S(1)}, f32[34,8,128]{2,1,0:T(8,128)S(1)}, u32[]{:S(2)}, u32[]{:S(2)}) collective-permute-start(f32[34,8,128]{2,1,0:T(8,128)S(1)} %get-tuple-element.41), channel_id=1, source_target_pairs={{0,1},{1,0},{2,3},{3,2},{4,8},{5,9},{6,10},{7,11},{8,4},{9,5},{10,... | collective-permute-start | bytes 417800 | tf_op jit(solution)/shard_map/ppermute | solution.py:49
  16.9 7.3 %collective-permute-start.6 = (f32[50,8,128]{2,1,0:T(8,128)S(1)}, f32[50,8,128]{2,1,0:T(8,128)S(1)}, u32[]{:S(2)}, u32[]{:S(2)}) collective-permute-start(f32[50,8,128]{2,1,0:T(8,128)S(1)} %get-tuple-element.45), channel_id=1, source_target_pairs={{0,3},{1,2},{2,1},{3,0},{4,7},{5,6},{6,5},{7,4},{8,11},{9,10},{10,... | collective-permute-start | bytes 614408 | tf_op jit(solution)/shard_map/ppermute | solution.py:49
  18.4 5.8 %collective-permute-start.7 = (f32[50,8,128]{2,1,0:T(8,128)S(1)}, f32[50,8,128]{2,1,0:T(8,128)S(1)}, u32[]{:S(2)}, u32[]{:S(2)}) collective-permute-start(f32[50,8,128]{2,1,0:T(8,128)S(1)} %get-tuple-element.46), channel_id=1, source_target_pairs={{0,1},{1,0},{2,3},{3,2},{4,5},{5,4},{6,7},{7,6},{8,9},{9,8},{10,11... | collective-permute-start | bytes 614408 | tf_op jit(solution)/shard_map/ppermute | solution.py:49
  20.1 4.7 %collective-permute-start.8 = (f32[24,8,128]{2,1,0:T(8,128)S(1)}, f32[24,8,128]{2,1,0:T(8,128)S(1)}, u32[]{:S(2)}, u32[]{:S(2)}) collective-permute-start(f32[24,8,128]{2,1,0:T(8,128)S(1)} %get-tuple-element.50), channel_id=1, source_target_pairs={{0,8},{1,2},{2,1},{3,11},{4,12},{5,6},{6,5},{7,15},{8,0},{9,10},{1... | collective-permute-start | bytes 294920 | tf_op jit(solution)/shard_map/ppermute | solution.py:49
  22.0 2.7 %collective-permute-start.9 = (f32[24,8,128]{2,1,0:T(8,128)S(1)}, f32[24,8,128]{2,1,0:T(8,128)S(1)}, u32[]{:S(2)}, u32[]{:S(2)}) collective-permute-start(f32[24,8,128]{2,1,0:T(8,128)S(1)} %get-tuple-element.51), channel_id=1, source_target_pairs={{0,1},{1,0},{2,3},{3,2},{4,5},{5,4},{6,7},{7,6},{8,9},{9,8},{10,11... | collective-permute-start | bytes 294920 | tf_op jit(solution)/shard_map/ppermute | solution.py:49

commit v7 on v6

--- a/solution.py
+++ b/solution.py
@@ -316,6 +316,9 @@
                 new[c, t, pl.ds(w, sub, stride=columns), :] = tau[c, t, w]
 
 
+CORNERS = ((0, 0), (0, 1), (0, 2), (0, 3), (1, 1), (1, 2))
+
+
 def join_kernel(dims, ends, part, wa, wb, side, sa, sb):
     layers, columns, sub = dims
     w_low, w_high, _, has_high = halves("width", ends[0])
@@ -331,10 +334,9 @@
             side[i, t, 2] = jnp.where(has_high, part[i, t, 3] + above[0], 0.0)
             side[i, t, 3] = above[1]
     for i in range(3):
-        for k in range(2):
-            for w in range(4):
-                at = (i * 2 + k) * 4 + w
-                sa[at], sb[at] = send_t(side[i, k, w], side[i, layers - 1 + k, w])
+        for q, (depth, w) in enumerate(CORNERS):
+            at = i * len(CORNERS) + q
+            sa[at], sb[at] = send_t(side[i, depth, w], side[i, layers - depth, w])
 
 
 def krylov_part(dims, ends, late, ext, img, stiff, top_stiff, right_stiff):
@@ -433,15 +435,16 @@
     t_low, t_high, _, has_top = halves("thick", ends[1])
     inner = columns - 1
     for i in range(3):
-        for at, w in enumerate((0, 1, columns + 1, columns + 2)):
-            a = [ja[(i * 2 + k) * 4 + at] for k in range(2)]
-            b = [jb[(i * 2 + k) * 4 + at] for k in range(2)]
-            below = [t_low(x, y) for x, y in zip(a, b)]
-            above = [t_high(x, y) for x, y in zip(a, b)]
-            ext[i, 0, w] = below[0]
-            ext[i, 1, w] = side[i, 0, at] + below[1]
-            ext[i, layers + 1, w] = jnp.where(has_top, side[i, layers, at] + above[0], 0.0)
-            ext[i, layers + 2, w] = above[1]
+        for q, (depth, at) in enumerate(CORNERS):
+            a, b = ja[i * len(CORNERS) + q], jb[i * len(CORNERS) + q]
+            below, above = t_low(a, b), t_high(a, b)
+            w = (0, 1, columns + 1, columns + 2)[at]
+            if depth == 0:
+                ext[i, 1, w] = side[i, 0, at] + below
+                ext[i, layers + 1, w] = jnp.where(has_top, side[i, layers, at] + above, 0.0)
+            else:
+                ext[i, 0, w] = below
+                ext[i, layers + 2, w] = above
     count = 6 * (layers + 1)
     more = krylov_part(
         dims, ends, 1, ext, img, stiff,
@@ -545,12 +548,12 @@
         [(3, layers + 1, columns - 1, *tile)] + [(broad, *tile)] * 2,
         count=3, cost=2 * 1024 * 1024,
     )(tau, part, stiff)
-    mb = swap(sb, t_across)
+    mb = swap(sb, t_missing)
     ma = swap(sa, t_first)
 
     side, sa, sb = call(
         functools.partial(join_kernel, dims, ends),
-        [(3, layers + 1, 4, *tile)] + [(24, *tile)] * 2,
+        [(3, layers + 1, 4, *tile)] + [(3 * len(CORNERS), *tile)] * 2,
         count=3,
     )(part, wa, wb)
     jb = swap(sb, t_second)

time: 39.1 us -> 38.7 us (0.990)
  starting transfers between devices: 12.7 us -> 14.5 us
  waiting for transfers between devices: 5.61 us -> 3.85 us
    ppermute x10, starting transfers between devices: 12.7 us -> 14.5 us  [swap(): return lax.ppermute(value, AXES, pairs)]
    ppermute x10, waiting for transfers between devices: 5.61 us -> 3.85 us  [swap(): return lax.ppermute(value, AXES, pairs)]
  transfers between devices with their start and end apart: 10 -> 10, of which waited for: 3 -> 2; matrix products, arithmetic and copies ran while one was open for 0% -> 0% of each run, Pallas kernels for 10% -> 10%
where the time goes in v7:
time: 38.7 us; the launch traced here: 38.6 us
  starting transfers between devices  14.5 us (37%)
  blocking collectives  12.5 us (32%)
  Pallas kernels  7.03 us (18%)
  waiting for transfers between devices  3.85 us (10%)
  between operations  0.71 us (2%)
    ppermute x10, starting transfers between devices, swap(): return lax.ppermute(value, AXES, pairs)  14.5 us
    all_to_all x1, blocking collectives, on_device(): sums = lax.all_to_all(sums, AXES, 0, 0, tiled=True)  12.5 us
    ppermute x10, waiting for transfers between devices, swap(): return lax.ppermute(value, AXES, pairs)  3.85 us
    pallas_call x1, Pallas kernels, on_device(): call(functools.partial(inner_kernel, dims), [(9, layers + 2, columns + 2,...  2.12 us
    pallas_call x1, Pallas kernels, on_device(): call(functools.partial(pack_kernel, dims, ends), [(9, layers, *tile)] * 2...  1.35 us
    pallas_call x1, Pallas kernels, on_device(): call(functools.partial(emit_kernel, dims), [(6, layers, rows, LANES), til...  1.01 us
    pallas_call x1, Pallas kernels, on_device(): call(functools.partial(finish_kernel, dims), [(3, layers, rows, LANES)],...  0.97 us
  transfers between devices with their start and end apart: 10, of which 2 were waited for; matrix products, arithmetic and copies ran while one was open for 0% of the time, Pallas kernels for 10%

profile of v7, /device:TPU:0, one launch (start us, length us, event | category | flops | bytes accessed | tf_op | source)
XLA Modules:
  0.0 38.6 jit_solution(4099393888356301917)
XLA Ops:
  0.6 1.4 %shard_map.50 = (f32[9,4,8,128]{3,2,1,0:T(8,128)S(1)}, f32[9,4,8,128]{3,2,1,0:T(8,128)S(1)}, f32[9,64,128]{2,1,0:T(8,128)S(1)}, f32[9,64,128]{2,1,0:T(8,128)S(1)...) custom-call(f32[6,4,64,128]{3,2,1,0:T(8,128)} %bitcast.25, ...), custom_call_target="tpu_custom_call" | custom-call | tf_op jit(solution)/shard_map/pallas_call | solution.py:512
  2.0 3.0 %collective-permute-start = (f32[9,4,8,128]{3,2,1,0:T(8,128)S(1)}, f32[9,4,8,128]{3,2,1,0:T(8,128)S(1)}, u32[]{:S(2)}, u32[]{:S(2)}) collective-permute-start(f32[9,4,8,128]{3,2,1,0:T(8,128)S(1)} %get-tuple-element.33), channel_id=1, source_target_pairs={{0,4},{1,5},{2,6},{3,7},{4,0},{5,1},{6,2},{7,3},{8,12},{9,13},{10,... | collective-permute-start | bytes 442376 | tf_op jit(solution)/shard_map/ppermute | solution.py:49
  5.0 0.0 collective-permute-start.1
  5.0 0.5 %collective-permute-start.2 = (f32[9,64,128]{2,1,0:T(8,128)S(1)}, f32[9,64,128]{2,1,0:T(8,128)S(1)}, u32[]{:S(2)}, u32[]{:S(2)}) collective-permute-start(f32[9,64,128]{2,1,0:T(8,128)S(1)} %get-tuple-element.35), channel_id=1, source_target_pairs={{0,1},{1,0},{2,3},{3,2},{4,5},{5,4},{6,7},{7,6},{8,9},{9,8},{10,11... | collective-permute-start | bytes 884744 | tf_op jit(solution)/shard_map/ppermute | solution.py:49
  5.5 0.7 %collective-permute-start.3 = (f32[9,64,128]{2,1,0:T(8,128)S(1)}, f32[9,64,128]{2,1,0:T(8,128)S(1)}, u32[]{:S(2)}, u32[]{:S(2)}) collective-permute-start(f32[9,64,128]{2,1,0:T(8,128)S(1)} %get-tuple-element.36), channel_id=1, source_target_pairs={{1,2},{2,1},{5,6},{6,5},{9,10},{10,9},{13,14},{14,13},{17,18},{18,... | collective-permute-start | bytes 884744 | tf_op jit(solution)/shard_map/ppermute | solution.py:49
  6.2 2.1 %shard_map.51 = (f32[9,6,10,8,128]{4,3,2,1,0:T(8,128)S(1)}, f32[6,4,8,8,128]{4,3,2,1,0:T(8,128)S(1)}) custom-call(f32[6,4,64,128]{3,2,1,0:T(8,128)S(1)} %get-tuple-element.29.dev, f32[3,4,64,128]{3,2,1,0:T(8,128)S(1)} %get-tuple-element.30.vel), custom_call_target="tpu_custom_call" | custom-call | bytes 12582912 | tf_op jit(solution)/shard_map/pallas_call | solution.py:524
  8.3 3.0 %collective-permute-done.wa = f32[9,4,8,128]{3,2,1,0:T(8,128)S(1)} collective-permute-done((f32[9,4,8,128]{3,2,1,0:T(8,128)S(1)}, f32[9,4,8,128]{3,2,1,0:T(8,128)S(1)}, u32[]{:S(2)}, u32[]{:S(2)}) %collective-permute-start) | collective-permute-done | bytes 147488 | tf_op jit(solution)/shard_map/ppermute | solution.py:49
  11.3 0.0 collective-permute-done.1.wb
  11.3 0.1 shard_map.52.tau_in
  11.4 0.0 collective-permute-done.2.ta
  11.4 0.0 collective-permute-done.3.tb
  11.4 0.3 shard_map.53
  11.7 2.5 %collective-permute-start.4 = (f32[34,8,128]{2,1,0:T(8,128)S(1)}, f32[34,8,128]{2,1,0:T(8,128)S(1)}, u32[]{:S(2)}, u32[]{:S(2)}) collective-permute-start(f32[34,8,128]{2,1,0:T(8,128)S(1)} %get-tuple-element.40), channel_id=1, source_target_pairs={{0,4},{1,5},{2,6},{3,7},{4,0},{5,1},{6,2},{7,3},{8,12},{9,13},{10,... | collective-permute-start | bytes 417800 | tf_op jit(solution)/shard_map/ppermute | solution.py:49
  14.3 2.4 %collective-permute-start.5 = (f32[34,8,128]{2,1,0:T(8,128)S(1)}, f32[34,8,128]{2,1,0:T(8,128)S(1)}, u32[]{:S(2)}, u32[]{:S(2)}) collective-permute-start(f32[34,8,128]{2,1,0:T(8,128)S(1)} %get-tuple-element.41), channel_id=1, source_target_pairs={{0,1},{1,0},{2,3},{3,2},{4,8},{5,9},{6,10},{7,11},{8,4},{9,5},{10,... | collective-permute-start | bytes 417800 | tf_op jit(solution)/shard_map/ppermute | solution.py:49
  16.7 0.2 shard_map.56
  16.9 0.7 %collective-permute-start.6 = (f32[50,8,128]{2,1,0:T(8,128)S(1)}, f32[50,8,128]{2,1,0:T(8,128)S(1)}, u32[]{:S(2)}, u32[]{:S(2)}) collective-permute-start(f32[50,8,128]{2,1,0:T(8,128)S(1)} %get-tuple-element.45), channel_id=1, source_target_pairs={{1,2},{2,1},{5,6},{6,5},{9,10},{10,9},{13,14},{14,13},{17,18},{18,... | collective-permute-start | bytes 614408 | tf_op jit(solution)/shard_map/ppermute | solution.py:49
  17.6 2.7 %collective-permute-start.7 = (f32[50,8,128]{2,1,0:T(8,128)S(1)}, f32[50,8,128]{2,1,0:T(8,128)S(1)}, u32[]{:S(2)}, u32[]{:S(2)}) collective-permute-start(f32[50,8,128]{2,1,0:T(8,128)S(1)} %get-tuple-element.46), channel_id=1, source_target_pairs={{0,1},{1,0},{2,3},{3,2},{4,5},{5,4},{6,7},{7,6},{8,9},{9,8},{10,11... | collective-permute-start | bytes 614408 | tf_op jit(solution)/shard_map/ppermute | solution.py:49
  20.3 0.0 collective-permute-done.4.wa
  20.3 0.0 collective-permute-done.5.wb
  20.3 0.1 shard_map.54
  20.3 1.7 %collective-permute-start.8 = (f32[18,8,128]{2,1,0:T(8,128)S(1)}, f32[18,8,128]{2,1,0:T(8,128)S(1)}, u32[]{:S(2)}, u32[]{:S(2)}) collective-permute-start(f32[18,8,128]{2,1,0:T(8,128)S(1)} %get-tuple-element.50), channel_id=1, source_target_pairs={{0,8},{1,2},{2,1},{3,11},{4,12},{5,6},{6,5},{7,15},{8,0},{9,10},{1... | collective-permute-start | bytes 221192 | tf_op jit(solution)/shard_map/ppermute | solution.py:49
  22.0 0.3 collective-permute-start.9
  22.3 1.0 %shard_map.55 = (f32[6,4,64,128]{3,2,1,0:T(8,128)}, f32[8,128]{1,0:T(8,128)S(1)}) custom-call(f32[6,4,8,8,128]{4,3,2,1,0:T(8,128)S(1)} %get-tuple-element.38.tau, f32[3,5,4,8,128]{4,3,2,1,0:T(8,128)S(1)} %get-tuple-element.42.after_join.side), custom_call_target="tpu_custom_call" | custom-call | bytes 6291456 | tf_op jit(solution)/shard_map/pallas_call | solution.py:562
  23.3 0.0 collective-permute-done.6.mb
  23.3 0.0 collective-permute-done.7.ma
  23.3 0.5 %shard_map.57 = (f32[3,7,11,8,128]{4,3,2,1,0:T(8,128)S(1)}, f32[3,5,9,8,128]{4,3,2,1,0:T(8,128)S(1)}, f32[5,8,128]{2,1,0:T(8,128)S(1)}) custom-call(f32[3,5,7,8,128]{4,3,2,1,0:T(8,128)S(1)} %get-tuple-element.44.mid, f32[3,5,4,8,128]{4,3,2,1,0:T(8,128)S(1)} %get-tuple-element.42.after_join.side, f32[50,8,128]{2,1,0:T(8,128)S(1)} %collective-permute-done.6.mb, ...), custom_call_target="tpu_custom_call" | custom-call | bytes 2097152 | tf_op jit(solution)/shard_map/pallas_call | solution.py:568
  23.9 0.9 %collective-permute-done.8.jb = f32[18,8,128]{2,1,0:T(8,128)S(1)} collective-permute-done((f32[18,8,128]{2,1,0:T(8,128)S(1)}, f32[18,8,128]{2,1,0:T(8,128)S(1)}, u32[]{:S(2)}, u32[]{:S(2)}) %collective-permute-start.8) | collective-permute-done | bytes 73760 | tf_op jit(solution)/shard_map/ppermute | solution.py:49
  24.8 0.0 collective-permute-done.9.ja
  24.8 0.4 shard_map.58
  25.1 12.5 %all_to_all.5.sums = f32[32,1,128]{2,1,0:T(1,128)S(1)} all-to-all(f32[32,1,128]{2,1,0:T(1,128)S(1)} %get-tuple-element.53), channel_id=1, replica_groups=mesh['width'=8,'thick'=4] {'width','thick'}, dimensions={0} | all-to-all | bytes 32768 | tf_op jit(solution)/shard_map/all_to_all | solution.py:578
  37.6 1.0 %shard_map.59 = f32[3,4,64,128]{3,2,1,0:T(8,128)} custom-call(f32[32,1,128]{2,1,0:T(1,128)S(1)} %all_to_all.5.sums, f32[3,7,11,8,128]{4,3,2,1,0:T(8,128)S(1)} %get-tuple-element.54.force, f32[3,5,9,8,128]{4,3,2,1,0:T(8,128)S(1)} %get-tuple-element.55.image), custom_call_target="tpu_custom_call" | custom-call | tf_op jit(solution)/shard_map/pallas_call | solution.py:580
Async XLA Ops:
  2.0 9.3 %collective-permute-start = (f32[9,4,8,128]{3,2,1,0:T(8,128)S(1)}, f32[9,4,8,128]{3,2,1,0:T(8,128)S(1)}, u32[]{:S(2)}, u32[]{:S(2)}) collective-permute-start(f32[9,4,8,128]{3,2,1,0:T(8,128)S(1)} %get-tuple-element.33), channel_id=1, source_target_pairs={{0,4},{1,5},{2,6},{3,7},{4,0},{5,1},{6,2},{7,3},{8,12},{9,13},{10,... | collective-permute-start | bytes 442376 | tf_op jit(solution)/shard_map/ppermute | solution.py:49
  5.0 6.3 %collective-permute-start.1 = (f32[9,4,8,128]{3,2,1,0:T(8,128)S(1)}, f32[9,4,8,128]{3,2,1,0:T(8,128)S(1)}, u32[]{:S(2)}, u32[]{:S(2)}) collective-permute-start(f32[9,4,8,128]{3,2,1,0:T(8,128)S(1)} %get-tuple-element.34), channel_id=1, source_target_pairs={{0,1},{1,0},{2,3},{3,2},{4,8},{5,9},{6,10},{7,11},{8,4},{9,5},{10,... | collective-permute-start | bytes 442376 | tf_op jit(solution)/shard_map/ppermute | solution.py:49
  5.0 6.4 %collective-permute-start.2 = (f32[9,64,128]{2,1,0:T(8,128)S(1)}, f32[9,64,128]{2,1,0:T(8,128)S(1)}, u32[]{:S(2)}, u32[]{:S(2)}) collective-permute-start(f32[9,64,128]{2,1,0:T(8,128)S(1)} %get-tuple-element.35), channel_id=1, source_target_pairs={{0,1},{1,0},{2,3},{3,2},{4,5},{5,4},{6,7},{7,6},{8,9},{9,8},{10,11... | collective-permute-start | bytes 884744 | tf_op jit(solution)/shard_map/ppermute | solution.py:49
  5.5 5.9 %collective-permute-start.3 = (f32[9,64,128]{2,1,0:T(8,128)S(1)}, f32[9,64,128]{2,1,0:T(8,128)S(1)}, u32[]{:S(2)}, u32[]{:S(2)}) collective-permute-start(f32[9,64,128]{2,1,0:T(8,128)S(1)} %get-tuple-element.36), channel_id=1, source_target_pairs={{1,2},{2,1},{5,6},{6,5},{9,10},{10,9},{13,14},{14,13},{17,18},{18,... | collective-permute-start | bytes 884744 | tf_op jit(solution)/shard_map/ppermute | solution.py:49
  11.7 8.6 %collective-permute-start.4 = (f32[34,8,128]{2,1,0:T(8,128)S(1)}, f32[34,8,128]{2,1,0:T(8,128)S(1)}, u32[]{:S(2)}, u32[]{:S(2)}) collective-permute-start(f32[34,8,128]{2,1,0:T(8,128)S(1)} %get-tuple-element.40), channel_id=1, source_target_pairs={{0,4},{1,5},{2,6},{3,7},{4,0},{5,1},{6,2},{7,3},{8,12},{9,13},{10,... | collective-permute-start | bytes 417800 | tf_op jit(solution)/shard_map/ppermute | solution.py:49
  14.3 6.0 %collective-permute-start.5 = (f32[34,8,128]{2,1,0:T(8,128)S(1)}, f32[34,8,128]{2,1,0:T(8,128)S(1)}, u32[]{:S(2)}, u32[]{:S(2)}) collective-permute-start(f32[34,8,128]{2,1,0:T(8,128)S(1)} %get-tuple-element.41), channel_id=1, source_target_pairs={{0,1},{1,0},{2,3},{3,2},{4,8},{5,9},{6,10},{7,11},{8,4},{9,5},{10,... | collective-permute-start | bytes 417800 | tf_op jit(solution)/shard_map/ppermute | solution.py:49
  16.9 6.5 %collective-permute-start.6 = (f32[50,8,128]{2,1,0:T(8,128)S(1)}, f32[50,8,128]{2,1,0:T(8,128)S(1)}, u32[]{:S(2)}, u32[]{:S(2)}) collective-permute-start(f32[50,8,128]{2,1,0:T(8,128)S(1)} %get-tuple-element.45), channel_id=1, source_target_pairs={{1,2},{2,1},{5,6},{6,5},{9,10},{10,9},{13,14},{14,13},{17,18},{18,... | collective-permute-start | bytes 614408 | tf_op jit(solution)/shard_map/ppermute | solution.py:49
  17.6 5.8 %collective-permute-start.7 = (f32[50,8,128]{2,1,0:T(8,128)S(1)}, f32[50,8,128]{2,1,0:T(8,128)S(1)}, u32[]{:S(2)}, u32[]{:S(2)}) collective-permute-start(f32[50,8,128]{2,1,0:T(8,128)S(1)} %get-tuple-element.46), channel_id=1, source_target_pairs={{0,1},{1,0},{2,3},{3,2},{4,5},{5,4},{6,7},{7,6},{8,9},{9,8},{10,11... | collective-permute-start | bytes 614408 | tf_op jit(solution)/shard_map/ppermute | solution.py:49
  20.3 4.4 %collective-permute-start.8 = (f32[18,8,128]{2,1,0:T(8,128)S(1)}, f32[18,8,128]{2,1,0:T(8,128)S(1)}, u32[]{:S(2)}, u32[]{:S(2)}) collective-permute-start(f32[18,8,128]{2,1,0:T(8,128)S(1)} %get-tuple-element.50), channel_id=1, source_target_pairs={{0,8},{1,2},{2,1},{3,11},{4,12},{5,6},{6,5},{7,15},{8,0},{9,10},{1... | collective-permute-start | bytes 221192 | tf_op jit(solution)/shard_map/ppermute | solution.py:49
  22.0 2.7 %collective-permute-start.9 = (f32[18,8,128]{2,1,0:T(8,128)S(1)}, f32[18,8,128]{2,1,0:T(8,128)S(1)}, u32[]{:S(2)}, u32[]{:S(2)}) collective-permute-start(f32[18,8,128]{2,1,0:T(8,128)S(1)} %get-tuple-element.51), channel_id=1, source_target_pairs={{0,1},{1,0},{2,3},{3,2},{4,5},{5,4},{6,7},{7,6},{8,9},{9,8},{10,11... | collective-permute-start | bytes 221192 | tf_op jit(solution)/shard_map/ppermute | solution.py:49
